TPU v7x, 32 devices: a whole 2x2x4 slice. The times are simulated.
32 devices in a mesh: groups: 2 (over y), latent: 4 (over z), rows: 4 (over x, core).
Axes of the slice: x: 2, y: 2, z: 4, core: 2. Of those that a mesh axis runs over, the one named last changes fastest.
Arguments:
- activations_in: bfloat16 [2, 128, 2304], P('groups', None, 'latent'), parts along dimension 0, may hold values from -6 to 6
- gate_proj: bfloat16 [2304, 4608], P('rows', 'latent'), may hold values from -0.125 to 0.125
- up_proj: bfloat16 [2304, 4608], P('rows', 'latent'), may hold values from -0.125 to 0.125
- down_proj: bfloat16 [4608, 2304], P('latent', 'rows'), may hold values from -0.09375 to 0.09375
- enc_weight: bfloat16 [4608, 65536], P(('groups', 'rows'), 'latent'), parts along dimension 0, may hold values from -6 to 6
- enc_bias: float32 [131072], P(('groups', 'latent')), parts along dimension 0, may hold values from -0.5 to 0.5
- dec_weight: bfloat16 [131072, 2304], P(('groups', 'latent'), 'rows'), parts along dimension 0, may hold values from -6 to 6
- dec_bias: float32 [4608], P(('groups', 'rows')), parts along dimension 0, may hold values from -0.5 to 0.5
Outputs:
- enc_weight_new: bfloat16 [4608, 65536], P(('groups', 'rows'), 'latent'), parts along dimension 0
- enc_bias_new: float32 [131072], P(('groups', 'latent')), parts along dimension 0
- dec_weight_new: bfloat16 [131072, 2304], P(('groups', 'latent'), 'rows'), parts along dimension 0
- dec_bias_new: float32 [4608], P(('groups', 'rows')), parts along dimension 0
There are 2 independent parts, one for each index of `groups`. A program takes and returns all parts, laid end to end along the dimension named above; an argument that names none is the same for every part. Nothing has to cross between parts.
All inputs are finite; a program needn't handle non-finite values.
Results may differ from a plain program's by a relative error of at most 0.02.
Values may be sent and summed in bfloat16 or wider, within the bound.
A program may use at most 128 MiB of HBM per device.

v0:
```python
import jax
import jax.numpy as jnp
from jax import lax
from jax.sharding import PartitionSpec as P

MODEL_WIDTH = 2304
LATENTS = 65536


sparsity_cost = 0.1
sharpness = 8.0
weight_rate = 2.0
enc_bias_rate = 0.01
dec_bias_rate = 0.002


def row_total(term):
    return lax.psum(term.astype(jnp.bfloat16), "rows").astype(jnp.float32)


def body(activations_in, gate_proj, up_proj, down_proj, enc_weight, enc_bias, dec_weight, dec_bias):
    gate_full, up_full = (
        lax.all_gather(gate_proj, "rows", axis=0, tiled=True),
        lax.all_gather(up_proj, "rows", axis=0, tiled=True),
    )
    batches = activations_in.shape[0]
    batch_tokens = activations_in.shape[1]
    all_tokens = batches * batch_tokens
    token_rows = activations_in.reshape(all_tokens, activations_in.shape[2])
    portion = lax.all_gather(token_rows, "latent", axis=1, tiled=True)
    gate_term = jnp.dot(portion, gate_full, preferred_element_type=jnp.float32)
    up_term = jnp.dot(portion, up_full, preferred_element_type=jnp.float32)
    hidden = (jax.nn.gelu(gate_term, approximate=True) * up_term).astype(jnp.bfloat16)
    partial_value = jnp.dot(hidden, down_proj, preferred_element_type=jnp.float32)
    features = lax.psum(partial_value, "latent").astype(jnp.bfloat16)
    features = features.reshape(batches, batch_tokens, features.shape[1])
    enc_scale = MODEL_WIDTH ** (-0.5)
    dec_scale = LATENTS ** (-0.5)
    inputs = features[0]
    local_pre = jnp.dot(inputs, enc_weight, preferred_element_type=jnp.float32)
    pre_latent = enc_scale * row_total(local_pre) + enc_bias
    latents = (jax.nn.softplus(sharpness * pre_latent) / sharpness).astype(jnp.bfloat16)
    local_rebuilt = jnp.dot(latents, dec_weight, preferred_element_type=jnp.float32)
    rebuilt_share = lax.psum_scatter(local_rebuilt, "latent", scatter_dimension=1, tiled=True)
    share_cols = rebuilt_share.shape[1]
    col_offset = lax.axis_index("latent") * share_cols
    inputs_here = lax.dynamic_slice_in_dim(inputs, col_offset, share_cols, 1)
    bias_here = lax.dynamic_slice_in_dim(dec_bias, col_offset, share_cols, 0)
    grad_share = (
        2.0 * (dec_scale * rebuilt_share + bias_here - inputs_here.astype(jnp.float32))
    ).astype(jnp.bfloat16)
    residual_grad = lax.all_gather(grad_share, "latent", axis=1, tiled=True)
    local_back = lax.dot_general(
        residual_grad, dec_weight, (((1,), (1,)), ((), ())), preferred_element_type=jnp.float32
    )
    back_sum = row_total(local_back)
    latent_grad = (
        jax.nn.sigmoid(sharpness * pre_latent) * (dec_scale * back_sum + sparsity_cost)
    ).astype(jnp.bfloat16)
    dec_grad = dec_scale * lax.dot_general(
        latents, residual_grad, (((0,), (0,)), ((), ())), preferred_element_type=jnp.float32
    )
    enc_grad = enc_scale * lax.dot_general(
        inputs, latent_grad, (((0,), (0,)), ((), ())), preferred_element_type=jnp.float32
    )
    enc_bias = enc_bias - enc_bias_rate * jnp.sum(latent_grad, axis=0, dtype=jnp.float32)
    dec_bias = dec_bias - dec_bias_rate * jnp.sum(residual_grad, axis=0, dtype=jnp.float32)
    enc_weight = (enc_weight.astype(jnp.float32) - weight_rate * enc_grad).astype(jnp.bfloat16)
    dec_weight = (dec_weight.astype(jnp.float32) - weight_rate * dec_grad).astype(jnp.bfloat16)
    return (enc_weight, enc_bias, dec_weight, dec_bias)


def solution(mesh):
    return jax.shard_map(
        body,
        mesh=mesh,
        in_specs=(
            P("groups", None, "latent"),
            P("rows", "latent"),
            P("rows", "latent"),
            P("latent", "rows"),
            P(("groups", "rows"), "latent"),
            P(("groups", "latent")),
            P(("groups", "latent"), "rows"),
            P(("groups", "rows")),
        ),
        out_specs=(
            P(("groups", "rows"), "latent"),
            P(("groups", "latent")),
            P(("groups", "latent"), "rows"),
            P(("groups", "rows")),
        ),
        check_vma=False,
    )
```

profile of v0, /device:TPU:0, one launch (start us, length us, event | category | flops | bytes accessed | tf_op | source)
XLA Modules:
  0.0 395.9 jit_solution(4908214912626969955)
XLA Ops:
  7.2 0.0 copy-start
  7.2 0.0 all-gather.4.cloned.1.call-start
  7.2 0.7 all-gather.4.cloned.1.call-update
  7.9 0.0 all-gather.6.cloned.1.call-start
  8.0 0.7 all-gather.6.cloned.1.call-update
  8.7 0.0 all-reduce.4.cloned.1.call-start
  8.7 18.5 %all-gather = bf16[1,128,2304]{1,2,0:T(8,128)(2,1)S(1)} all-gather(bf16[1,128,576]{1,2,0:T(8,128)(2,1)} %param.8), channel_id=2, replica_groups=mesh['groups'=2,'latent'=4,'rows'=4] {'latent'}, dimensions={2}, use_global_device_ids=true | all-gather | bytes 737280 | tf_op jit(solution)/shard_map/all_gather | solution.py:30
  27.2 25.9 %all-gather.4.cloned.1.call-done = bf16[2304,1152]{1,0:T(8,128)(2,1)} async-done(((bf16[576,1152]{1,0:T(8,128)(2,1)}), bf16[2304,1152]{1,0:T(8,128)(2,1)}) %all-gather.4.cloned.1.call-update) | async-done | bytes 5308432 | tf_op jit(solution)/shard_map/all_gather | solution.py:23
  53.1 3.5 fusion.14
  56.6 38.9 %all-gather.6.cloned.1.call-done = bf16[2304,1152]{1,0:T(8,128)(2,1)} async-done(((bf16[576,1152]{1,0:T(8,128)(2,1)}), bf16[2304,1152]{1,0:T(8,128)(2,1)}) %all-gather.6.cloned.1.call-update) | async-done | bytes 5308432 | tf_op jit(solution)/shard_map/all_gather | solution.py:24
  95.5 4.0 fusion.3
  99.4 25.3 %all-reduce.7 = bf16[128,576]{0,1:T(8,128)(2,1)S(1)} all-reduce(f32[128,576]{0,1:T(8,128)S(1)} %fusion.3), channel_id=1, replica_groups=mesh['groups'=2,'latent'=4,'rows'=4] {'latent'}, use_global_device_ids=true, to_apply=%region_0.0 | all-reduce | flops 73728 | bytes 442368 | tf_op jit(solution)/shard_map/psum | solution.py:35
  124.8 12.0 %convolution_convert_fusion.1 = bf16[128,16384]{1,0:T(8,128)(2,1)} fusion(bf16[128,576]{0,1:T(8,128)(2,1)S(1)} %all-reduce.7, bf16[576,16384]{1,0:T(8,128)(2,1)} %param.12), kind=kOutput, calls=%fused_computation.4 | convolution fusion | flops 2418016256 | bytes 23216128 | tf_op jit(solution)/shard_map/dot_general | solution.py:40
  136.7 0.0 all-reduce.4.cloned.1.call-update
  136.8 0.2 reduce-scatter.2.cloned.1.call-start
  137.0 82.7 %all-reduce.4.cloned.1.call-done = bf16[128,16384]{1,0:T(8,128)(2,1)} async-done(((bf16[128,16384]{1,0:T(8,128)(2,1)}), bf16[128,16384]{1,0:T(8,128)(2,1)}) %all-reduce.4.cloned.1.call-update) | async-done | bytes 4194320 | tf_op jit(solution)/shard_map/psum | solution.py:18
  219.7 15.9 %fusion.25 = f32[128,576]{0,1:T(8,128)} fusion(bf16[16384,576]{0,1:T(8,128)(2,1)} %param.14, bf16[128,16384]{1,0:T(8,128)(2,1)} %all-reduce.4.cloned.1.call-done, f32[16384]{0:T(1024)S(1)} %copy-done.2), kind=kOutput, calls=%fused_computation.36 | convolution fusion | flops 2441084928 | bytes 23429120 | tf_op jit(solution)/shard_map/dot_general | solution.py:43
  235.6 0.0 reduce-scatter.2.cloned.1.call-update
  235.6 0.0 all-reduce.6.cloned.1.call-start
  235.7 0.1 dynamic_slice.6
  235.8 20.4 %reduce-scatter.2.cloned.1.call-done = f32[128,144]{0,1:T(8,128)} async-done(((f32[128,576]{0,1:T(8,128)}), f32[128,144]{0,1:T(8,128)}) %reduce-scatter.2.cloned.1.call-update) | async-done | bytes 73744 | tf_op jit(solution)/shard_map/reduce_scatter | solution.py:44
  256.2 1.0 multiply_convert_fusion.1
  257.1 13.5 %all_gather.15 = bf16[128,576]{0,1:T(8,128)(2,1)S(1)} all-gather(bf16[128,144]{0,1:T(8,128)(2,1)S(1)} %multiply_convert_fusion.1), channel_id=1, replica_groups=mesh['groups'=2,'latent'=4,'rows'=4] {'latent'}, dimensions={1}, use_global_device_ids=true | all-gather | bytes 184320 | tf_op jit(solution)/shard_map/all_gather | solution.py:52
  270.6 12.0 %convolution_convert_fusion = bf16[128,16384]{1,0:T(8,128)(2,1)} fusion(bf16[128,576]{0,1:T(8,128)(2,1)S(1)} %all_gather.15, bf16[16384,576]{0,1:T(8,128)(2,1)} %param.14), kind=kOutput, calls=%fused_computation.3 | convolution fusion | flops 2418016256 | bytes 23216128 | tf_op jit(solution)/shard_map/dot_general | solution.py:53
  282.6 0.1 convert_reduce_fusion.1
  282.7 0.0 all-reduce.6.cloned.1.call-update
  282.7 0.6 multiply_subtract_fusion.1
  283.3 32.5 %subtract_convert_fusion = bf16[16384,576]{0,1:T(8,128)(2,1)} fusion(bf16[16384,576]{0,1:T(8,128)(2,1)} %param.14, bf16[128,576]{0,1:T(8,128)(2,1)S(1)} %all_gather.15, bf16[128,16384]{1,0:T(8,128)(2,1)} %all-reduce.4.cloned.1.call-done, f32[16384]{0:T(1024)S(1)} %copy-done.2), kind=kOutput, calls=%fused_computation | convolution fusion | flops 2478833664 | bytes 42156032 | tf_op jit(solution)/shard_map/dot_general | solution.py:60
  315.8 50.7 %all-reduce.6.cloned.1.call-done = bf16[128,16384]{1,0:T(8,128)(2,1)} async-done(((bf16[128,16384]{1,0:T(8,128)(2,1)}), bf16[128,16384]{1,0:T(8,128)(2,1)}) %all-reduce.6.cloned.1.call-update) | async-done | bytes 4194320 | tf_op jit(solution)/shard_map/psum | solution.py:18
  366.5 7.7 %convert_reduce_fusion = (f32[16384]{0:T(1024)S(1)}, bf16[128,16384]{1,0:T(8,128)(2,1)}) fusion(bf16[128,16384]{1,0:T(8,128)(2,1)} %all-reduce.6.cloned.1.call-done, f32[16384]{0:T(1024)S(1)} %copy-done.2, bf16[128,16384]{1,0:T(8,128)(2,1)} %all-reduce.4.cloned.1.call-done), kind=kLoop, calls=%fused_computation.7 | loop fusion | flops 29343744 | bytes 12713984 | tf_op jit(solution)/shard_map/reduce_sum | solution.py:66
  374.2 14.5 %subtract_convert_fusion.1 = bf16[576,16384]{1,0:T(8,128)(2,1)} fusion(bf16[576,16384]{1,0:T(8,128)(2,1)} %param.12, bf16[128,576]{0,1:T(8,128)(2,1)S(1)} %all-reduce.7, bf16[128,16384]{1,0:T(8,128)(2,1)} %get-tuple-element.5), kind=kOutput, calls=%fused_computation.1 | convolution fusion | flops 2453667840 | bytes 42090496 | tf_op jit(solution)/shard_map/dot_general | solution.py:63
  388.7 0.6 multiply_subtract_fusion
  (7 shorter events, 0.0 us)
Async XLA Ops:
  7.2 88.3 %copy-start = (bf16[1152,576]{0,1:T(8,128)(2,1)S(1)}, bf16[1152,576]{0,1:T(8,128)(2,1)}, u32[]{:S(2)}) copy-start(bf16[1152,576]{0,1:T(8,128)(2,1)} %param.11) | copy-start | bytes 3981316
  7.2 45.9 %all-gather.4.cloned.1.call-start = ((), (), s32[]{:S(2)}) async-start(), calls=%async_computation.1 | async-start | bytes 6635520 | tf_op jit(solution)/shard_map/all_gather | solution.py:23
  7.9 87.5 %all-gather.6.cloned.1.call-start = ((), (), s32[]{:S(2)}) async-start(), calls=%async_computation.2 | async-start | bytes 6635520 | tf_op jit(solution)/shard_map/all_gather | solution.py:24
  8.7 211.0 %all-reduce.4.cloned.1.call-start = ((), (), s32[]{:S(2)}) async-start(), calls=%async_computation.3 | async-start | bytes 8388608 | tf_op jit(solution)/shard_map/psum | solution.py:18
  124.7 94.9 %copy-start.2 = (f32[16384]{0:T(1024)S(1)}, f32[16384]{0:T(1024)}, u32[]{:S(2)}) copy-start(f32[16384]{0:T(1024)} %param.13) | copy-start | bytes 196612
  136.8 98.9 %copy-start.3 = (f32[576]{0:T(1024)S(1)}, f32[576]{0:T(1024)}, u32[]{:S(2)}) copy-start(f32[576]{0:T(1024)} %param.15) | copy-start | bytes 6916
  136.8 119.4 %reduce-scatter.2.cloned.1.call-start = ((), (), s32[]{:S(2)}) async-start(), calls=%async_computation.4 | async-start | bytes 368640 | tf_op jit(solution)/shard_map/reduce_scatter | solution.py:44
  235.6 130.9 %all-reduce.6.cloned.1.call-start = ((), (), s32[]{:S(2)}) async-start(), calls=%async_computation.5 | async-start | bytes 8388608 | tf_op jit(solution)/shard_map/psum | solution.py:18
  374.2 15.1 %copy-start.1 = (bf16[1152,576]{0,1:T(8,128)(2,1)S(1)}, bf16[1152,576]{0,1:T(8,128)(2,1)}, u32[]{:S(2)}) copy-start(bf16[1152,576]{0,1:T(8,128)(2,1)} %param.11) | copy-start | bytes 3981316
Sparse Core Ops, SparseCore 0:
  9.5 43.4 all-gather.3
  54.6 40.7 all-gather.5
  136.9 82.7 all-reduce.3
  235.8 20.3 reduce-scatter.1
  282.9 83.6 all-reduce.5
where the time goes:
time: 396 us
  waiting for transfers between devices  220 us (56%)
  matrix products  94.3 us (24%)
  blocking collectives  57.3 us (14%)
  between operations  13.8 us (3%)
  other arithmetic  10 us (3%)
    psum x2, waiting for transfers between devices, row_total(): return lax.psum(term.astype(jnp.bfloat16), 'rows').astype(jnp.float32)  133 us
    all_gather x1, waiting for transfers between devices, body(): lax.all_gather(up_proj, 'rows', axis=0, tiled=True)  38.9 us
    dot_general x1, matrix products, body(): lax.dot_general(latents, residual_grad, (((0,), (0,)), ((), ())), preferr...  32.5 us
    all_gather x1, waiting for transfers between devices, body(): lax.all_gather(gate_proj, 'rows', axis=0, tiled=True)  25.9 us
    psum x1, blocking collectives, body(): features = lax.psum(partial_value, 'latent').astype(jnp.bfloat16)  25.3 us
    reduce_scatter x1, waiting for transfers between devices, body(): lax.psum_scatter(local_rebuilt, 'latent', scatter_dimension=1, tiled=True)  20.4 us
    all_gather x1, blocking collectives, body(): portion = lax.all_gather(token_rows, 'latent', axis=1, tiled=True)  18.5 us
    dot_general x1, matrix products, body(): jnp.dot(latents, dec_weight, preferred_element_type=jnp.float32)  15.9 us
  transfers between devices with their start and end apart: 5, of which 5 were waited for; matrix products, arithmetic and copies ran while one was open for 9% of the time, Pallas kernels for 0%

commit v1 on v0

v1 whole, which is shorter than its diff:
```python
import jax
import jax.numpy as jnp
from jax import lax
from jax.sharding import PartitionSpec as P

MODEL_WIDTH = 2304
LATENTS = 65536


sparsity_cost = 0.1
sharpness = 8.0
weight_rate = 2.0
enc_bias_rate = 0.01
dec_bias_rate = 0.002

BF16 = jnp.bfloat16
F32 = jnp.float32


def swap(x, axis, n, bit):
    return lax.ppermute(x, axis, [(i, i ^ bit) for i in range(n)])


def halves_scatter(x, axis, n, wire):
    me = lax.axis_index(axis)
    bit = 1
    while bit < n:
        size = x.shape[0] // 2
        mine = (me // bit) % 2
        keep = lax.dynamic_slice_in_dim(x, mine * size, size, 0)
        give = lax.dynamic_slice_in_dim(x, (1 - mine) * size, size, 0)
        got = swap(give.astype(wire), axis, n, bit)
        x = keep.astype(F32) + got.astype(F32)
        bit *= 2
    return x


def token_offset(axis, n, tokens):
    me = lax.axis_index(axis)
    offset, size, bit = 0, tokens, 1
    while bit < n:
        size //= 2
        offset = offset + ((me // bit) % 2) * size
        bit *= 2
    return offset, size


def halves_gather(x, axis, n):
    me = lax.axis_index(axis)
    bit = n // 2
    while bit >= 1:
        got = swap(x, axis, n, bit)
        first = ((me // bit) % 2) == 0
        x = jnp.concatenate([jnp.where(first, x, got), jnp.where(first, got, x)], axis=0)
        bit //= 2
    return x


def direct_scatter(x, axis, n, wire):
    me = lax.axis_index(axis)
    size = x.shape[0] // n
    total = lax.dynamic_slice_in_dim(x, me * size, size, 0)
    gots = []
    for shift in range(1, n):
        to = lax.rem(me + shift, n)
        give = lax.dynamic_slice_in_dim(x, to * size, size, 0).astype(wire)
        gots.append(lax.ppermute(give, axis, [(i, (i + shift) % n) for i in range(n)]))
    for got in gots:
        total = total + got.astype(F32)
    return total


def direct_gather(x, axis, n):
    me = lax.axis_index(axis)
    size = x.shape[0]
    out = jnp.zeros((size * n,) + x.shape[1:], x.dtype)
    parts = [(me, x)]
    for shift in range(1, n):
        got = lax.ppermute(x, axis, [(i, (i + shift) % n) for i in range(n)])
        parts.append((lax.rem(me - shift + n, n), got))
    for at, part in parts:
        out = lax.dynamic_update_slice_in_dim(out, part, at * size, 0)
    return out


def body(n_latent, n_rows, activations_in, gate_proj, up_proj, down_proj, enc_weight, enc_bias, dec_weight, dec_bias):
    tokens = activations_in.shape[1]
    width = enc_weight.shape[0]
    local = enc_weight.shape[1]
    here = activations_in.reshape(tokens, activations_in.shape[2])
    if n_latent == n_rows:
        pairs = [(a * n_rows + b, b * n_rows + a) for a in range(n_latent) for b in range(n_rows)]
        portion = lax.ppermute(here, ("latent", "rows"), pairs)
    else:
        everything = lax.all_gather(here, "latent", axis=1, tiled=True)
        portion = lax.dynamic_slice_in_dim(everything, lax.axis_index("rows") * width, width, 1)
    small = n_latent <= 8
    scatter_l = (lambda v: direct_scatter(v, "latent", n_latent, F32)) if small else (
        lambda v: lax.psum_scatter(v, "latent", scatter_dimension=0, tiled=True))
    gather_l = (lambda v: direct_gather(v, "latent", n_latent)) if small else (
        lambda v: lax.all_gather(v, "latent", axis=0, tiled=True))

    gate_part = jnp.dot(portion, gate_proj, preferred_element_type=F32)
    up_part = jnp.dot(portion, up_proj, preferred_element_type=F32)
    both = halves_scatter(jnp.concatenate([gate_part, up_part], axis=1), "rows", n_rows, F32)
    gate_term, up_term = both[:, :gate_proj.shape[1]], both[:, gate_proj.shape[1]:]
    hidden = (jax.nn.gelu(gate_term, approximate=True) * up_term).astype(BF16)
    hidden = halves_gather(hidden, "rows", n_rows)
    partial_value = jnp.dot(hidden, down_proj, preferred_element_type=F32)
    inputs_here = scatter_l(partial_value).astype(BF16)
    inputs = gather_l(inputs_here)

    enc_scale = MODEL_WIDTH ** (-0.5)
    dec_scale = LATENTS ** (-0.5)
    chunks = max(1, min(4, local // 512))
    step = local // chunks
    local_rebuilt = jnp.zeros((tokens, width), F32)
    latents, pres = [], []
    for c in range(chunks):
        part = jnp.dot(inputs, enc_weight[:, c * step:(c + 1) * step], preferred_element_type=F32).astype(BF16)
        encoded = halves_scatter(part, "rows", n_rows, BF16)
        pre = enc_scale * encoded + enc_bias[c * step:(c + 1) * step]
        pres.append(pre)
        mine = (jax.nn.softplus(sharpness * pre) / sharpness).astype(BF16)
        full = halves_gather(mine, "rows", n_rows)
        latents.append(full)
        local_rebuilt = local_rebuilt + jnp.dot(full, dec_weight[c * step:(c + 1) * step], preferred_element_type=F32)
    rebuilt_share = scatter_l(local_rebuilt)
    grad_share = (
        2.0 * (dec_scale * rebuilt_share + dec_bias - inputs_here.astype(F32))
    ).astype(BF16)
    residual_grad = gather_l(grad_share)
    grads = []
    for c in range(chunks):
        part = lax.dot_general(
            residual_grad, dec_weight[c * step:(c + 1) * step], (((1,), (1,)), ((), ())), preferred_element_type=F32
        ).astype(BF16)
        back = halves_scatter(part, "rows", n_rows, BF16)
        mine = (jax.nn.sigmoid(sharpness * pres[c]) * (dec_scale * back + sparsity_cost)).astype(BF16)
        grads.append(halves_gather(mine, "rows", n_rows))
    latents = jnp.concatenate(latents, axis=1)
    latent_grad = jnp.concatenate(grads, axis=1)
    dec_grad = dec_scale * lax.dot_general(
        latents, residual_grad, (((0,), (0,)), ((), ())), preferred_element_type=F32
    )
    enc_grad = enc_scale * lax.dot_general(
        inputs, latent_grad, (((0,), (0,)), ((), ())), preferred_element_type=F32
    )
    enc_bias = enc_bias - enc_bias_rate * jnp.sum(latent_grad, axis=0, dtype=F32)
    dec_bias = dec_bias - dec_bias_rate * jnp.sum(residual_grad, axis=0, dtype=F32)
    enc_weight = (enc_weight.astype(F32) - weight_rate * enc_grad).astype(BF16)
    dec_weight = (dec_weight.astype(F32) - weight_rate * dec_grad).astype(BF16)
    return (enc_weight, enc_bias, dec_weight, dec_bias)


def solution(mesh):
    def step(*args):
        return body(mesh.shape["latent"], mesh.shape["rows"], *args)

    return jax.shard_map(
        step,
        mesh=mesh,
        in_specs=(
            P("groups", None, "latent"),
            P("rows", "latent"),
            P("rows", "latent"),
            P("latent", "rows"),
            P(("groups", "rows"), "latent"),
            P(("groups", "latent")),
            P(("groups", "latent"), "rows"),
            P(("groups", "rows")),
        ),
        out_specs=(
            P(("groups", "rows"), "latent"),
            P(("groups", "latent")),
            P(("groups", "latent"), "rows"),
            P(("groups", "rows")),
        ),
        check_vma=False,
    )
```

time: 396 us -> 365 us (0.922); the launches traced: 396 us -> 358 us
  waiting for transfers between devices: 220 us -> 139 us
  starting transfers between devices: 0.38 us -> 63.1 us
  blocking collectives: 57.3 us -> 0 us
  other arithmetic: 10 us -> 38.1 us
  local copies, waits for them, and re-layouts: 0.11 us -> 23.9 us
  between operations: 13.8 us -> 1.97 us
    ppermute x0 -> x49, waiting for transfers between devices: none -> 139 us  [the longest x36 82.7 us: swap(): return lax.ppermute(x, axis, [(i, i ^ bit) for i in range(n)])]
    psum x2 -> x0, waiting for transfers between devices: 133 us -> none  [row_total(): return lax.psum(term.astype(jnp.bfloat16), 'rows').astype(jnp.float32)]
    all_gather x2 -> x0, waiting for transfers between devices: 64.8 us -> none  [the longest x1 38.9 us: body(): lax.all_gather(up_proj, 'rows', axis=0, tiled=True)]
    ppermute x0 -> x49, starting transfers between devices: none -> 63.1 us  [the longest x36 40.8 us: swap(): return lax.ppermute(x, axis, [(i, i ^ bit) for i in range(n)])]
    all_gather x2 -> x0, blocking collectives: 32 us -> none  [the longest x1 18.5 us: body(): portion = lax.all_gather(token_rows, 'latent', axis=1, tiled=True)]
    psum x1 -> x0, blocking collectives: 25.3 us -> none  [body(): features = lax.psum(partial_value, 'latent').astype(jnp.bfloat16)]
    reduce_scatter x1 -> x0, waiting for transfers between devices: 20.4 us -> none  [body(): lax.psum_scatter(local_rebuilt, 'latent', scatter_dimension=1, tiled=True)]
    dynamic_update_slice x0 -> x8, local copies, waits for them, and re-layouts: none -> 18.1 us  [direct_gather(): out = lax.dynamic_update_slice_in_dim(out, part, at * size, 0)]
  transfers between devices with their start and end apart: 5 -> 49, of which waited for: 5 -> 29; matrix products, arithmetic and copies ran while one was open for 9% -> 9% of each run, Pallas kernels for 0% -> 0%
where the time goes in v1:
time: 365 us; the launch traced here: 358 us
  waiting for transfers between devices  139 us (38%)
  matrix products  92.1 us (25%)
  starting transfers between devices  63.1 us (17%)
  other arithmetic  38.1 us (10%)
  local copies, waits for them, and re-layouts  23.9 us (7%)
    ppermute x36, waiting for transfers between devices, swap(): return lax.ppermute(x, axis, [(i, i ^ bit) for i in range(n)])  82.7 us
    ppermute x6, waiting for transfers between devices, direct_scatter(): lax.ppermute(give, axis, [(i, (i + shift) % n) for i in range(n)])  49.1 us
    ppermute x36, starting transfers between devices, swap(): return lax.ppermute(x, axis, [(i, i ^ bit) for i in range(n)])  40.8 us
    dot_general x1, matrix products, body(): lax.dot_general(inputs, latent_grad, (((0,), (0,)), ((), ())), preferred_...  30.2 us
    reduce_sum x1, other arithmetic, body(): jnp.sum(latent_grad, axis=0, dtype=F32)  23.8 us
    dot_general x1, matrix products, body(): lax.dot_general(latents, residual_grad, (((0,), (0,)), ((), ())), preferr...  22.3 us
    dynamic_update_slice x8, local copies, waits for them, and re-layouts, direct_gather(): out = lax.dynamic_update_slice_in_dim(out, part, at * size, 0)  18.1 us
    dot_general x4, matrix products, body(): lax.dot_general(residual_grad, dec_weight[c * step:(c + 1) * step], (((1,...  17.4 us
  transfers between devices with their start and end apart: 49, of which 29 were waited for; matrix products, arithmetic and copies ran while one was open for 9% of the time, Pallas kernels for 0%

profile of v1, /device:TPU:0, one launch (start us, length us, event | category | flops | bytes accessed | tf_op | source)
XLA Modules:
  0.0 358.1 jit_solution(14609580137279860677)
XLA Ops:
  4.6 6.7 %collective-permute-start.1 = (f32[64,2304]{1,0:T(8,128)S(1)}, f32[64,2304]{1,0:T(8,128)}, u32[]{:S(2)}, u32[]{:S(2)}) collective-permute-start(f32[64,2304]{1,0:T(8,128)S(1)} %fusion.52), channel_id=1, source_target_pairs={{0,1},{1,0},{2,3},{3,2},{4,5},{5,4},{6,7},{7,6},{8,9},{9,8},{10,11... | collective-permute-start | bytes 1769480 | tf_op jit(solution)/shard_map/ppermute | solution.py:21
  14.3 8.6 %collective-permute-start.2 = (f32[32,2304]{1,0:T(8,128)S(1)}, f32[32,2304]{1,0:T(8,128)S(1)}, u32[]{:S(2)}, u32[]{:S(2)}) collective-permute-start(f32[32,2304]{1,0:T(8,128)S(1)} %constant_dynamic-slice_fusion.14), channel_id=1, source_target_pairs={{0,2},{1,3},{2,0},{3,1},{4,6},{5,7},{6,4},{7,5},{8,10},{9,11},{10,... | collective-permute-start | bytes 884744 | tf_op jit(solution)/shard_map/ppermute | solution.py:21
  22.9 7.3 %collective-permute-done.2 = f32[32,2304]{1,0:T(8,128)S(1)} collective-permute-done((f32[32,2304]{1,0:T(8,128)S(1)}, f32[32,2304]{1,0:T(8,128)S(1)}, u32[]{:S(2)}, u32[]{:S(2)}) %collective-permute-start.2) | collective-permute-done | bytes 294944 | tf_op jit(solution)/shard_map/ppermute | solution.py:21
  40.3 6.8 %collective-permute-done.7 = f32[32,576]{0,1:T(8,128)S(1)} collective-permute-done((f32[32,576]{0,1:T(8,128)S(1)}, f32[32,576]{0,1:T(8,128)S(1)}, u32[]{:S(2)}, u32[]{:S(2)}) %collective-permute-start.7) | collective-permute-done | bytes 73760 | tf_op jit(solution)/shard_map/ppermute | solution.py:67
  47.2 17.6 %collective-permute-done.6 = f32[32,576]{0,1:T(8,128)S(1)} collective-permute-done((f32[32,576]{0,1:T(8,128)S(1)}, f32[32,576]{0,1:T(8,128)S(1)}, u32[]{:S(2)}, u32[]{:S(2)}) %collective-permute-start.6) | collective-permute-done | bytes 73760 | tf_op jit(solution)/shard_map/ppermute | solution.py:67
  89.4 3.5 convolution_convert_fusion.6
  92.9 3.5 convolution_convert_fusion.7
  103.6 4.2 %collective-permute-done.24 = bf16[32,4096]{1,0:T(8,128)(2,1)S(1)} collective-permute-done((bf16[32,4096]{1,0:T(8,128)(2,1)S(1)}, bf16[32,4096]{1,0:T(8,128)(2,1)S(1)}, u32[]{:S(2)}, u32[]{:S(2)}) %collective-permute-start.24) | collective-permute-done | bytes 262176 | tf_op jit(solution)/shard_map/ppermute | solution.py:21
  110.0 3.4 collective-permute-done.20
  115.6 3.4 collective-permute-done.16
  121.3 3.4 collective-permute-done.12
  126.9 3.4 collective-permute-done.25
  130.5 5.5 %collective-permute-done.21 = bf16[32,4096]{1,0:T(8,128)(2,1)S(1)} collective-permute-done((bf16[32,4096]{1,0:T(8,128)(2,1)S(1)}, bf16[32,4096]{1,0:T(8,128)(2,1)S(1)}, u32[]{:S(2)}, u32[]{:S(2)}) %collective-permute-start.21) | collective-permute-done | bytes 262176 | tf_op jit(solution)/shard_map/ppermute | solution.py:21
  136.1 5.4 %collective-permute-done.17 = bf16[32,4096]{1,0:T(8,128)(2,1)S(1)} collective-permute-done((bf16[32,4096]{1,0:T(8,128)(2,1)S(1)}, bf16[32,4096]{1,0:T(8,128)(2,1)S(1)}, u32[]{:S(2)}, u32[]{:S(2)}) %collective-permute-start.17) | collective-permute-done | bytes 262176 | tf_op jit(solution)/shard_map/ppermute | solution.py:21
  141.7 4.6 %collective-permute-done.13 = bf16[32,4096]{1,0:T(8,128)(2,1)S(1)} collective-permute-done((bf16[32,4096]{1,0:T(8,128)(2,1)S(1)}, bf16[32,4096]{1,0:T(8,128)(2,1)S(1)}, u32[]{:S(2)}, u32[]{:S(2)}) %collective-permute-start.13) | collective-permute-done | bytes 262176 | tf_op jit(solution)/shard_map/ppermute | solution.py:21
  153.7 4.3 %collective-permute-start.29 = (f32[32,576]{0,1:T(8,128)S(1)}, f32[32,576]{0,1:T(8,128)S(1)}, u32[]{:S(2)}, u32[]{:S(2)}) collective-permute-start(f32[32,576]{0,1:T(8,128)S(1)} %get-tuple-element.37), channel_id=1, source_target_pairs={{0,12},{4,0},{8,4},{12,8},{1,13},{5,1},{9,5},{13,9},{2,14},{6,2},{... | collective-permute-start | bytes 221192 | tf_op jit(solution)/shard_map/ppermute | solution.py:67
  159.2 6.3 %collective-permute-done.29 = f32[32,576]{0,1:T(8,128)S(1)} collective-permute-done((f32[32,576]{0,1:T(8,128)S(1)}, f32[32,576]{0,1:T(8,128)S(1)}, u32[]{:S(2)}, u32[]{:S(2)}) %collective-permute-start.29) | collective-permute-done | bytes 73760 | tf_op jit(solution)/shard_map/ppermute | solution.py:67
  165.5 18.3 %collective-permute-done.28 = f32[32,576]{0,1:T(8,128)S(1)} collective-permute-done((f32[32,576]{0,1:T(8,128)S(1)}, f32[32,576]{0,1:T(8,128)S(1)}, u32[]{:S(2)}, u32[]{:S(2)}) %collective-permute-start.28) | collective-permute-done | bytes 73760 | tf_op jit(solution)/shard_map/ppermute | solution.py:67
  204.5 4.3 %convolution_convert_fusion = bf16[128,4096]{1,0:T(8,128)(2,1)} fusion(bf16[128,576]{0,1:T(8,128)(2,1)S(1)} %dynamic_update_slice.31, bf16[16384,576]{0,1:T(8,128)(2,1)} %param.14), kind=kOutput, calls=%fused_computation.3 | convolution fusion | flops 604504064 | bytes 5914624 | tf_op jit(solution)/shard_map/dot_general | solution.py:135
  208.8 4.3 %convolution_convert_fusion.1 = bf16[128,4096]{1,0:T(8,128)(2,1)} fusion(bf16[128,576]{0,1:T(8,128)(2,1)S(1)} %dynamic_update_slice.31, bf16[16384,576]{0,1:T(8,128)(2,1)} %param.14), kind=kOutput, calls=%fused_computation.4 | convolution fusion | flops 604504064 | bytes 5914624 | tf_op jit(solution)/shard_map/dot_general | solution.py:135
  213.2 4.4 %convolution_convert_fusion.2 = bf16[128,4096]{1,0:T(8,128)(2,1)} fusion(bf16[128,576]{0,1:T(8,128)(2,1)S(1)} %dynamic_update_slice.31, bf16[16384,576]{0,1:T(8,128)(2,1)} %param.14), kind=kOutput, calls=%fused_computation.5 | convolution fusion | flops 604504064 | bytes 5914624 | tf_op jit(solution)/shard_map/dot_general | solution.py:135
  217.5 4.4 %convolution_convert_fusion.3 = bf16[128,4096]{1,0:T(8,128)(2,1)} fusion(bf16[128,576]{0,1:T(8,128)(2,1)S(1)} %dynamic_update_slice.31, bf16[16384,576]{0,1:T(8,128)(2,1)} %param.14), kind=kOutput, calls=%fused_computation.6 | convolution fusion | flops 604504064 | bytes 5914624 | tf_op jit(solution)/shard_map/dot_general | solution.py:135
  221.9 22.3 %subtract_convert_fusion = bf16[16384,576]{0,1:T(8,128)(2,1)} fusion(bf16[16384,576]{0,1:T(8,128)(2,1)} %param.14, bf16[128,576]{0,1:T(8,128)(2,1)S(1)} %dynamic_update_slice.31, bf16[64,4096]{1,0:T(8,128)(2,1)} %copy-done.20, bf16[64,4096]{1,0:T(8,128)(2,1)} %copy-done.19, bf16[64,4096]{1,0:T(8,128)(2,1)} %copy-done.22, bf16[64,4096]{1,0:T(8,128)(2,1)} %copy-done.21, ...), kind=kOutput, calls=%fused_computation | convolution fusion | flops 2487222272 | bytes 42090496 | tf_op jit(solution)/shard_map/dot_general | solution.py:143
  262.5 4.2 %collective-permute-done.42 = bf16[32,4096]{1,0:T(8,128)(2,1)S(1)} collective-permute-done((bf16[32,4096]{1,0:T(8,128)(2,1)S(1)}, bf16[32,4096]{1,0:T(8,128)(2,1)S(1)}, u32[]{:S(2)}, u32[]{:S(2)}) %collective-permute-start.42) | collective-permute-done | bytes 262176 | tf_op jit(solution)/shard_map/ppermute | solution.py:21
  268.1 4.2 %collective-permute-done.38 = bf16[32,4096]{1,0:T(8,128)(2,1)S(1)} collective-permute-done((bf16[32,4096]{1,0:T(8,128)(2,1)S(1)}, bf16[32,4096]{1,0:T(8,128)(2,1)S(1)}, u32[]{:S(2)}, u32[]{:S(2)}) %collective-permute-start.38) | collective-permute-done | bytes 262176 | tf_op jit(solution)/shard_map/ppermute | solution.py:21
  273.8 4.2 %collective-permute-done.34 = bf16[32,4096]{1,0:T(8,128)(2,1)S(1)} collective-permute-done((bf16[32,4096]{1,0:T(8,128)(2,1)S(1)}, bf16[32,4096]{1,0:T(8,128)(2,1)S(1)}, u32[]{:S(2)}, u32[]{:S(2)}) %collective-permute-start.34) | collective-permute-done | bytes 262176 | tf_op jit(solution)/shard_map/ppermute | solution.py:21
  279.4 4.2 %collective-permute-done.47 = bf16[32,4096]{1,0:T(8,128)(2,1)S(1)} collective-permute-done((bf16[32,4096]{1,0:T(8,128)(2,1)S(1)}, bf16[32,4096]{1,0:T(8,128)(2,1)S(1)}, u32[]{:S(2)}, u32[]{:S(2)}) %collective-permute-start.47) | collective-permute-done | bytes 262176 | tf_op jit(solution)/shard_map/ppermute | solution.py:21
  283.8 5.5 %collective-permute-done.43 = bf16[32,4096]{1,0:T(8,128)(2,1)S(1)} collective-permute-done((bf16[32,4096]{1,0:T(8,128)(2,1)S(1)}, bf16[32,4096]{1,0:T(8,128)(2,1)S(1)}, u32[]{:S(2)}, u32[]{:S(2)}) %collective-permute-start.43) | collective-permute-done | bytes 262176 | tf_op jit(solution)/shard_map/ppermute | solution.py:21
  289.4 5.5 %collective-permute-done.39 = bf16[32,4096]{1,0:T(8,128)(2,1)S(1)} collective-permute-done((bf16[32,4096]{1,0:T(8,128)(2,1)S(1)}, bf16[32,4096]{1,0:T(8,128)(2,1)S(1)}, u32[]{:S(2)}, u32[]{:S(2)}) %collective-permute-start.39) | collective-permute-done | bytes 262176 | tf_op jit(solution)/shard_map/ppermute | solution.py:21
  295.0 4.5 %collective-permute-done.35 = bf16[32,4096]{1,0:T(8,128)(2,1)S(1)} collective-permute-done((bf16[32,4096]{1,0:T(8,128)(2,1)S(1)}, bf16[32,4096]{1,0:T(8,128)(2,1)S(1)}, u32[]{:S(2)}, u32[]{:S(2)}) %collective-permute-start.35) | collective-permute-done | bytes 262176 | tf_op jit(solution)/shard_map/ppermute | solution.py:21
  303.3 30.2 %subtract_convert_fusion.1 = bf16[576,16384]{1,0:T(8,128)(2,1)} fusion(bf16[576,16384]{1,0:T(8,128)(2,1)} %param.12, bf16[128,576]{0,1:T(8,128)(2,1)S(1)} %copy-done.7, bf16[64,4096]{1,0:T(8,128)(2,1)S(1)} %get-tuple-element.11, bf16[64,4096]{1,0:T(8,128)(2,1)S(1)} %get-tuple-element.10, bf16[64,4096]{1,0:T(8,128)(2,1)} %get-tuple-element.9, ...), kind=kOutput, calls=%fused_computation.1 | convolution fusion | flops 2487222272 | bytes 42090496 | tf_op jit(solution)/shard_map/dot_general | solution.py:146
  333.5 23.8 %convert_reduce_fusion = f32[16384]{0:T(1024)S(1)} fusion(bf16[64,4096]{1,0:T(8,128)(2,1)S(1)} %get-tuple-element.11, bf16[64,4096]{1,0:T(8,128)(2,1)S(1)} %get-tuple-element.10, bf16[64,4096]{1,0:T(8,128)(2,1)} %get-tuple-element.9, bf16[64,4096]{1,0:T(8,128)(2,1)S(1)} %get-tuple-element.8, bf16[64,4096]{1,0:T(8,128)(2,1)} %get-tuple-element.7, ...), kind=kLoop, calls=%fused_computation.2 | loop fusion | flops 35635200 | bytes 4259840 | tf_op jit(solution)/shard_map/reduce_sum | solution.py:149
  (235 shorter events, 113.7 us)
Async XLA Ops:
  14.3 15.9 %collective-permute-start.2 = (f32[32,2304]{1,0:T(8,128)S(1)}, f32[32,2304]{1,0:T(8,128)S(1)}, u32[]{:S(2)}, u32[]{:S(2)}) collective-permute-start(f32[32,2304]{1,0:T(8,128)S(1)} %constant_dynamic-slice_fusion.14), channel_id=1, source_target_pairs={{0,2},{1,3},{2,0},{3,1},{4,6},{5,7},{6,4},{7,5},{8,10},{9,11},{10,... | collective-permute-start | bytes 884744 | tf_op jit(solution)/shard_map/ppermute | solution.py:21
  37.2 10.0 %collective-permute-start.7 = (f32[32,576]{0,1:T(8,128)S(1)}, f32[32,576]{0,1:T(8,128)S(1)}, u32[]{:S(2)}, u32[]{:S(2)}) collective-permute-start(f32[32,576]{0,1:T(8,128)S(1)} %get-tuple-element.40), channel_id=1, source_target_pairs={{0,12},{4,0},{8,4},{12,8},{1,13},{5,1},{9,5},{13,9},{2,14},{6,2},{... | collective-permute-start | bytes 221192 | tf_op jit(solution)/shard_map/ppermute | solution.py:67
  39.7 25.2 %collective-permute-start.6 = (f32[32,576]{0,1:T(8,128)S(1)}, f32[32,576]{0,1:T(8,128)S(1)}, u32[]{:S(2)}, u32[]{:S(2)}) collective-permute-start(f32[32,576]{0,1:T(8,128)S(1)} %get-tuple-element.41), channel_id=1, source_target_pairs={{0,8},{4,12},{8,0},{12,4},{1,9},{5,13},{9,1},{13,5},{2,10},{6,14},... | collective-permute-start | bytes 221192 | tf_op jit(solution)/shard_map/ppermute | solution.py:67
  39.7 25.2 %collective-permute-start.5 = (f32[32,576]{0,1:T(8,128)S(1)}, f32[32,576]{0,1:T(8,128)S(1)}, u32[]{:S(2)}, u32[]{:S(2)}) collective-permute-start(f32[32,576]{0,1:T(8,128)S(1)} %get-tuple-element.39), channel_id=1, source_target_pairs={{0,4},{4,8},{8,12},{12,0},{1,5},{5,9},{9,13},{13,1},{2,6},{6,10},{... | collective-permute-start | bytes 221192 | tf_op jit(solution)/shard_map/ppermute | solution.py:67
  66.1 12.2 %collective-permute-start.9 = (bf16[32,576]{0,1:T(8,128)(2,1)S(1)}, bf16[32,576]{0,1:T(8,128)(2,1)S(1)}, u32[]{:S(2)}, u32[]{:S(2)}) collective-permute-start(bf16[32,576]{0,1:T(8,128)(2,1)S(1)} %add_convert_fusion), channel_id=1, source_target_pairs={{0,8},{4,12},{8,0},{12,4},{1,9},{5,13},{9,1},{13,5},{2,10},{6,14},... | collective-permute-start | bytes 110600 | tf_op jit(solution)/shard_map/ppermute | solution.py:79
  68.1 12.1 %collective-permute-start.10 = (bf16[32,576]{0,1:T(8,128)(2,1)S(1)}, bf16[32,576]{0,1:T(8,128)(2,1)S(1)}, u32[]{:S(2)}, u32[]{:S(2)}) collective-permute-start(bf16[32,576]{0,1:T(8,128)(2,1)S(1)} %add_convert_fusion), channel_id=1, source_target_pairs={{0,12},{4,0},{8,4},{12,8},{1,13},{5,1},{9,5},{13,9},{2,14},{6,2},{... | collective-permute-start | bytes 110600 | tf_op jit(solution)/shard_map/ppermute | solution.py:79
  98.6 9.2 %collective-permute-start.24 = (bf16[32,4096]{1,0:T(8,128)(2,1)S(1)}, bf16[32,4096]{1,0:T(8,128)(2,1)S(1)}, u32[]{:S(2)}, u32[]{:S(2)}) collective-permute-start(bf16[32,4096]{1,0:T(8,128)(2,1)S(1)} %dynamic-slice_convert_fusion.4), channel_id=1, source_target_pairs={{0,2},{1,3},{2,0},{3,1},{4,6},{5,7},{6,4},{7,5},{8,10},{9,11},{10,... | collective-permute-start | bytes 786440 | tf_op jit(solution)/shard_map/ppermute | solution.py:21
  100.6 12.9 %collective-permute-start.20 = (bf16[32,4096]{1,0:T(8,128)(2,1)S(1)}, bf16[32,4096]{1,0:T(8,128)(2,1)S(1)}, u32[]{:S(2)}, u32[]{:S(2)}) collective-permute-start(bf16[32,4096]{1,0:T(8,128)(2,1)S(1)} %dynamic-slice_convert_fusion.5), channel_id=1, source_target_pairs={{0,2},{1,3},{2,0},{3,1},{4,6},{5,7},{6,4},{7,5},{8,10},{9,11},{10,... | collective-permute-start | bytes 786440 | tf_op jit(solution)/shard_map/ppermute | solution.py:21
  101.3 17.8 %collective-permute-start.16 = (bf16[32,4096]{1,0:T(8,128)(2,1)S(1)}, bf16[32,4096]{1,0:T(8,128)(2,1)S(1)}, u32[]{:S(2)}, u32[]{:S(2)}) collective-permute-start(bf16[32,4096]{1,0:T(8,128)(2,1)S(1)} %dynamic-slice_convert_fusion.6), channel_id=1, source_target_pairs={{0,2},{1,3},{2,0},{3,1},{4,6},{5,7},{6,4},{7,5},{8,10},{9,11},{10,... | collective-permute-start | bytes 786440 | tf_op jit(solution)/shard_map/ppermute | solution.py:21
  103.0 21.6 %collective-permute-start.12 = (bf16[32,4096]{1,0:T(8,128)(2,1)S(1)}, bf16[32,4096]{1,0:T(8,128)(2,1)S(1)}, u32[]{:S(2)}, u32[]{:S(2)}) collective-permute-start(bf16[32,4096]{1,0:T(8,128)(2,1)S(1)} %dynamic-slice_convert_fusion.7), channel_id=1, source_target_pairs={{0,2},{1,3},{2,0},{3,1},{4,6},{5,7},{6,4},{7,5},{8,10},{9,11},{10,... | collective-permute-start | bytes 786440 | tf_op jit(solution)/shard_map/ppermute | solution.py:21
  108.2 22.1 %collective-permute-start.25 = (bf16[32,4096]{1,0:T(8,128)(2,1)S(1)}, bf16[32,4096]{1,0:T(8,128)(2,1)S(1)}, u32[]{:S(2)}, u32[]{:S(2)}) collective-permute-start(bf16[32,4096]{1,0:T(8,128)(2,1)S(1)} %fusion.62), channel_id=1, source_target_pairs={{0,2},{1,3},{2,0},{3,1},{4,6},{5,7},{6,4},{7,5},{8,10},{9,11},{10,... | collective-permute-start | bytes 786440 | tf_op jit(solution)/shard_map/ppermute | solution.py:21
  113.8 22.1 %collective-permute-start.21 = (bf16[32,4096]{1,0:T(8,128)(2,1)S(1)}, bf16[32,4096]{1,0:T(8,128)(2,1)S(1)}, u32[]{:S(2)}, u32[]{:S(2)}) collective-permute-start(bf16[32,4096]{1,0:T(8,128)(2,1)S(1)} %fusion.60), channel_id=1, source_target_pairs={{0,2},{1,3},{2,0},{3,1},{4,6},{5,7},{6,4},{7,5},{8,10},{9,11},{10,... | collective-permute-start | bytes 786440 | tf_op jit(solution)/shard_map/ppermute | solution.py:21
  119.5 22.1 %collective-permute-start.17 = (bf16[32,4096]{1,0:T(8,128)(2,1)S(1)}, bf16[32,4096]{1,0:T(8,128)(2,1)S(1)}, u32[]{:S(2)}, u32[]{:S(2)}) collective-permute-start(bf16[32,4096]{1,0:T(8,128)(2,1)S(1)} %fusion.58), channel_id=1, source_target_pairs={{0,2},{1,3},{2,0},{3,1},{4,6},{5,7},{6,4},{7,5},{8,10},{9,11},{10,... | collective-permute-start | bytes 786440 | tf_op jit(solution)/shard_map/ppermute | solution.py:21
  125.1 21.2 %collective-permute-start.13 = (bf16[32,4096]{1,0:T(8,128)(2,1)S(1)}, bf16[32,4096]{1,0:T(8,128)(2,1)S(1)}, u32[]{:S(2)}, u32[]{:S(2)}) collective-permute-start(bf16[32,4096]{1,0:T(8,128)(2,1)S(1)} %fusion.56), channel_id=1, source_target_pairs={{0,2},{1,3},{2,0},{3,1},{4,6},{5,7},{6,4},{7,5},{8,10},{9,11},{10,... | collective-permute-start | bytes 786440 | tf_op jit(solution)/shard_map/ppermute | solution.py:21
  130.4 16.1 %collective-permute-start.26 = (bf16[64,4096]{1,0:T(8,128)(2,1)S(1)}, bf16[64,4096]{1,0:T(8,128)(2,1)S(1)}, u32[]{:S(2)}, u32[]{:S(2)}) collective-permute-start(bf16[64,4096]{1,0:T(8,128)(2,1)S(1)} %pad_maximum_fusion.3), channel_id=1, source_target_pairs={{0,1},{1,0},{2,3},{3,2},{4,5},{5,4},{6,7},{7,6},{8,9},{9,8},{10,11... | collective-permute-start | bytes 1572872 | tf_op jit(solution)/shard_map/ppermute | solution.py:21
  136.0 10.7 %collective-permute-start.22 = (bf16[64,4096]{1,0:T(8,128)(2,1)S(1)}, bf16[64,4096]{1,0:T(8,128)(2,1)S(1)}, u32[]{:S(2)}, u32[]{:S(2)}) collective-permute-start(bf16[64,4096]{1,0:T(8,128)(2,1)S(1)} %pad_maximum_fusion.2), channel_id=1, source_target_pairs={{0,1},{1,0},{2,3},{3,2},{4,5},{5,4},{6,7},{7,6},{8,9},{9,8},{10,11... | collective-permute-start | bytes 1572872 | tf_op jit(solution)/shard_map/ppermute | solution.py:21
  153.7 11.8 %collective-permute-start.29 = (f32[32,576]{0,1:T(8,128)S(1)}, f32[32,576]{0,1:T(8,128)S(1)}, u32[]{:S(2)}, u32[]{:S(2)}) collective-permute-start(f32[32,576]{0,1:T(8,128)S(1)} %get-tuple-element.37), channel_id=1, source_target_pairs={{0,12},{4,0},{8,4},{12,8},{1,13},{5,1},{9,5},{13,9},{2,14},{6,2},{... | collective-permute-start | bytes 221192 | tf_op jit(solution)/shard_map/ppermute | solution.py:67
  158.0 25.8 %collective-permute-start.28 = (f32[32,576]{0,1:T(8,128)S(1)}, f32[32,576]{0,1:T(8,128)S(1)}, u32[]{:S(2)}, u32[]{:S(2)}) collective-permute-start(f32[32,576]{0,1:T(8,128)S(1)} %get-tuple-element.38), channel_id=1, source_target_pairs={{0,8},{4,12},{8,0},{12,4},{1,9},{5,13},{9,1},{13,5},{2,10},{6,14},... | collective-permute-start | bytes 221192 | tf_op jit(solution)/shard_map/ppermute | solution.py:67
  158.0 25.8 %collective-permute-start.27 = (f32[32,576]{0,1:T(8,128)S(1)}, f32[32,576]{0,1:T(8,128)S(1)}, u32[]{:S(2)}, u32[]{:S(2)}) collective-permute-start(f32[32,576]{0,1:T(8,128)S(1)} %get-tuple-element.36), channel_id=1, source_target_pairs={{0,4},{4,8},{8,12},{12,0},{1,5},{5,9},{9,13},{13,1},{2,6},{6,10},{... | collective-permute-start | bytes 221192 | tf_op jit(solution)/shard_map/ppermute | solution.py:67
  184.7 8.9 %collective-permute-start.30 = (bf16[32,576]{0,1:T(8,128)(2,1)}, bf16[32,576]{0,1:T(8,128)(2,1)}, u32[]{:S(2)}, u32[]{:S(2)}) collective-permute-start(bf16[32,576]{0,1:T(8,128)(2,1)} %multiply_convert_fusion.4), channel_id=1, source_target_pairs={{0,4},{4,8},{8,12},{12,0},{1,5},{5,9},{9,13},{13,1},{2,6},{6,10},{... | collective-permute-start | bytes 110600 | tf_op jit(solution)/shard_map/ppermute | solution.py:79
  185.8 12.9 %collective-permute-start.31 = (bf16[32,576]{0,1:T(8,128)(2,1)}, bf16[32,576]{0,1:T(8,128)(2,1)}, u32[]{:S(2)}, u32[]{:S(2)}) collective-permute-start(bf16[32,576]{0,1:T(8,128)(2,1)} %multiply_convert_fusion.4), channel_id=1, source_target_pairs={{0,8},{4,12},{8,0},{12,4},{1,9},{5,13},{9,1},{13,5},{2,10},{6,14},... | collective-permute-start | bytes 110600 | tf_op jit(solution)/shard_map/ppermute | solution.py:79
  187.7 13.9 %collective-permute-start.32 = (bf16[32,576]{0,1:T(8,128)(2,1)}, bf16[32,576]{0,1:T(8,128)(2,1)}, u32[]{:S(2)}, u32[]{:S(2)}) collective-permute-start(bf16[32,576]{0,1:T(8,128)(2,1)} %multiply_convert_fusion.4), channel_id=1, source_target_pairs={{0,12},{4,0},{8,4},{12,8},{1,13},{5,1},{9,5},{13,9},{2,14},{6,2},{... | collective-permute-start | bytes 110600 | tf_op jit(solution)/shard_map/ppermute | solution.py:79
  251.9 9.2 %collective-permute-start.46 = (bf16[32,4096]{1,0:T(8,128)(2,1)S(1)}, bf16[32,4096]{1,0:T(8,128)(2,1)S(1)}, u32[]{:S(2)}, u32[]{:S(2)}) collective-permute-start(bf16[32,4096]{1,0:T(8,128)(2,1)S(1)} %dynamic-slice_convert_fusion), channel_id=1, source_target_pairs={{0,2},{1,3},{2,0},{3,1},{4,6},{5,7},{6,4},{7,5},{8,10},{9,11},{10,... | collective-permute-start | bytes 786440 | tf_op jit(solution)/shard_map/ppermute | solution.py:21
  254.2 12.6 %collective-permute-start.42 = (bf16[32,4096]{1,0:T(8,128)(2,1)S(1)}, bf16[32,4096]{1,0:T(8,128)(2,1)S(1)}, u32[]{:S(2)}, u32[]{:S(2)}) collective-permute-start(bf16[32,4096]{1,0:T(8,128)(2,1)S(1)} %dynamic-slice_convert_fusion.1), channel_id=1, source_target_pairs={{0,2},{1,3},{2,0},{3,1},{4,6},{5,7},{6,4},{7,5},{8,10},{9,11},{10,... | collective-permute-start | bytes 786440 | tf_op jit(solution)/shard_map/ppermute | solution.py:21
  255.4 17.0 %collective-permute-start.38 = (bf16[32,4096]{1,0:T(8,128)(2,1)S(1)}, bf16[32,4096]{1,0:T(8,128)(2,1)S(1)}, u32[]{:S(2)}, u32[]{:S(2)}) collective-permute-start(bf16[32,4096]{1,0:T(8,128)(2,1)S(1)} %dynamic-slice_convert_fusion.2), channel_id=1, source_target_pairs={{0,2},{1,3},{2,0},{3,1},{4,6},{5,7},{6,4},{7,5},{8,10},{9,11},{10,... | collective-permute-start | bytes 786440 | tf_op jit(solution)/shard_map/ppermute | solution.py:21
  256.7 21.3 %collective-permute-start.34 = (bf16[32,4096]{1,0:T(8,128)(2,1)S(1)}, bf16[32,4096]{1,0:T(8,128)(2,1)S(1)}, u32[]{:S(2)}, u32[]{:S(2)}) collective-permute-start(bf16[32,4096]{1,0:T(8,128)(2,1)S(1)} %dynamic-slice_convert_fusion.3), channel_id=1, source_target_pairs={{0,2},{1,3},{2,0},{3,1},{4,6},{5,7},{6,4},{7,5},{8,10},{9,11},{10,... | collective-permute-start | bytes 786440 | tf_op jit(solution)/shard_map/ppermute | solution.py:21
  261.4 22.2 %collective-permute-start.47 = (bf16[32,4096]{1,0:T(8,128)(2,1)S(1)}, bf16[32,4096]{1,0:T(8,128)(2,1)S(1)}, u32[]{:S(2)}, u32[]{:S(2)}) collective-permute-start(bf16[32,4096]{1,0:T(8,128)(2,1)S(1)} %multiply_convert_fusion), channel_id=1, source_target_pairs={{0,2},{1,3},{2,0},{3,1},{4,6},{5,7},{6,4},{7,5},{8,10},{9,11},{10,... | collective-permute-start | bytes 786440 | tf_op jit(solution)/shard_map/ppermute | solution.py:21
  267.0 22.2 %collective-permute-start.43 = (bf16[32,4096]{1,0:T(8,128)(2,1)S(1)}, bf16[32,4096]{1,0:T(8,128)(2,1)S(1)}, u32[]{:S(2)}, u32[]{:S(2)}) collective-permute-start(bf16[32,4096]{1,0:T(8,128)(2,1)S(1)} %multiply_convert_fusion.1), channel_id=1, source_target_pairs={{0,2},{1,3},{2,0},{3,1},{4,6},{5,7},{6,4},{7,5},{8,10},{9,11},{10,... | collective-permute-start | bytes 786440 | tf_op jit(solution)/shard_map/ppermute | solution.py:21
  272.6 22.2 %collective-permute-start.39 = (bf16[32,4096]{1,0:T(8,128)(2,1)S(1)}, bf16[32,4096]{1,0:T(8,128)(2,1)S(1)}, u32[]{:S(2)}, u32[]{:S(2)}) collective-permute-start(bf16[32,4096]{1,0:T(8,128)(2,1)S(1)} %multiply_convert_fusion.2), channel_id=1, source_target_pairs={{0,2},{1,3},{2,0},{3,1},{4,6},{5,7},{6,4},{7,5},{8,10},{9,11},{10,... | collective-permute-start | bytes 786440 | tf_op jit(solution)/shard_map/ppermute | solution.py:21
  278.3 21.3 %collective-permute-start.35 = (bf16[32,4096]{1,0:T(8,128)(2,1)S(1)}, bf16[32,4096]{1,0:T(8,128)(2,1)S(1)}, u32[]{:S(2)}, u32[]{:S(2)}) collective-permute-start(bf16[32,4096]{1,0:T(8,128)(2,1)S(1)} %multiply_convert_fusion.3), channel_id=1, source_target_pairs={{0,2},{1,3},{2,0},{3,1},{4,6},{5,7},{6,4},{7,5},{8,10},{9,11},{10,... | collective-permute-start | bytes 786440 | tf_op jit(solution)/shard_map/ppermute | solution.py:21
  283.7 16.0 %collective-permute-start.48 = (bf16[64,4096]{1,0:T(8,128)(2,1)S(1)}, bf16[64,4096]{1,0:T(8,128)(2,1)S(1)}, u32[]{:S(2)}, u32[]{:S(2)}) collective-permute-start(bf16[64,4096]{1,0:T(8,128)(2,1)S(1)} %pad_maximum_fusion.7), channel_id=1, source_target_pairs={{0,1},{1,0},{2,3},{3,2},{4,5},{5,4},{6,7},{7,6},{8,9},{9,8},{10,11... | collective-permute-start | bytes 1572872 | tf_op jit(solution)/shard_map/ppermute | solution.py:21
  289.3 10.6 %collective-permute-start.44 = (bf16[64,4096]{1,0:T(8,128)(2,1)S(1)}, bf16[64,4096]{1,0:T(8,128)(2,1)S(1)}, u32[]{:S(2)}, u32[]{:S(2)}) collective-permute-start(bf16[64,4096]{1,0:T(8,128)(2,1)S(1)} %pad_maximum_fusion.6), channel_id=1, source_target_pairs={{0,1},{1,0},{2,3},{3,2},{4,5},{5,4},{6,7},{7,6},{8,9},{9,8},{10,11... | collective-permute-start | bytes 1572872 | tf_op jit(solution)/shard_map/ppermute | solution.py:21
  (51 other events, 945.2 us)

commit v2 on v1

v2 whole, which is shorter than its diff:
```python
import functools

import jax
import jax.numpy as jnp
from jax import lax
from jax.experimental import pallas as pl
from jax.experimental.pallas import tpu as pltpu
from jax.sharding import PartitionSpec as P

MODEL_WIDTH = 2304
LATENTS = 65536


sparsity_cost = 0.1
sharpness = 8.0
weight_rate = 2.0
enc_bias_rate = 0.01
dec_bias_rate = 0.002

BF16 = jnp.bfloat16
F32 = jnp.float32


def swap(x, axis, n, bit):
    return lax.ppermute(x, axis, [(i, i ^ bit) for i in range(n)])


def halves_scatter(x, axis, n, wire):
    me = lax.axis_index(axis)
    bit = 1
    while bit < n:
        size = x.shape[0] // 2
        mine = (me // bit) % 2
        keep = lax.dynamic_slice_in_dim(x, mine * size, size, 0)
        give = lax.dynamic_slice_in_dim(x, (1 - mine) * size, size, 0)
        got = swap(give.astype(wire), axis, n, bit)
        x = keep.astype(F32) + got.astype(F32)
        bit *= 2
    return x


def halves_gather(x, axis, n):
    me = lax.axis_index(axis)
    bit = n // 2
    while bit >= 1:
        got = swap(x, axis, n, bit)
        first = ((me // bit) % 2) == 0
        x = jnp.concatenate([jnp.where(first, x, got), jnp.where(first, got, x)], axis=0)
        bit //= 2
    return x


def direct_scatter(x, axis, n, wire):
    me = lax.axis_index(axis)
    size = x.shape[0] // n
    total = lax.dynamic_slice_in_dim(x, me * size, size, 0)
    gots = []
    for shift in range(1, n):
        to = lax.rem(me + shift, n)
        give = lax.dynamic_slice_in_dim(x, to * size, size, 0).astype(wire)
        gots.append(lax.ppermute(give, axis, [(i, (i + shift) % n) for i in range(n)]))
    for got in gots:
        total = total + got.astype(F32)
    return total


def direct_gather(x, axis, n):
    me = lax.axis_index(axis)
    size = x.shape[0]
    out = jnp.zeros((size * n,) + x.shape[1:], x.dtype)
    parts = [(me, x)]
    for shift in range(1, n):
        got = lax.ppermute(x, axis, [(i, (i + shift) % n) for i in range(n)])
        parts.append((lax.rem(me - shift + n, n), got))
    for at, part in parts:
        out = lax.dynamic_update_slice_in_dim(out, part, at * size, 0)
    return out


def update_kernel(rate, has_buf, left_ref, right_ref, w_ref, *rest):
    out_ref, sums_ref = rest[1:] if has_buf else rest
    right = right_ref[...]
    grad = jnp.dot(left_ref[...], right, preferred_element_type=F32)
    out_ref[...] = (w_ref[...].astype(F32) - rate * grad).astype(out_ref.dtype)
    ones = jnp.ones((8, right.shape[0]), right.dtype)
    sums_ref[...] = jnp.dot(ones, right, preferred_element_type=F32)


def update(rate, left, right, weight, first, buf):
    depth, tokens = left.shape
    columns = right.shape[1]
    tile = min(2048, columns)
    base = first // tile
    block = pl.BlockSpec((depth, tile), lambda i: (0, base + i))
    in_specs = [
        pl.BlockSpec((depth, tokens), lambda i: (0, 0)),
        pl.BlockSpec((tokens, tile), lambda i: (0, i)),
        block,
    ]
    args = [left, right, weight]
    if buf is not None:
        in_specs.append(pl.BlockSpec(memory_space=pl.ANY))
        args.append(buf)
    return pl.pallas_call(
        functools.partial(update_kernel, rate, buf is not None),
        grid=(columns // tile,),
        out_shape=(
            jax.ShapeDtypeStruct(weight.shape, weight.dtype),
            jax.ShapeDtypeStruct((8, columns), F32),
        ),
        in_specs=in_specs,
        out_specs=(block, pl.BlockSpec((8, tile), lambda i: (0, i))),
        input_output_aliases={} if buf is None else {3: 0},
        compiler_params=pltpu.CompilerParams(vmem_limit_bytes=24 * 1024 * 1024),
        cost_estimate=pl.CostEstimate(
            flops=2 * depth * tokens * columns, bytes_accessed=4 * depth * columns, transcendentals=0
        ),
    )(*args)


def body(n_latent, n_rows, activations_in, gate_proj, up_proj, down_proj, enc_weight, enc_bias, dec_weight, dec_bias):
    tokens = activations_in.shape[1]
    width, local = enc_weight.shape
    here = activations_in.reshape(tokens, activations_in.shape[2])
    if n_latent == n_rows:
        pairs = [(a * n_rows + b, b * n_rows + a) for a in range(n_latent) for b in range(n_rows)]
        portion = lax.ppermute(here, ("latent", "rows"), pairs)
    else:
        everything = lax.all_gather(here, "latent", axis=1, tiled=True)
        portion = lax.dynamic_slice_in_dim(everything, lax.axis_index("rows") * width, width, 1)
    if n_latent <= 8:
        scatter_l = lambda v, wire: direct_scatter(v, "latent", n_latent, wire)
        gather_l = lambda v: direct_gather(v, "latent", n_latent)
    else:
        scatter_l = lambda v, wire: lax.psum_scatter(v, "latent", scatter_dimension=0, tiled=True)
        gather_l = lambda v: lax.all_gather(v, "latent", axis=0, tiled=True)

    gate_part = jnp.dot(portion, gate_proj, preferred_element_type=F32)
    up_part = jnp.dot(portion, up_proj, preferred_element_type=F32)
    both = jnp.concatenate([gate_part, up_part], axis=1).astype(BF16)
    both = halves_scatter(both, "rows", n_rows, BF16)
    gate_term, up_term = both[:, :gate_proj.shape[1]], both[:, gate_proj.shape[1]:]
    hidden = (jax.nn.gelu(gate_term, approximate=True) * up_term).astype(BF16)
    hidden = halves_gather(hidden, "rows", n_rows)
    partial_value = lax.dot_general(down_proj, hidden, (((0,), (1,)), ((), ())), preferred_element_type=F32)
    inputs_here = scatter_l(partial_value, BF16).astype(BF16)
    inputs = gather_l(inputs_here)
    share = inputs_here.shape[0]
    bias_here = lax.dynamic_slice_in_dim(dec_bias, lax.axis_index("latent") * share, share, 0)

    enc_scale = MODEL_WIDTH ** (-0.5)
    dec_scale = LATENTS ** (-0.5)
    dec_turned = dec_weight.T
    chunks = max(1, min(4, local // 512))
    step = local // chunks
    spans = [slice(c * step, (c + 1) * step) for c in range(chunks)]
    over_width = (((0,), (0,)), ((), ()))
    local_rebuilt = jnp.zeros((width, tokens), F32)
    latents, pres = [], []
    for span in spans:
        part = lax.dot_general(inputs, enc_weight[:, span], over_width, preferred_element_type=F32).astype(BF16)
        encoded = halves_scatter(part, "rows", n_rows, BF16)
        pre = enc_scale * encoded + enc_bias[span]
        pres.append(pre)
        mine = (jax.nn.softplus(sharpness * pre) / sharpness).astype(BF16)
        full = halves_gather(mine, "rows", n_rows)
        latents.append(full)
        local_rebuilt = local_rebuilt + lax.dot_general(
            dec_turned[:, span], full, (((1,), (1,)), ((), ())), preferred_element_type=F32
        )
    rebuilt_share = scatter_l(local_rebuilt, F32)
    grad_share = (
        2.0 * (dec_scale * rebuilt_share + bias_here[:, None] - inputs_here.astype(F32))
    ).astype(BF16)
    residual_grad = gather_l(grad_share)
    grads = []
    for c, span in enumerate(spans):
        part = lax.dot_general(residual_grad, dec_turned[:, span], over_width, preferred_element_type=F32).astype(BF16)
        back = halves_scatter(part, "rows", n_rows, BF16)
        mine = (jax.nn.sigmoid(sharpness * pres[c]) * (dec_scale * back + sparsity_cost)).astype(BF16)
        grads.append(halves_gather(mine, "rows", n_rows))
    dec_new = enc_new = None
    for c, span in enumerate(spans):
        dec_new, _ = update(weight_rate * dec_scale, residual_grad, latents[c], dec_turned, c * step, dec_new)
    sums = []
    for c, span in enumerate(spans):
        enc_new, total = update(weight_rate * enc_scale, inputs, grads[c], enc_weight, c * step, enc_new)
        sums.append(total[0])
    enc_bias = enc_bias - enc_bias_rate * jnp.concatenate(sums)
    dec_bias = dec_bias - dec_bias_rate * jnp.sum(residual_grad, axis=1, dtype=F32)
    return (enc_new, enc_bias, dec_new.T, dec_bias)


def solution(mesh):
    def step(*args):
        return body(mesh.shape["latent"], mesh.shape["rows"], *args)


    return jax.shard_map(
        step,
        mesh=mesh,
        in_specs=(
            P("groups", None, "latent"),
            P("rows", "latent"),
            P("rows", "latent"),
            P("latent", "rows"),
            P(("groups", "rows"), "latent"),
            P(("groups", "latent")),
            P(("groups", "latent"), "rows"),
            P(("groups", "rows")),
        ),
        out_specs=(
            P(("groups", "rows"), "latent"),
            P(("groups", "latent")),
            P(("groups", "latent"), "rows"),
            P(("groups", "rows")),
        ),
        check_vma=False,
    )
```

time: 365 us -> 225 us (0.62); the launches traced: 358 us -> 224 us
  matrix products: 92.1 us -> 26.3 us
  waiting for transfers between devices: 139 us -> 98.1 us
  Pallas kernels: 0 us -> 27.4 us
  other arithmetic: 38.1 us -> 11.7 us
  local copies, waits for them, and re-layouts: 23.9 us -> 4.19 us
  starting transfers between devices: 63.1 us -> 54.7 us
    dot_general x15 -> x13, matrix products: 89.9 us -> 24.1 us  [the longest x4 13.7 us: body(): lax.dot_general(inputs, enc_weight[:, span], over_width, preferred_elemen...]
    ppermute x6, waiting for transfers between devices: 49.1 us -> 12 us  [direct_scatter(): lax.ppermute(give, axis, [(i, (i + shift) % n) for i in range(n)])]
    pallas_call x0 -> x8, Pallas kernels: none -> 27.4 us  [update(): pl.pallas_call(functools.partial(update_kernel, rate, buf is not None), g...]
    reduce_sum x2 -> x1, other arithmetic: 23.9 us -> 0.14 us  [body(): jnp.sum(residual_grad, axis=1, dtype=F32)]
    dynamic_update_slice x8 -> x6, local copies, waits for them, and re-layouts: 18.1 us -> 0.06 us  [direct_gather(): out = lax.dynamic_update_slice_in_dim(out, part, at * size, 0)]
    ppermute x36, starting transfers between devices: 40.8 us -> 36.8 us  [swap(): return lax.ppermute(x, axis, [(i, i ^ bit) for i in range(n)])]
  transfers between devices with their start and end apart: 49 -> 49, of which waited for: 29 -> 31; matrix products, arithmetic and copies ran while one was open for 9% -> 8% of each run, Pallas kernels for 0% -> 8%
where the time goes in v2:
time: 225 us; the launch traced here: 224 us
  waiting for transfers between devices  98.1 us (44%)
  starting transfers between devices  54.7 us (24%)
  Pallas kernels  27.4 us (12%)
  matrix products  26.3 us (12%)
  other arithmetic  11.7 us (5%)
  local copies, waits for them, and re-layouts  4.19 us (2%)
    ppermute x36, waiting for transfers between devices, swap(): return lax.ppermute(x, axis, [(i, i ^ bit) for i in range(n)])  82.2 us
    ppermute x36, starting transfers between devices, swap(): return lax.ppermute(x, axis, [(i, i ^ bit) for i in range(n)])  36.8 us
    pallas_call x8, Pallas kernels, update(): pl.pallas_call(functools.partial(update_kernel, rate, buf is not None), g...  27.4 us
    dot_general x4, matrix products, body(): lax.dot_general(inputs, enc_weight[:, span], over_width, preferred_elemen...  13.7 us
    ppermute x6, waiting for transfers between devices, direct_scatter(): lax.ppermute(give, axis, [(i, (i + shift) % n) for i in range(n)])  12 us
    ppermute x6, starting transfers between devices, direct_gather(): got = lax.ppermute(x, axis, [(i, (i + shift) % n) for i in range(n)])  8.94 us
    ppermute x6, starting transfers between devices, direct_scatter(): lax.ppermute(give, axis, [(i, (i + shift) % n) for i in range(n)])  7.34 us
    dot_general x4, matrix products, body(): lax.dot_general(dec_turned[:, span], full, (((1,), (1,)), ((), ())), pref...  5.81 us
  transfers between devices with their start and end apart: 49, of which 31 were waited for; matrix products, arithmetic and copies ran while one was open for 8% of the time, Pallas kernels for 8%

profile of v2, /device:TPU:0, one launch (start us, length us, event | category | flops | bytes accessed | tf_op | source)
XLA Modules:
  0.0 224.3 jit_solution(16352516456279675767)
XLA Ops:
  4.7 6.7 %collective-permute-start.1 = (bf16[64,2304]{1,0:T(8,128)(2,1)S(1)}, bf16[64,2304]{1,0:T(8,128)(2,1)S(1)}, u32[]{:S(2)}, u32[]{:S(2)}) collective-permute-start(bf16[64,2304]{1,0:T(8,128)(2,1)S(1)} %fusion.33), channel_id=1, source_target_pairs={{0,1},{1,0},{2,3},{3,2},{4,5},{5,4},{6,7},{7,6},{8,9},{9,8},{10,11... | collective-permute-start | bytes 884744 | tf_op jit(solution)/shard_map/ppermute | solution.py:25
  12.7 8.6 %collective-permute-start.2 = (bf16[32,2304]{1,0:T(8,128)(2,1)S(1)}, bf16[32,2304]{1,0:T(8,128)(2,1)S(1)}, u32[]{:S(2)}, u32[]{:S(2)}) collective-permute-start(bf16[32,2304]{1,0:T(8,128)(2,1)S(1)} %dynamic-slice_convert_fusion.8), channel_id=1, source_target_pairs={{0,2},{1,3},{2,0},{3,1},{4,6},{5,7},{6,4},{7,5},{8,10},{9,11},{10,... | collective-permute-start | bytes 442376 | tf_op jit(solution)/shard_map/ppermute | solution.py:25
  21.3 4.1 %collective-permute-done.2 = bf16[32,2304]{1,0:T(8,128)(2,1)S(1)} collective-permute-done((bf16[32,2304]{1,0:T(8,128)(2,1)S(1)}, bf16[32,2304]{1,0:T(8,128)(2,1)S(1)}, u32[]{:S(2)}, u32[]{:S(2)}) %collective-permute-start.2) | collective-permute-done | bytes 147488 | tf_op jit(solution)/shard_map/ppermute | solution.py:25
  36.5 3.2 %collective-permute-done.6 = bf16[144,128]{1,0:T(8,128)(2,1)S(1)} collective-permute-done((bf16[144,128]{1,0:T(8,128)(2,1)S(1)}, bf16[144,128]{1,0:T(8,128)(2,1)S(1)}, u32[]{:S(2)}, u32[]{:S(2)}) %collective-permute-start.6) | collective-permute-done | bytes 36896 | tf_op jit(solution)/shard_map/ppermute | solution.py:61
  47.6 3.4 %convolution_convert_fusion.7 = bf16[128,4096]{1,0:T(8,128)(2,1)S(1)} fusion(bf16[576,128]{1,0:T(8,128)(2,1)S(1)} %constant_dynamic-update-slice_fusion.4.left_ref, bf16[576,16384]{1,0:T(8,128)(2,1)} %w_ref.7), kind=kOutput, calls=%fused_computation.7 | convolution fusion | flops 604504064 | bytes 5914624 | tf_op jit(solution)/shard_map/dot_general | solution.py:161
  51.0 3.3 %convolution_convert_fusion.4 = bf16[128,4096]{1,0:T(8,128)(2,1)S(1)} fusion(bf16[576,128]{1,0:T(8,128)(2,1)S(1)} %constant_dynamic-update-slice_fusion.4.left_ref, bf16[576,16384]{1,0:T(8,128)(2,1)} %w_ref.7), kind=kOutput, calls=%fused_computation.4 | convolution fusion | flops 604504064 | bytes 5914624 | tf_op jit(solution)/shard_map/dot_general | solution.py:161
  54.4 3.5 %convolution_convert_fusion.5 = bf16[128,4096]{1,0:T(8,128)(2,1)S(1)} fusion(bf16[576,128]{1,0:T(8,128)(2,1)S(1)} %constant_dynamic-update-slice_fusion.4.left_ref, bf16[576,16384]{1,0:T(8,128)(2,1)} %w_ref.7), kind=kOutput, calls=%fused_computation.5 | convolution fusion | flops 604504064 | bytes 5914624 | tf_op jit(solution)/shard_map/dot_general | solution.py:161
  57.9 3.5 %convolution_convert_fusion.6 = bf16[128,4096]{1,0:T(8,128)(2,1)S(1)} fusion(bf16[576,128]{1,0:T(8,128)(2,1)S(1)} %constant_dynamic-update-slice_fusion.4.left_ref, bf16[576,16384]{1,0:T(8,128)(2,1)} %w_ref.7), kind=kOutput, calls=%fused_computation.6 | convolution fusion | flops 604504064 | bytes 5914624 | tf_op jit(solution)/shard_map/dot_general | solution.py:161
  68.4 4.4 %collective-permute-done.12 = bf16[32,4096]{1,0:T(8,128)(2,1)S(1)} collective-permute-done((bf16[32,4096]{1,0:T(8,128)(2,1)S(1)}, bf16[32,4096]{1,0:T(8,128)(2,1)S(1)}, u32[]{:S(2)}, u32[]{:S(2)}) %collective-permute-start.12) | collective-permute-done | bytes 262176 | tf_op jit(solution)/shard_map/ppermute | solution.py:25
  74.3 4.2 %collective-permute-done.22 = bf16[32,4096]{1,0:T(8,128)(2,1)S(1)} collective-permute-done((bf16[32,4096]{1,0:T(8,128)(2,1)S(1)}, bf16[32,4096]{1,0:T(8,128)(2,1)S(1)}, u32[]{:S(2)}, u32[]{:S(2)}) %collective-permute-start.22) | collective-permute-done | bytes 262176 | tf_op jit(solution)/shard_map/ppermute | solution.py:25
  79.9 4.2 %collective-permute-done.18 = bf16[32,4096]{1,0:T(8,128)(2,1)S(1)} collective-permute-done((bf16[32,4096]{1,0:T(8,128)(2,1)S(1)}, bf16[32,4096]{1,0:T(8,128)(2,1)S(1)}, u32[]{:S(2)}, u32[]{:S(2)}) %collective-permute-start.18) | collective-permute-done | bytes 262176 | tf_op jit(solution)/shard_map/ppermute | solution.py:25
  85.5 4.2 %collective-permute-done.14 = bf16[32,4096]{1,0:T(8,128)(2,1)S(1)} collective-permute-done((bf16[32,4096]{1,0:T(8,128)(2,1)S(1)}, bf16[32,4096]{1,0:T(8,128)(2,1)S(1)}, u32[]{:S(2)}, u32[]{:S(2)}) %collective-permute-start.14) | collective-permute-done | bytes 262176 | tf_op jit(solution)/shard_map/ppermute | solution.py:25
  91.1 4.2 %collective-permute-done.25 = bf16[32,4096]{1,0:T(8,128)(2,1)S(1)} collective-permute-done((bf16[32,4096]{1,0:T(8,128)(2,1)S(1)}, bf16[32,4096]{1,0:T(8,128)(2,1)S(1)}, u32[]{:S(2)}, u32[]{:S(2)}) %collective-permute-start.25) | collective-permute-done | bytes 262176 | tf_op jit(solution)/shard_map/ppermute | solution.py:25
  95.5 5.4 %collective-permute-done.23 = bf16[32,4096]{1,0:T(8,128)(2,1)S(1)} collective-permute-done((bf16[32,4096]{1,0:T(8,128)(2,1)S(1)}, bf16[32,4096]{1,0:T(8,128)(2,1)S(1)}, u32[]{:S(2)}, u32[]{:S(2)}) %collective-permute-start.23) | collective-permute-done | bytes 262176 | tf_op jit(solution)/shard_map/ppermute | solution.py:25
  101.1 5.4 %collective-permute-done.19 = bf16[32,4096]{1,0:T(8,128)(2,1)S(1)} collective-permute-done((bf16[32,4096]{1,0:T(8,128)(2,1)S(1)}, bf16[32,4096]{1,0:T(8,128)(2,1)S(1)}, u32[]{:S(2)}, u32[]{:S(2)}) %collective-permute-start.19) | collective-permute-done | bytes 262176 | tf_op jit(solution)/shard_map/ppermute | solution.py:25
  106.7 4.6 %collective-permute-done.15 = bf16[32,4096]{1,0:T(8,128)(2,1)S(1)} collective-permute-done((bf16[32,4096]{1,0:T(8,128)(2,1)S(1)}, bf16[32,4096]{1,0:T(8,128)(2,1)S(1)}, u32[]{:S(2)}, u32[]{:S(2)}) %collective-permute-start.15) | collective-permute-done | bytes 262176 | tf_op jit(solution)/shard_map/ppermute | solution.py:25
  118.5 3.5 %collective-permute-start.29 = (f32[144,128]{1,0:T(8,128)S(1)}, f32[144,128]{1,0:T(8,128)S(1)}, u32[]{:S(2)}, u32[]{:S(2)}) collective-permute-start(f32[144,128]{1,0:T(8,128)S(1)} %get-tuple-element.65), channel_id=1, source_target_pairs={{0,12},{4,0},{8,4},{12,8},{1,13},{5,1},{9,5},{13,9},{2,14},{6,2},{... | collective-permute-start | bytes 221192 | tf_op jit(solution)/shard_map/ppermute | solution.py:61
  124.7 4.9 %collective-permute-done.28 = f32[144,128]{1,0:T(8,128)S(1)} collective-permute-done((f32[144,128]{1,0:T(8,128)S(1)}, f32[144,128]{1,0:T(8,128)S(1)}, u32[]{:S(2)}, u32[]{:S(2)}) %collective-permute-start.28) | collective-permute-done | bytes 73760 | tf_op jit(solution)/shard_map/ppermute | solution.py:61
  144.1 3.4 %shard_map.115 = (bf16[576,16384]{1,0:T(8,128)(2,1)}, f32[8,4096]{1,0:T(8,128)}) custom-call(bf16[576,128]{1,0:T(8,128)(2,1)S(1)} %constant_dynamic-update-slice_fusion.left_ref, bf16[128,4096]{1,0:T(8,128)(2,1)S(1)} %pad_maximum_fusion.right_ref, bf16[576,16384]{1,0:T(8,128)(2,1)S(1)} %bitcast.68), custom_call_target="tpu_custom_call" | custom-call | flops 603979776 | bytes 9437184 | tf_op jit(solution)/shard_map/pallas_call | solution.py:104
  147.5 3.4 %shard_map.116 = (bf16[576,16384]{1,0:T(8,128)(2,1)}, f32[8,4096]{1,0:T(8,128)}) custom-call(bf16[576,128]{1,0:T(8,128)(2,1)S(1)} %constant_dynamic-update-slice_fusion.left_ref, bf16[128,4096]{1,0:T(8,128)(2,1)S(1)} %pad_maximum_fusion.1.right_ref, bf16[576,16384]{1,0:T(8,128)(2,1)S(1)} %bitcast.69, ...), custom_call_target="tpu_custom_call", output_to_operand_aliasing={{0}: (3, {})} | custom-call | flops 603979776 | bytes 9437184 | tf_op jit(solution)/shard_map/pallas_call | solution.py:104
  150.9 3.4 %shard_map.117 = (bf16[576,16384]{1,0:T(8,128)(2,1)}, f32[8,4096]{1,0:T(8,128)}) custom-call(bf16[576,128]{1,0:T(8,128)(2,1)S(1)} %constant_dynamic-update-slice_fusion.left_ref, bf16[128,4096]{1,0:T(8,128)(2,1)S(1)} %pad_maximum_fusion.2.right_ref, bf16[576,16384]{1,0:T(8,128)(2,1)S(1)} %bitcast.70, ...), custom_call_target="tpu_custom_call", output_to_operand_aliasing={{0}: (3, {})} | custom-call | flops 603979776 | bytes 9437184 | tf_op jit(solution)/shard_map/pallas_call | solution.py:104
  154.3 3.7 %shard_map.118 = (bf16[576,16384]{1,0:T(8,128)(2,1)}, f32[8,4096]{1,0:T(8,128)}) custom-call(bf16[576,128]{1,0:T(8,128)(2,1)S(1)} %constant_dynamic-update-slice_fusion.left_ref, bf16[128,4096]{1,0:T(8,128)(2,1)S(1)} %pad_maximum_fusion.3.right_ref, bf16[576,16384]{1,0:T(8,128)(2,1)S(1)} %bitcast.71, ...), custom_call_target="tpu_custom_call", output_to_operand_aliasing={{0}: (3, {})} | custom-call | flops 603979776 | bytes 9437184 | tf_op jit(solution)/shard_map/pallas_call | solution.py:104
  169.4 4.4 %collective-permute-done.34 = bf16[32,4096]{1,0:T(8,128)(2,1)S(1)} collective-permute-done((bf16[32,4096]{1,0:T(8,128)(2,1)S(1)}, bf16[32,4096]{1,0:T(8,128)(2,1)S(1)}, u32[]{:S(2)}, u32[]{:S(2)}) %collective-permute-start.34) | collective-permute-done | bytes 262176 | tf_op jit(solution)/shard_map/ppermute | solution.py:25
  175.0 4.4 %collective-permute-done.46 = bf16[32,4096]{1,0:T(8,128)(2,1)S(1)} collective-permute-done((bf16[32,4096]{1,0:T(8,128)(2,1)S(1)}, bf16[32,4096]{1,0:T(8,128)(2,1)S(1)}, u32[]{:S(2)}, u32[]{:S(2)}) %collective-permute-start.46) | collective-permute-done | bytes 262176 | tf_op jit(solution)/shard_map/ppermute | solution.py:25
  180.6 4.4 %collective-permute-done.42 = bf16[32,4096]{1,0:T(8,128)(2,1)S(1)} collective-permute-done((bf16[32,4096]{1,0:T(8,128)(2,1)S(1)}, bf16[32,4096]{1,0:T(8,128)(2,1)S(1)}, u32[]{:S(2)}, u32[]{:S(2)}) %collective-permute-start.42) | collective-permute-done | bytes 262176 | tf_op jit(solution)/shard_map/ppermute | solution.py:25
  186.2 4.4 %collective-permute-done.39 = bf16[32,4096]{1,0:T(8,128)(2,1)S(1)} collective-permute-done((bf16[32,4096]{1,0:T(8,128)(2,1)S(1)}, bf16[32,4096]{1,0:T(8,128)(2,1)S(1)}, u32[]{:S(2)}, u32[]{:S(2)}) %collective-permute-start.39) | collective-permute-done | bytes 262176 | tf_op jit(solution)/shard_map/ppermute | solution.py:25
  190.9 11.1 %collective-permute-done.47 = bf16[32,4096]{1,0:T(8,128)(2,1)S(1)} collective-permute-done((bf16[32,4096]{1,0:T(8,128)(2,1)S(1)}, bf16[32,4096]{1,0:T(8,128)(2,1)S(1)}, u32[]{:S(2)}, u32[]{:S(2)}) %collective-permute-start.47) | collective-permute-done | bytes 262176 | tf_op jit(solution)/shard_map/ppermute | solution.py:25
  202.1 4.5 %collective-permute-done.43 = bf16[32,4096]{1,0:T(8,128)(2,1)S(1)} collective-permute-done((bf16[32,4096]{1,0:T(8,128)(2,1)S(1)}, bf16[32,4096]{1,0:T(8,128)(2,1)S(1)}, u32[]{:S(2)}, u32[]{:S(2)}) %collective-permute-start.43) | collective-permute-done | bytes 262176 | tf_op jit(solution)/shard_map/ppermute | solution.py:25
  209.2 3.4 %shard_map.111 = (bf16[576,16384]{1,0:T(8,128)(2,1)}, f32[8,4096]{1,0:T(8,128)S(1)}) custom-call(bf16[576,128]{1,0:T(8,128)(2,1)S(1)} %constant_dynamic-update-slice_fusion.4.left_ref, bf16[128,4096]{1,0:T(8,128)(2,1)S(1)} %pad_maximum_fusion.7.right_ref, bf16[576,16384]{1,0:T(8,128)(2,1)S(1)} %bitcast.73), custom_call_target="tpu_custom_call" | custom-call | flops 603979776 | bytes 9437184 | tf_op jit(solution)/shard_map/pallas_call | solution.py:104
  213.3 3.4 %shard_map.112 = (bf16[576,16384]{1,0:T(8,128)(2,1)}, f32[8,4096]{1,0:T(8,128)S(1)}) custom-call(bf16[576,128]{1,0:T(8,128)(2,1)S(1)} %constant_dynamic-update-slice_fusion.4.left_ref, bf16[128,4096]{1,0:T(8,128)(2,1)S(1)} %pad_maximum_fusion.6.right_ref, bf16[576,16384]{1,0:T(8,128)(2,1)S(1)} %bitcast.73, ...), custom_call_target="tpu_custom_call", output_to_operand_aliasing={{0}: (3, {})} | custom-call | flops 603979776 | bytes 9437184 | tf_op jit(solution)/shard_map/pallas_call | solution.py:104
  216.8 3.4 %shard_map.113 = (bf16[576,16384]{1,0:T(8,128)(2,1)}, f32[8,4096]{1,0:T(8,128)S(1)}) custom-call(bf16[576,128]{1,0:T(8,128)(2,1)S(1)} %constant_dynamic-update-slice_fusion.4.left_ref, bf16[128,4096]{1,0:T(8,128)(2,1)S(1)} %pad_maximum_fusion.5.right_ref, bf16[576,16384]{1,0:T(8,128)(2,1)S(1)} %bitcast.73, ...), custom_call_target="tpu_custom_call", output_to_operand_aliasing={{0}: (3, {})} | custom-call | flops 603979776 | bytes 9437184 | tf_op jit(solution)/shard_map/pallas_call | solution.py:104
  220.1 3.4 %shard_map.114 = (bf16[576,16384]{1,0:T(8,128)(2,1)}, f32[8,4096]{1,0:T(8,128)S(1)}) custom-call(bf16[576,128]{1,0:T(8,128)(2,1)S(1)} %constant_dynamic-update-slice_fusion.4.left_ref, bf16[128,4096]{1,0:T(8,128)(2,1)S(1)} %pad_maximum_fusion.4.right_ref, bf16[576,16384]{1,0:T(8,128)(2,1)S(1)} %bitcast.73, ...), custom_call_target="tpu_custom_call", output_to_operand_aliasing={{0}: (3, {})} | custom-call | flops 603979776 | bytes 9437184 | tf_op jit(solution)/shard_map/pallas_call | solution.py:104
  (254 shorter events, 80.3 us)
Async XLA Ops:
  4.7 7.9 %collective-permute-start.1 = (bf16[64,2304]{1,0:T(8,128)(2,1)S(1)}, bf16[64,2304]{1,0:T(8,128)(2,1)S(1)}, u32[]{:S(2)}, u32[]{:S(2)}) collective-permute-start(bf16[64,2304]{1,0:T(8,128)(2,1)S(1)} %fusion.33), channel_id=1, source_target_pairs={{0,1},{1,0},{2,3},{3,2},{4,5},{5,4},{6,7},{7,6},{8,9},{9,8},{10,11... | collective-permute-start | bytes 884744 | tf_op jit(solution)/shard_map/ppermute | solution.py:25
  12.7 12.8 %collective-permute-start.2 = (bf16[32,2304]{1,0:T(8,128)(2,1)S(1)}, bf16[32,2304]{1,0:T(8,128)(2,1)S(1)}, u32[]{:S(2)}, u32[]{:S(2)}) collective-permute-start(bf16[32,2304]{1,0:T(8,128)(2,1)S(1)} %dynamic-slice_convert_fusion.8), channel_id=1, source_target_pairs={{0,2},{1,3},{2,0},{3,1},{4,6},{5,7},{6,4},{7,5},{8,10},{9,11},{10,... | collective-permute-start | bytes 442376 | tf_op jit(solution)/shard_map/ppermute | solution.py:25
  40.5 5.9 %collective-permute-start.8 = (bf16[144,128]{1,0:T(8,128)(2,1)S(1)}, bf16[144,128]{1,0:T(8,128)(2,1)S(1)}, u32[]{:S(2)}, u32[]{:S(2)}) collective-permute-start(bf16[144,128]{1,0:T(8,128)(2,1)S(1)} %get-tuple-element.31), channel_id=1, source_target_pairs={{0,4},{4,8},{8,12},{12,0},{1,5},{5,9},{9,13},{13,1},{2,6},{6,10},{... | collective-permute-start | bytes 110600 | tf_op jit(solution)/shard_map/ppermute | solution.py:73
  63.6 9.2 %collective-permute-start.12 = (bf16[32,4096]{1,0:T(8,128)(2,1)S(1)}, bf16[32,4096]{1,0:T(8,128)(2,1)S(1)}, u32[]{:S(2)}, u32[]{:S(2)}) collective-permute-start(bf16[32,4096]{1,0:T(8,128)(2,1)S(1)} %dynamic-slice_convert_fusion.7), channel_id=1, source_target_pairs={{0,2},{1,3},{2,0},{3,1},{4,6},{5,7},{6,4},{7,5},{8,10},{9,11},{10,... | collective-permute-start | bytes 786440 | tf_op jit(solution)/shard_map/ppermute | solution.py:25
  64.8 13.6 %collective-permute-start.22 = (bf16[32,4096]{1,0:T(8,128)(2,1)S(1)}, bf16[32,4096]{1,0:T(8,128)(2,1)S(1)}, u32[]{:S(2)}, u32[]{:S(2)}) collective-permute-start(bf16[32,4096]{1,0:T(8,128)(2,1)S(1)} %dynamic-slice_convert_fusion.4), channel_id=1, source_target_pairs={{0,2},{1,3},{2,0},{3,1},{4,6},{5,7},{6,4},{7,5},{8,10},{9,11},{10,... | collective-permute-start | bytes 786440 | tf_op jit(solution)/shard_map/ppermute | solution.py:25
  66.1 18.0 %collective-permute-start.18 = (bf16[32,4096]{1,0:T(8,128)(2,1)S(1)}, bf16[32,4096]{1,0:T(8,128)(2,1)S(1)}, u32[]{:S(2)}, u32[]{:S(2)}) collective-permute-start(bf16[32,4096]{1,0:T(8,128)(2,1)S(1)} %dynamic-slice_convert_fusion.5), channel_id=1, source_target_pairs={{0,2},{1,3},{2,0},{3,1},{4,6},{5,7},{6,4},{7,5},{8,10},{9,11},{10,... | collective-permute-start | bytes 786440 | tf_op jit(solution)/shard_map/ppermute | solution.py:25
  67.3 22.4 %collective-permute-start.14 = (bf16[32,4096]{1,0:T(8,128)(2,1)S(1)}, bf16[32,4096]{1,0:T(8,128)(2,1)S(1)}, u32[]{:S(2)}, u32[]{:S(2)}) collective-permute-start(bf16[32,4096]{1,0:T(8,128)(2,1)S(1)} %dynamic-slice_convert_fusion.6), channel_id=1, source_target_pairs={{0,2},{1,3},{2,0},{3,1},{4,6},{5,7},{6,4},{7,5},{8,10},{9,11},{10,... | collective-permute-start | bytes 786440 | tf_op jit(solution)/shard_map/ppermute | solution.py:25
  73.3 22.1 %collective-permute-start.25 = (bf16[32,4096]{1,0:T(8,128)(2,1)S(1)}, bf16[32,4096]{1,0:T(8,128)(2,1)S(1)}, u32[]{:S(2)}, u32[]{:S(2)}) collective-permute-start(bf16[32,4096]{1,0:T(8,128)(2,1)S(1)} %fusion.32), channel_id=1, source_target_pairs={{0,2},{1,3},{2,0},{3,1},{4,6},{5,7},{6,4},{7,5},{8,10},{9,11},{10,... | collective-permute-start | bytes 786440 | tf_op jit(solution)/shard_map/ppermute | solution.py:25
  78.9 22.1 %collective-permute-start.23 = (bf16[32,4096]{1,0:T(8,128)(2,1)S(1)}, bf16[32,4096]{1,0:T(8,128)(2,1)S(1)}, u32[]{:S(2)}, u32[]{:S(2)}) collective-permute-start(bf16[32,4096]{1,0:T(8,128)(2,1)S(1)} %fusion.30), channel_id=1, source_target_pairs={{0,2},{1,3},{2,0},{3,1},{4,6},{5,7},{6,4},{7,5},{8,10},{9,11},{10,... | collective-permute-start | bytes 786440 | tf_op jit(solution)/shard_map/ppermute | solution.py:25
  84.5 22.1 %collective-permute-start.19 = (bf16[32,4096]{1,0:T(8,128)(2,1)S(1)}, bf16[32,4096]{1,0:T(8,128)(2,1)S(1)}, u32[]{:S(2)}, u32[]{:S(2)}) collective-permute-start(bf16[32,4096]{1,0:T(8,128)(2,1)S(1)} %fusion.28), channel_id=1, source_target_pairs={{0,2},{1,3},{2,0},{3,1},{4,6},{5,7},{6,4},{7,5},{8,10},{9,11},{10,... | collective-permute-start | bytes 786440 | tf_op jit(solution)/shard_map/ppermute | solution.py:25
  90.1 21.2 %collective-permute-start.15 = (bf16[32,4096]{1,0:T(8,128)(2,1)S(1)}, bf16[32,4096]{1,0:T(8,128)(2,1)S(1)}, u32[]{:S(2)}, u32[]{:S(2)}) collective-permute-start(bf16[32,4096]{1,0:T(8,128)(2,1)S(1)} %fusion.26), channel_id=1, source_target_pairs={{0,2},{1,3},{2,0},{3,1},{4,6},{5,7},{6,4},{7,5},{8,10},{9,11},{10,... | collective-permute-start | bytes 786440 | tf_op jit(solution)/shard_map/ppermute | solution.py:25
  95.4 16.1 %collective-permute-start.26 = (bf16[64,4096]{1,0:T(8,128)(2,1)S(1)}, bf16[64,4096]{1,0:T(8,128)(2,1)S(1)}, u32[]{:S(2)}, u32[]{:S(2)}) collective-permute-start(bf16[64,4096]{1,0:T(8,128)(2,1)S(1)} %pad_maximum_fusion.11), channel_id=1, source_target_pairs={{0,1},{1,0},{2,3},{3,2},{4,5},{5,4},{6,7},{7,6},{8,9},{9,8},{10,11... | collective-permute-start | bytes 1572872 | tf_op jit(solution)/shard_map/ppermute | solution.py:25
  101.0 12.2 %collective-permute-start.24 = (bf16[64,4096]{1,0:T(8,128)(2,1)S(1)}, bf16[64,4096]{1,0:T(8,128)(2,1)S(1)}, u32[]{:S(2)}, u32[]{:S(2)}) collective-permute-start(bf16[64,4096]{1,0:T(8,128)(2,1)S(1)} %pad_maximum_fusion.10), channel_id=1, source_target_pairs={{0,1},{1,0},{2,3},{3,2},{4,5},{5,4},{6,7},{7,6},{8,9},{9,8},{10,11... | collective-permute-start | bytes 1572872 | tf_op jit(solution)/shard_map/ppermute | solution.py:25
  106.7 8.2 %collective-permute-start.20 = (bf16[64,4096]{1,0:T(8,128)(2,1)S(1)}, bf16[64,4096]{1,0:T(8,128)(2,1)S(1)}, u32[]{:S(2)}, u32[]{:S(2)}) collective-permute-start(bf16[64,4096]{1,0:T(8,128)(2,1)S(1)} %pad_maximum_fusion.9), channel_id=1, source_target_pairs={{0,1},{1,0},{2,3},{3,2},{4,5},{5,4},{6,7},{7,6},{8,9},{9,8},{10,11... | collective-permute-start | bytes 1572872 | tf_op jit(solution)/shard_map/ppermute | solution.py:25
  118.5 6.2 %collective-permute-start.29 = (f32[144,128]{1,0:T(8,128)S(1)}, f32[144,128]{1,0:T(8,128)S(1)}, u32[]{:S(2)}, u32[]{:S(2)}) collective-permute-start(f32[144,128]{1,0:T(8,128)S(1)} %get-tuple-element.65), channel_id=1, source_target_pairs={{0,12},{4,0},{8,4},{12,8},{1,13},{5,1},{9,5},{13,9},{2,14},{6,2},{... | collective-permute-start | bytes 221192 | tf_op jit(solution)/shard_map/ppermute | solution.py:61
  122.0 7.6 %collective-permute-start.28 = (f32[144,128]{1,0:T(8,128)S(1)}, f32[144,128]{1,0:T(8,128)S(1)}, u32[]{:S(2)}, u32[]{:S(2)}) collective-permute-start(f32[144,128]{1,0:T(8,128)S(1)} %get-tuple-element.66), channel_id=1, source_target_pairs={{0,8},{4,12},{8,0},{12,4},{1,9},{5,13},{9,1},{13,5},{2,10},{6,14},... | collective-permute-start | bytes 221192 | tf_op jit(solution)/shard_map/ppermute | solution.py:61
  122.0 7.6 %collective-permute-start.27 = (f32[144,128]{1,0:T(8,128)S(1)}, f32[144,128]{1,0:T(8,128)S(1)}, u32[]{:S(2)}, u32[]{:S(2)}) collective-permute-start(f32[144,128]{1,0:T(8,128)S(1)} %get-tuple-element.64), channel_id=1, source_target_pairs={{0,4},{4,8},{8,12},{12,0},{1,5},{5,9},{9,13},{13,1},{2,6},{6,10},{... | collective-permute-start | bytes 221192 | tf_op jit(solution)/shard_map/ppermute | solution.py:61
  129.8 6.1 %collective-permute-start.30 = (bf16[144,128]{1,0:T(8,128)(2,1)S(1)}, bf16[144,128]{1,0:T(8,128)(2,1)S(1)}, u32[]{:S(2)}, u32[]{:S(2)}) collective-permute-start(bf16[144,128]{1,0:T(8,128)(2,1)S(1)} %get-tuple-element.29), channel_id=1, source_target_pairs={{0,4},{4,8},{8,12},{12,0},{1,5},{5,9},{9,13},{13,1},{2,6},{6,10},{... | collective-permute-start | bytes 110600 | tf_op jit(solution)/shard_map/ppermute | solution.py:73
  130.2 5.8 %collective-permute-start.31 = (bf16[144,128]{1,0:T(8,128)(2,1)S(1)}, bf16[144,128]{1,0:T(8,128)(2,1)S(1)}, u32[]{:S(2)}, u32[]{:S(2)}) collective-permute-start(bf16[144,128]{1,0:T(8,128)(2,1)S(1)} %get-tuple-element.29), channel_id=1, source_target_pairs={{0,8},{4,12},{8,0},{12,4},{1,9},{5,13},{9,1},{13,5},{2,10},{6,14},... | collective-permute-start | bytes 110600 | tf_op jit(solution)/shard_map/ppermute | solution.py:73
  140.5 18.2 %collective-permute-start.37 = (bf16[64,4096]{1,0:T(8,128)(2,1)S(1)}, bf16[64,4096]{1,0:T(8,128)(2,1)S(1)}, u32[]{:S(2)}, u32[]{:S(2)}) collective-permute-start(bf16[64,4096]{1,0:T(8,128)(2,1)S(1)} %constant_dynamic-slice_fusion.2), channel_id=1, source_target_pairs={{0,1},{1,0},{2,3},{3,2},{4,5},{5,4},{6,7},{7,6},{8,9},{9,8},{10,11... | collective-permute-start | bytes 1572872 | tf_op jit(solution)/shard_map/ppermute | solution.py:25
  141.5 18.4 %collective-permute-start.33 = (bf16[64,4096]{1,0:T(8,128)(2,1)}, bf16[64,4096]{1,0:T(8,128)(2,1)}, u32[]{:S(2)}, u32[]{:S(2)}) collective-permute-start(bf16[64,4096]{1,0:T(8,128)(2,1)} %constant_dynamic-slice_fusion.3), channel_id=1, source_target_pairs={{0,1},{1,0},{2,3},{3,2},{4,5},{5,4},{6,7},{7,6},{8,9},{9,8},{10,11... | collective-permute-start | bytes 1572872 | tf_op jit(solution)/shard_map/ppermute | solution.py:25
  142.8 19.7 %collective-permute-start.45 = (bf16[64,4096]{1,0:T(8,128)(2,1)}, bf16[64,4096]{1,0:T(8,128)(2,1)}, u32[]{:S(2)}, u32[]{:S(2)}) collective-permute-start(bf16[64,4096]{1,0:T(8,128)(2,1)} %constant_dynamic-slice_fusion), channel_id=1, source_target_pairs={{0,1},{1,0},{2,3},{3,2},{4,5},{5,4},{6,7},{7,6},{8,9},{9,8},{10,11... | collective-permute-start | bytes 1572872 | tf_op jit(solution)/shard_map/ppermute | solution.py:25
  143.6 21.2 %collective-permute-start.41 = (bf16[64,4096]{1,0:T(8,128)(2,1)}, bf16[64,4096]{1,0:T(8,128)(2,1)}, u32[]{:S(2)}, u32[]{:S(2)}) collective-permute-start(bf16[64,4096]{1,0:T(8,128)(2,1)} %constant_dynamic-slice_fusion.1), channel_id=1, source_target_pairs={{0,1},{1,0},{2,3},{3,2},{4,5},{5,4},{6,7},{7,6},{8,9},{9,8},{10,11... | collective-permute-start | bytes 1572872 | tf_op jit(solution)/shard_map/ppermute | solution.py:25
  159.0 9.2 %collective-permute-start.38 = (bf16[32,4096]{1,0:T(8,128)(2,1)S(1)}, bf16[32,4096]{1,0:T(8,128)(2,1)S(1)}, u32[]{:S(2)}, u32[]{:S(2)}) collective-permute-start(bf16[32,4096]{1,0:T(8,128)(2,1)S(1)} %dynamic-slice_convert_fusion.2), channel_id=1, source_target_pairs={{0,2},{1,3},{2,0},{3,1},{4,6},{5,7},{6,4},{7,5},{8,10},{9,11},{10,... | collective-permute-start | bytes 786440 | tf_op jit(solution)/shard_map/ppermute | solution.py:25
  161.4 12.4 %collective-permute-start.34 = (bf16[32,4096]{1,0:T(8,128)(2,1)S(1)}, bf16[32,4096]{1,0:T(8,128)(2,1)S(1)}, u32[]{:S(2)}, u32[]{:S(2)}) collective-permute-start(bf16[32,4096]{1,0:T(8,128)(2,1)S(1)} %dynamic-slice_convert_fusion.3), channel_id=1, source_target_pairs={{0,2},{1,3},{2,0},{3,1},{4,6},{5,7},{6,4},{7,5},{8,10},{9,11},{10,... | collective-permute-start | bytes 786440 | tf_op jit(solution)/shard_map/ppermute | solution.py:25
  163.7 15.7 %collective-permute-start.46 = (bf16[32,4096]{1,0:T(8,128)(2,1)S(1)}, bf16[32,4096]{1,0:T(8,128)(2,1)S(1)}, u32[]{:S(2)}, u32[]{:S(2)}) collective-permute-start(bf16[32,4096]{1,0:T(8,128)(2,1)S(1)} %dynamic-slice_convert_fusion), channel_id=1, source_target_pairs={{0,2},{1,3},{2,0},{3,1},{4,6},{5,7},{6,4},{7,5},{8,10},{9,11},{10,... | collective-permute-start | bytes 786440 | tf_op jit(solution)/shard_map/ppermute | solution.py:25
  166.0 19.1 %collective-permute-start.42 = (bf16[32,4096]{1,0:T(8,128)(2,1)S(1)}, bf16[32,4096]{1,0:T(8,128)(2,1)S(1)}, u32[]{:S(2)}, u32[]{:S(2)}) collective-permute-start(bf16[32,4096]{1,0:T(8,128)(2,1)S(1)} %dynamic-slice_convert_fusion.1), channel_id=1, source_target_pairs={{0,2},{1,3},{2,0},{3,1},{4,6},{5,7},{6,4},{7,5},{8,10},{9,11},{10,... | collective-permute-start | bytes 786440 | tf_op jit(solution)/shard_map/ppermute | solution.py:25
  168.5 22.2 %collective-permute-start.39 = (bf16[32,4096]{1,0:T(8,128)(2,1)S(1)}, bf16[32,4096]{1,0:T(8,128)(2,1)S(1)}, u32[]{:S(2)}, u32[]{:S(2)}) collective-permute-start(bf16[32,4096]{1,0:T(8,128)(2,1)S(1)} %multiply_convert_fusion.2), channel_id=1, source_target_pairs={{0,2},{1,3},{2,0},{3,1},{4,6},{5,7},{6,4},{7,5},{8,10},{9,11},{10,... | collective-permute-start | bytes 786440 | tf_op jit(solution)/shard_map/ppermute | solution.py:25
  174.1 32.7 %collective-permute-start.35 = (bf16[32,4096]{1,0:T(8,128)(2,1)S(1)}, bf16[32,4096]{1,0:T(8,128)(2,1)S(1)}, u32[]{:S(2)}, u32[]{:S(2)}) collective-permute-start(bf16[32,4096]{1,0:T(8,128)(2,1)S(1)} %multiply_convert_fusion.3), channel_id=1, source_target_pairs={{0,2},{1,3},{2,0},{3,1},{4,6},{5,7},{6,4},{7,5},{8,10},{9,11},{10,... | collective-permute-start | bytes 786440 | tf_op jit(solution)/shard_map/ppermute | solution.py:25
  179.7 22.2 %collective-permute-start.47 = (bf16[32,4096]{1,0:T(8,128)(2,1)S(1)}, bf16[32,4096]{1,0:T(8,128)(2,1)S(1)}, u32[]{:S(2)}, u32[]{:S(2)}) collective-permute-start(bf16[32,4096]{1,0:T(8,128)(2,1)S(1)} %multiply_convert_fusion), channel_id=1, source_target_pairs={{0,2},{1,3},{2,0},{3,1},{4,6},{5,7},{6,4},{7,5},{8,10},{9,11},{10,... | collective-permute-start | bytes 786440 | tf_op jit(solution)/shard_map/ppermute | solution.py:25
  185.3 21.3 %collective-permute-start.43 = (bf16[32,4096]{1,0:T(8,128)(2,1)S(1)}, bf16[32,4096]{1,0:T(8,128)(2,1)S(1)}, u32[]{:S(2)}, u32[]{:S(2)}) collective-permute-start(bf16[32,4096]{1,0:T(8,128)(2,1)S(1)} %multiply_convert_fusion.1), channel_id=1, source_target_pairs={{0,2},{1,3},{2,0},{3,1},{4,6},{5,7},{6,4},{7,5},{8,10},{9,11},{10,... | collective-permute-start | bytes 786440 | tf_op jit(solution)/shard_map/ppermute | solution.py:25
  190.8 21.9 %collective-permute-start.40 = (bf16[64,4096]{1,0:T(8,128)(2,1)S(1)}, bf16[64,4096]{1,0:T(8,128)(2,1)S(1)}, u32[]{:S(2)}, u32[]{:S(2)}) collective-permute-start(bf16[64,4096]{1,0:T(8,128)(2,1)S(1)} %pad_maximum_fusion.13), channel_id=1, source_target_pairs={{0,1},{1,0},{2,3},{3,2},{4,5},{5,4},{6,7},{7,6},{8,9},{9,8},{10,11... | collective-permute-start | bytes 1572872 | tf_op jit(solution)/shard_map/ppermute | solution.py:25
  (53 other events, 999.4 us)

commit v3 on v2

--- a/solution.py
+++ b/solution.py
@@ -86,7 +86,7 @@
     sums_ref[...] = jnp.dot(ones, right, preferred_element_type=F32)
 
 
-def update(rate, left, right, weight, first, buf):
+def update(rate, left, right, weight, first, buf, grant):
     depth, tokens = left.shape
     columns = right.shape[1]
     tile = min(2048, columns)
@@ -111,7 +111,7 @@
         in_specs=in_specs,
         out_specs=(block, pl.BlockSpec((8, tile), lambda i: (0, i))),
         input_output_aliases={} if buf is None else {3: 0},
-        compiler_params=pltpu.CompilerParams(vmem_limit_bytes=24 * 1024 * 1024),
+        compiler_params=pltpu.CompilerParams(vmem_limit_bytes=grant),
         cost_estimate=pl.CostEstimate(
             flops=2 * depth * tokens * columns, bytes_accessed=4 * depth * columns, transcendentals=0
         ),
@@ -181,10 +181,10 @@
         grads.append(halves_gather(mine, "rows", n_rows))
     dec_new = enc_new = None
     for c, span in enumerate(spans):
-        dec_new, _ = update(weight_rate * dec_scale, residual_grad, latents[c], dec_turned, c * step, dec_new)
+        dec_new, _ = update(weight_rate * dec_scale, residual_grad, latents[c], dec_turned, c * step, dec_new, 24 << 20)
     sums = []
     for c, span in enumerate(spans):
-        enc_new, total = update(weight_rate * enc_scale, inputs, grads[c], enc_weight, c * step, enc_new)
+        enc_new, total = update(weight_rate * enc_scale, inputs, grads[c], enc_weight, c * step, enc_new, 52 << 20)
         sums.append(total[0])
     enc_bias = enc_bias - enc_bias_rate * jnp.concatenate(sums)
     dec_bias = dec_bias - dec_bias_rate * jnp.sum(residual_grad, axis=1, dtype=F32)

time: 225 us -> 227 us (level)
  Pallas kernels: 27.4 us -> 32.4 us
  waiting for transfers between devices: 98.1 us -> 102 us
  other arithmetic: 11.7 us -> 8.26 us
  local copies, waits for them, and re-layouts: 4.19 us -> 1 us
    pallas_call x8, Pallas kernels: 27.4 us -> 32.4 us  [update(): pl.pallas_call(functools.partial(update_kernel, rate, buf is not None), g...]
    ppermute x36, waiting for transfers between devices: 82.2 us -> 86 us  [swap(): return lax.ppermute(x, axis, [(i, i ^ bit) for i in range(n)])]
    add x10, other arithmetic: 4.42 us -> 0.95 us  [halves_scatter(): x = keep.astype(F32) + got.astype(F32)]
    dynamic_slice x8, local copies, waits for them, and re-layouts: 2.7 us -> 0.31 us  [halves_scatter(): give = lax.dynamic_slice_in_dim(x, (1 - mine) * size, size, 0)]
  transfers between devices with their start and end apart: 49 -> 49, of which waited for: 31 -> 30; matrix products, arithmetic and copies ran while one was open for 8% -> 5% of each run, Pallas kernels for 8% -> 8%
where the time goes in v3:
time: 227 us
  waiting for transfers between devices  102 us (45%)
  starting transfers between devices  55.2 us (24%)
  Pallas kernels  32.4 us (14%)
  matrix products  26.3 us (12%)
  other arithmetic  8.26 us (4%)
    ppermute x36, waiting for transfers between devices, swap(): return lax.ppermute(x, axis, [(i, i ^ bit) for i in range(n)])  86 us
    ppermute x36, starting transfers between devices, swap(): return lax.ppermute(x, axis, [(i, i ^ bit) for i in range(n)])  37.1 us
    pallas_call x8, Pallas kernels, update(): pl.pallas_call(functools.partial(update_kernel, rate, buf is not None), g...  32.4 us
    dot_general x4, matrix products, body(): lax.dot_general(inputs, enc_weight[:, span], over_width, preferred_elemen...  13.7 us
    ppermute x6, waiting for transfers between devices, direct_scatter(): lax.ppermute(give, axis, [(i, (i + shift) % n) for i in range(n)])  12 us
    ppermute x6, starting transfers between devices, direct_gather(): got = lax.ppermute(x, axis, [(i, (i + shift) % n) for i in range(n)])  8.96 us
    ppermute x6, starting transfers between devices, direct_scatter(): lax.ppermute(give, axis, [(i, (i + shift) % n) for i in range(n)])  7.37 us
    dot_general x4, matrix products, body(): lax.dot_general(dec_turned[:, span], full, (((1,), (1,)), ((), ())), pref...  5.82 us
  transfers between devices with their start and end apart: 49, of which 30 were waited for; matrix products, arithmetic and copies ran while one was open for 5% of the time, Pallas kernels for 8%

profile of v3, /device:TPU:0, one launch (start us, length us, event | category | flops | bytes accessed | tf_op | source)
XLA Modules:
  0.0 226.6 jit_solution(12397285362488587801)
XLA Ops:
  4.7 6.7 %collective-permute-start.1 = (bf16[64,2304]{1,0:T(8,128)(2,1)S(1)}, bf16[64,2304]{1,0:T(8,128)(2,1)S(1)}, u32[]{:S(2)}, u32[]{:S(2)}) collective-permute-start(bf16[64,2304]{1,0:T(8,128)(2,1)S(1)} %fusion.33), channel_id=1, source_target_pairs={{0,1},{1,0},{2,3},{3,2},{4,5},{5,4},{6,7},{7,6},{8,9},{9,8},{10,11... | collective-permute-start | bytes 884744 | tf_op jit(solution)/shard_map/ppermute | solution.py:25
  12.7 8.6 %collective-permute-start.2 = (bf16[32,2304]{1,0:T(8,128)(2,1)S(1)}, bf16[32,2304]{1,0:T(8,128)(2,1)S(1)}, u32[]{:S(2)}, u32[]{:S(2)}) collective-permute-start(bf16[32,2304]{1,0:T(8,128)(2,1)S(1)} %dynamic-slice_convert_fusion.8), channel_id=1, source_target_pairs={{0,2},{1,3},{2,0},{3,1},{4,6},{5,7},{6,4},{7,5},{8,10},{9,11},{10,... | collective-permute-start | bytes 442376 | tf_op jit(solution)/shard_map/ppermute | solution.py:25
  21.3 4.1 %collective-permute-done.2 = bf16[32,2304]{1,0:T(8,128)(2,1)S(1)} collective-permute-done((bf16[32,2304]{1,0:T(8,128)(2,1)S(1)}, bf16[32,2304]{1,0:T(8,128)(2,1)S(1)}, u32[]{:S(2)}, u32[]{:S(2)}) %collective-permute-start.2) | collective-permute-done | bytes 147488 | tf_op jit(solution)/shard_map/ppermute | solution.py:25
  47.0 3.3 %convolution_convert_fusion.7 = bf16[128,4096]{1,0:T(8,128)(2,1)S(1)} fusion(bf16[576,128]{1,0:T(8,128)(2,1)S(1)} %constant_dynamic-update-slice_fusion.4.left_ref, bf16[576,16384]{1,0:T(8,128)(2,1)} %w_ref.7), kind=kOutput, calls=%fused_computation.7 | convolution fusion | flops 604504064 | bytes 5914624 | tf_op jit(solution)/shard_map/dot_general | solution.py:161
  50.3 3.4 %convolution_convert_fusion.4 = bf16[128,4096]{1,0:T(8,128)(2,1)S(1)} fusion(bf16[576,128]{1,0:T(8,128)(2,1)S(1)} %constant_dynamic-update-slice_fusion.4.left_ref, bf16[576,16384]{1,0:T(8,128)(2,1)} %w_ref.7), kind=kOutput, calls=%fused_computation.4 | convolution fusion | flops 604504064 | bytes 5914624 | tf_op jit(solution)/shard_map/dot_general | solution.py:161
  53.7 3.5 %convolution_convert_fusion.5 = bf16[128,4096]{1,0:T(8,128)(2,1)S(1)} fusion(bf16[576,128]{1,0:T(8,128)(2,1)S(1)} %constant_dynamic-update-slice_fusion.4.left_ref, bf16[576,16384]{1,0:T(8,128)(2,1)} %w_ref.7), kind=kOutput, calls=%fused_computation.5 | convolution fusion | flops 604504064 | bytes 5914624 | tf_op jit(solution)/shard_map/dot_general | solution.py:161
  57.2 3.5 %convolution_convert_fusion.6 = bf16[128,4096]{1,0:T(8,128)(2,1)S(1)} fusion(bf16[576,128]{1,0:T(8,128)(2,1)S(1)} %constant_dynamic-update-slice_fusion.4.left_ref, bf16[576,16384]{1,0:T(8,128)(2,1)} %w_ref.7), kind=kOutput, calls=%fused_computation.6 | convolution fusion | flops 604504064 | bytes 5914624 | tf_op jit(solution)/shard_map/dot_general | solution.py:161
  67.7 4.4 %collective-permute-done.12 = bf16[32,4096]{1,0:T(8,128)(2,1)S(1)} collective-permute-done((bf16[32,4096]{1,0:T(8,128)(2,1)S(1)}, bf16[32,4096]{1,0:T(8,128)(2,1)S(1)}, u32[]{:S(2)}, u32[]{:S(2)}) %collective-permute-start.12) | collective-permute-done | bytes 262176 | tf_op jit(solution)/shard_map/ppermute | solution.py:25
  73.5 4.3 %collective-permute-done.22 = bf16[32,4096]{1,0:T(8,128)(2,1)S(1)} collective-permute-done((bf16[32,4096]{1,0:T(8,128)(2,1)S(1)}, bf16[32,4096]{1,0:T(8,128)(2,1)S(1)}, u32[]{:S(2)}, u32[]{:S(2)}) %collective-permute-start.22) | collective-permute-done | bytes 262176 | tf_op jit(solution)/shard_map/ppermute | solution.py:25
  79.1 4.3 %collective-permute-done.18 = bf16[32,4096]{1,0:T(8,128)(2,1)S(1)} collective-permute-done((bf16[32,4096]{1,0:T(8,128)(2,1)S(1)}, bf16[32,4096]{1,0:T(8,128)(2,1)S(1)}, u32[]{:S(2)}, u32[]{:S(2)}) %collective-permute-start.18) | collective-permute-done | bytes 262176 | tf_op jit(solution)/shard_map/ppermute | solution.py:25
  84.7 4.3 %collective-permute-done.14 = bf16[32,4096]{1,0:T(8,128)(2,1)S(1)} collective-permute-done((bf16[32,4096]{1,0:T(8,128)(2,1)S(1)}, bf16[32,4096]{1,0:T(8,128)(2,1)S(1)}, u32[]{:S(2)}, u32[]{:S(2)}) %collective-permute-start.14) | collective-permute-done | bytes 262176 | tf_op jit(solution)/shard_map/ppermute | solution.py:25
  90.4 4.3 %collective-permute-done.25 = bf16[32,4096]{1,0:T(8,128)(2,1)S(1)} collective-permute-done((bf16[32,4096]{1,0:T(8,128)(2,1)S(1)}, bf16[32,4096]{1,0:T(8,128)(2,1)S(1)}, u32[]{:S(2)}, u32[]{:S(2)}) %collective-permute-start.25) | collective-permute-done | bytes 262176 | tf_op jit(solution)/shard_map/ppermute | solution.py:25
  94.8 5.4 %collective-permute-done.23 = bf16[32,4096]{1,0:T(8,128)(2,1)S(1)} collective-permute-done((bf16[32,4096]{1,0:T(8,128)(2,1)S(1)}, bf16[32,4096]{1,0:T(8,128)(2,1)S(1)}, u32[]{:S(2)}, u32[]{:S(2)}) %collective-permute-start.23) | collective-permute-done | bytes 262176 | tf_op jit(solution)/shard_map/ppermute | solution.py:25
  100.4 5.5 %collective-permute-done.19 = bf16[32,4096]{1,0:T(8,128)(2,1)S(1)} collective-permute-done((bf16[32,4096]{1,0:T(8,128)(2,1)S(1)}, bf16[32,4096]{1,0:T(8,128)(2,1)S(1)}, u32[]{:S(2)}, u32[]{:S(2)}) %collective-permute-start.19) | collective-permute-done | bytes 262176 | tf_op jit(solution)/shard_map/ppermute | solution.py:25
  106.0 4.6 %collective-permute-done.15 = bf16[32,4096]{1,0:T(8,128)(2,1)S(1)} collective-permute-done((bf16[32,4096]{1,0:T(8,128)(2,1)S(1)}, bf16[32,4096]{1,0:T(8,128)(2,1)S(1)}, u32[]{:S(2)}, u32[]{:S(2)}) %collective-permute-start.15) | collective-permute-done | bytes 262176 | tf_op jit(solution)/shard_map/ppermute | solution.py:25
  117.8 3.6 %collective-permute-start.29 = (f32[144,128]{1,0:T(8,128)S(1)}, f32[144,128]{1,0:T(8,128)S(1)}, u32[]{:S(2)}, u32[]{:S(2)}) collective-permute-start(f32[144,128]{1,0:T(8,128)S(1)} %get-tuple-element.65), channel_id=1, source_target_pairs={{0,12},{4,0},{8,4},{12,8},{1,13},{5,1},{9,5},{13,9},{2,14},{6,2},{... | collective-permute-start | bytes 221192 | tf_op jit(solution)/shard_map/ppermute | solution.py:61
  124.0 5.0 %collective-permute-done.28 = f32[144,128]{1,0:T(8,128)S(1)} collective-permute-done((f32[144,128]{1,0:T(8,128)S(1)}, f32[144,128]{1,0:T(8,128)S(1)}, u32[]{:S(2)}, u32[]{:S(2)}) %collective-permute-start.28) | collective-permute-done | bytes 73760 | tf_op jit(solution)/shard_map/ppermute | solution.py:61
  141.3 3.4 %shard_map.115 = (bf16[576,16384]{1,0:T(8,128)(2,1)}, f32[8,4096]{1,0:T(8,128)}) custom-call(bf16[576,128]{1,0:T(8,128)(2,1)S(1)} %constant_dynamic-update-slice_fusion.left_ref, bf16[128,4096]{1,0:T(8,128)(2,1)S(1)} %pad_maximum_fusion.right_ref, bf16[576,16384]{1,0:T(8,128)(2,1)S(1)} %bitcast.68), custom_call_target="tpu_custom_call" | custom-call | flops 603979776 | bytes 9437184 | tf_op jit(solution)/shard_map/pallas_call | solution.py:104
  144.7 3.4 %shard_map.116 = (bf16[576,16384]{1,0:T(8,128)(2,1)}, f32[8,4096]{1,0:T(8,128)}) custom-call(bf16[576,128]{1,0:T(8,128)(2,1)S(1)} %constant_dynamic-update-slice_fusion.left_ref, bf16[128,4096]{1,0:T(8,128)(2,1)S(1)} %pad_maximum_fusion.1.right_ref, bf16[576,16384]{1,0:T(8,128)(2,1)S(1)} %bitcast.69, ...), custom_call_target="tpu_custom_call", output_to_operand_aliasing={{0}: (3, {})} | custom-call | flops 603979776 | bytes 9437184 | tf_op jit(solution)/shard_map/pallas_call | solution.py:104
  148.1 3.4 %shard_map.117 = (bf16[576,16384]{1,0:T(8,128)(2,1)}, f32[8,4096]{1,0:T(8,128)}) custom-call(bf16[576,128]{1,0:T(8,128)(2,1)S(1)} %constant_dynamic-update-slice_fusion.left_ref, bf16[128,4096]{1,0:T(8,128)(2,1)S(1)} %pad_maximum_fusion.2.right_ref, bf16[576,16384]{1,0:T(8,128)(2,1)S(1)} %bitcast.70, ...), custom_call_target="tpu_custom_call", output_to_operand_aliasing={{0}: (3, {})} | custom-call | flops 603979776 | bytes 9437184 | tf_op jit(solution)/shard_map/pallas_call | solution.py:104
  151.4 3.4 %shard_map.118 = (bf16[576,16384]{1,0:T(8,128)(2,1)}, f32[8,4096]{1,0:T(8,128)}) custom-call(bf16[576,128]{1,0:T(8,128)(2,1)S(1)} %constant_dynamic-update-slice_fusion.left_ref, bf16[128,4096]{1,0:T(8,128)(2,1)S(1)} %pad_maximum_fusion.3.right_ref, bf16[576,16384]{1,0:T(8,128)(2,1)S(1)} %bitcast.71, ...), custom_call_target="tpu_custom_call", output_to_operand_aliasing={{0}: (3, {})} | custom-call | flops 603979776 | bytes 9437184 | tf_op jit(solution)/shard_map/pallas_call | solution.py:104
  160.5 4.4 %collective-permute-done.38 = bf16[32,4096]{1,0:T(8,128)(2,1)S(1)} collective-permute-done((bf16[32,4096]{1,0:T(8,128)(2,1)S(1)}, bf16[32,4096]{1,0:T(8,128)(2,1)S(1)}, u32[]{:S(2)}, u32[]{:S(2)}) %collective-permute-start.38) | collective-permute-done | bytes 262176 | tf_op jit(solution)/shard_map/ppermute | solution.py:25
  166.2 4.4 %collective-permute-done.34 = bf16[32,4096]{1,0:T(8,128)(2,1)S(1)} collective-permute-done((bf16[32,4096]{1,0:T(8,128)(2,1)S(1)}, bf16[32,4096]{1,0:T(8,128)(2,1)S(1)}, u32[]{:S(2)}, u32[]{:S(2)}) %collective-permute-start.34) | collective-permute-done | bytes 262176 | tf_op jit(solution)/shard_map/ppermute | solution.py:25
  171.8 4.4 %collective-permute-done.46 = bf16[32,4096]{1,0:T(8,128)(2,1)S(1)} collective-permute-done((bf16[32,4096]{1,0:T(8,128)(2,1)S(1)}, bf16[32,4096]{1,0:T(8,128)(2,1)S(1)}, u32[]{:S(2)}, u32[]{:S(2)}) %collective-permute-start.46) | collective-permute-done | bytes 262176 | tf_op jit(solution)/shard_map/ppermute | solution.py:25
  177.4 4.4 %collective-permute-done.42 = bf16[32,4096]{1,0:T(8,128)(2,1)S(1)} collective-permute-done((bf16[32,4096]{1,0:T(8,128)(2,1)S(1)}, bf16[32,4096]{1,0:T(8,128)(2,1)S(1)}, u32[]{:S(2)}, u32[]{:S(2)}) %collective-permute-start.42) | collective-permute-done | bytes 262176 | tf_op jit(solution)/shard_map/ppermute | solution.py:25
  183.1 4.4 %collective-permute-done.39 = bf16[32,4096]{1,0:T(8,128)(2,1)S(1)} collective-permute-done((bf16[32,4096]{1,0:T(8,128)(2,1)S(1)}, bf16[32,4096]{1,0:T(8,128)(2,1)S(1)}, u32[]{:S(2)}, u32[]{:S(2)}) %collective-permute-start.39) | collective-permute-done | bytes 262176 | tf_op jit(solution)/shard_map/ppermute | solution.py:25
  187.6 11.1 %collective-permute-done.47 = bf16[32,4096]{1,0:T(8,128)(2,1)S(1)} collective-permute-done((bf16[32,4096]{1,0:T(8,128)(2,1)S(1)}, bf16[32,4096]{1,0:T(8,128)(2,1)S(1)}, u32[]{:S(2)}, u32[]{:S(2)}) %collective-permute-start.47) | collective-permute-done | bytes 262176 | tf_op jit(solution)/shard_map/ppermute | solution.py:25
  198.9 4.8 %collective-permute-done.43 = bf16[32,4096]{1,0:T(8,128)(2,1)S(1)} collective-permute-done((bf16[32,4096]{1,0:T(8,128)(2,1)S(1)}, bf16[32,4096]{1,0:T(8,128)(2,1)S(1)}, u32[]{:S(2)}, u32[]{:S(2)}) %collective-permute-start.43) | collective-permute-done | bytes 262176 | tf_op jit(solution)/shard_map/ppermute | solution.py:25
  206.2 4.7 %shard_map.111 = (bf16[576,16384]{1,0:T(8,128)(2,1)}, f32[8,4096]{1,0:T(8,128)S(1)}) custom-call(bf16[576,128]{1,0:T(8,128)(2,1)S(1)} %constant_dynamic-update-slice_fusion.4.left_ref, bf16[128,4096]{1,0:T(8,128)(2,1)S(1)} %pad_maximum_fusion.7.right_ref, bf16[576,16384]{1,0:T(8,128)(2,1)} %w_ref.7), custom_call_target="tpu_custom_call" | custom-call | flops 603979776 | bytes 9437184 | tf_op jit(solution)/shard_map/pallas_call | solution.py:104
  211.7 4.7 %shard_map.112 = (bf16[576,16384]{1,0:T(8,128)(2,1)}, f32[8,4096]{1,0:T(8,128)S(1)}) custom-call(bf16[576,128]{1,0:T(8,128)(2,1)S(1)} %constant_dynamic-update-slice_fusion.4.left_ref, bf16[128,4096]{1,0:T(8,128)(2,1)S(1)} %pad_maximum_fusion.6.right_ref, bf16[576,16384]{1,0:T(8,128)(2,1)} %w_ref.7, ...), custom_call_target="tpu_custom_call", output_to_operand_aliasing={{0}: (3, {})} | custom-call | flops 603979776 | bytes 9437184 | tf_op jit(solution)/shard_map/pallas_call | solution.py:104
  216.4 4.7 %shard_map.113 = (bf16[576,16384]{1,0:T(8,128)(2,1)}, f32[8,4096]{1,0:T(8,128)S(1)}) custom-call(bf16[576,128]{1,0:T(8,128)(2,1)S(1)} %constant_dynamic-update-slice_fusion.4.left_ref, bf16[128,4096]{1,0:T(8,128)(2,1)S(1)} %pad_maximum_fusion.5.right_ref, bf16[576,16384]{1,0:T(8,128)(2,1)} %w_ref.7, ...), custom_call_target="tpu_custom_call", output_to_operand_aliasing={{0}: (3, {})} | custom-call | flops 603979776 | bytes 9437184 | tf_op jit(solution)/shard_map/pallas_call | solution.py:104
  221.1 4.8 %shard_map.114 = (bf16[576,16384]{1,0:T(8,128)(2,1)}, f32[8,4096]{1,0:T(8,128)S(1)}) custom-call(bf16[576,128]{1,0:T(8,128)(2,1)S(1)} %constant_dynamic-update-slice_fusion.4.left_ref, bf16[128,4096]{1,0:T(8,128)(2,1)S(1)} %pad_maximum_fusion.4.right_ref, bf16[576,16384]{1,0:T(8,128)(2,1)} %w_ref.7, ...), custom_call_target="tpu_custom_call", output_to_operand_aliasing={{0}: (3, {})} | custom-call | flops 603979776 | bytes 9437184 | tf_op jit(solution)/shard_map/pallas_call | solution.py:104
  (201 shorter events, 76.0 us)
Async XLA Ops:
  4.7 7.9 %collective-permute-start.1 = (bf16[64,2304]{1,0:T(8,128)(2,1)S(1)}, bf16[64,2304]{1,0:T(8,128)(2,1)S(1)}, u32[]{:S(2)}, u32[]{:S(2)}) collective-permute-start(bf16[64,2304]{1,0:T(8,128)(2,1)S(1)} %fusion.33), channel_id=1, source_target_pairs={{0,1},{1,0},{2,3},{3,2},{4,5},{5,4},{6,7},{7,6},{8,9},{9,8},{10,11... | collective-permute-start | bytes 884744 | tf_op jit(solution)/shard_map/ppermute | solution.py:25
  12.7 12.8 %collective-permute-start.2 = (bf16[32,2304]{1,0:T(8,128)(2,1)S(1)}, bf16[32,2304]{1,0:T(8,128)(2,1)S(1)}, u32[]{:S(2)}, u32[]{:S(2)}) collective-permute-start(bf16[32,2304]{1,0:T(8,128)(2,1)S(1)} %dynamic-slice_convert_fusion.8), channel_id=1, source_target_pairs={{0,2},{1,3},{2,0},{3,1},{4,6},{5,7},{6,4},{7,5},{8,10},{9,11},{10,... | collective-permute-start | bytes 442376 | tf_op jit(solution)/shard_map/ppermute | solution.py:25
  40.5 5.8 %collective-permute-start.8 = (bf16[144,128]{1,0:T(8,128)(2,1)S(1)}, bf16[144,128]{1,0:T(8,128)(2,1)S(1)}, u32[]{:S(2)}, u32[]{:S(2)}) collective-permute-start(bf16[144,128]{1,0:T(8,128)(2,1)S(1)} %get-tuple-element.31), channel_id=1, source_target_pairs={{0,4},{4,8},{8,12},{12,0},{1,5},{5,9},{9,13},{13,1},{2,6},{6,10},{... | collective-permute-start | bytes 110600 | tf_op jit(solution)/shard_map/ppermute | solution.py:73
  62.9 9.2 %collective-permute-start.12 = (bf16[32,4096]{1,0:T(8,128)(2,1)S(1)}, bf16[32,4096]{1,0:T(8,128)(2,1)S(1)}, u32[]{:S(2)}, u32[]{:S(2)}) collective-permute-start(bf16[32,4096]{1,0:T(8,128)(2,1)S(1)} %dynamic-slice_convert_fusion.7), channel_id=1, source_target_pairs={{0,2},{1,3},{2,0},{3,1},{4,6},{5,7},{6,4},{7,5},{8,10},{9,11},{10,... | collective-permute-start | bytes 786440 | tf_op jit(solution)/shard_map/ppermute | solution.py:25
  64.0 13.7 %collective-permute-start.22 = (bf16[32,4096]{1,0:T(8,128)(2,1)S(1)}, bf16[32,4096]{1,0:T(8,128)(2,1)S(1)}, u32[]{:S(2)}, u32[]{:S(2)}) collective-permute-start(bf16[32,4096]{1,0:T(8,128)(2,1)S(1)} %dynamic-slice_convert_fusion.4), channel_id=1, source_target_pairs={{0,2},{1,3},{2,0},{3,1},{4,6},{5,7},{6,4},{7,5},{8,10},{9,11},{10,... | collective-permute-start | bytes 786440 | tf_op jit(solution)/shard_map/ppermute | solution.py:25
  65.4 18.0 %collective-permute-start.18 = (bf16[32,4096]{1,0:T(8,128)(2,1)S(1)}, bf16[32,4096]{1,0:T(8,128)(2,1)S(1)}, u32[]{:S(2)}, u32[]{:S(2)}) collective-permute-start(bf16[32,4096]{1,0:T(8,128)(2,1)S(1)} %dynamic-slice_convert_fusion.5), channel_id=1, source_target_pairs={{0,2},{1,3},{2,0},{3,1},{4,6},{5,7},{6,4},{7,5},{8,10},{9,11},{10,... | collective-permute-start | bytes 786440 | tf_op jit(solution)/shard_map/ppermute | solution.py:25
  66.5 22.5 %collective-permute-start.14 = (bf16[32,4096]{1,0:T(8,128)(2,1)S(1)}, bf16[32,4096]{1,0:T(8,128)(2,1)S(1)}, u32[]{:S(2)}, u32[]{:S(2)}) collective-permute-start(bf16[32,4096]{1,0:T(8,128)(2,1)S(1)} %dynamic-slice_convert_fusion.6), channel_id=1, source_target_pairs={{0,2},{1,3},{2,0},{3,1},{4,6},{5,7},{6,4},{7,5},{8,10},{9,11},{10,... | collective-permute-start | bytes 786440 | tf_op jit(solution)/shard_map/ppermute | solution.py:25
  72.5 22.1 %collective-permute-start.25 = (bf16[32,4096]{1,0:T(8,128)(2,1)S(1)}, bf16[32,4096]{1,0:T(8,128)(2,1)S(1)}, u32[]{:S(2)}, u32[]{:S(2)}) collective-permute-start(bf16[32,4096]{1,0:T(8,128)(2,1)S(1)} %fusion.32), channel_id=1, source_target_pairs={{0,2},{1,3},{2,0},{3,1},{4,6},{5,7},{6,4},{7,5},{8,10},{9,11},{10,... | collective-permute-start | bytes 786440 | tf_op jit(solution)/shard_map/ppermute | solution.py:25
  78.2 22.1 %collective-permute-start.23 = (bf16[32,4096]{1,0:T(8,128)(2,1)S(1)}, bf16[32,4096]{1,0:T(8,128)(2,1)S(1)}, u32[]{:S(2)}, u32[]{:S(2)}) collective-permute-start(bf16[32,4096]{1,0:T(8,128)(2,1)S(1)} %fusion.30), channel_id=1, source_target_pairs={{0,2},{1,3},{2,0},{3,1},{4,6},{5,7},{6,4},{7,5},{8,10},{9,11},{10,... | collective-permute-start | bytes 786440 | tf_op jit(solution)/shard_map/ppermute | solution.py:25
  83.8 22.1 %collective-permute-start.19 = (bf16[32,4096]{1,0:T(8,128)(2,1)S(1)}, bf16[32,4096]{1,0:T(8,128)(2,1)S(1)}, u32[]{:S(2)}, u32[]{:S(2)}) collective-permute-start(bf16[32,4096]{1,0:T(8,128)(2,1)S(1)} %fusion.28), channel_id=1, source_target_pairs={{0,2},{1,3},{2,0},{3,1},{4,6},{5,7},{6,4},{7,5},{8,10},{9,11},{10,... | collective-permute-start | bytes 786440 | tf_op jit(solution)/shard_map/ppermute | solution.py:25
  89.4 21.2 %collective-permute-start.15 = (bf16[32,4096]{1,0:T(8,128)(2,1)S(1)}, bf16[32,4096]{1,0:T(8,128)(2,1)S(1)}, u32[]{:S(2)}, u32[]{:S(2)}) collective-permute-start(bf16[32,4096]{1,0:T(8,128)(2,1)S(1)} %fusion.26), channel_id=1, source_target_pairs={{0,2},{1,3},{2,0},{3,1},{4,6},{5,7},{6,4},{7,5},{8,10},{9,11},{10,... | collective-permute-start | bytes 786440 | tf_op jit(solution)/shard_map/ppermute | solution.py:25
  94.7 16.1 %collective-permute-start.26 = (bf16[64,4096]{1,0:T(8,128)(2,1)S(1)}, bf16[64,4096]{1,0:T(8,128)(2,1)S(1)}, u32[]{:S(2)}, u32[]{:S(2)}) collective-permute-start(bf16[64,4096]{1,0:T(8,128)(2,1)S(1)} %pad_maximum_fusion.11), channel_id=1, source_target_pairs={{0,1},{1,0},{2,3},{3,2},{4,5},{5,4},{6,7},{7,6},{8,9},{9,8},{10,11... | collective-permute-start | bytes 1572872 | tf_op jit(solution)/shard_map/ppermute | solution.py:25
  100.3 12.2 %collective-permute-start.24 = (bf16[64,4096]{1,0:T(8,128)(2,1)S(1)}, bf16[64,4096]{1,0:T(8,128)(2,1)S(1)}, u32[]{:S(2)}, u32[]{:S(2)}) collective-permute-start(bf16[64,4096]{1,0:T(8,128)(2,1)S(1)} %pad_maximum_fusion.10), channel_id=1, source_target_pairs={{0,1},{1,0},{2,3},{3,2},{4,5},{5,4},{6,7},{7,6},{8,9},{9,8},{10,11... | collective-permute-start | bytes 1572872 | tf_op jit(solution)/shard_map/ppermute | solution.py:25
  105.9 8.2 %collective-permute-start.20 = (bf16[64,4096]{1,0:T(8,128)(2,1)S(1)}, bf16[64,4096]{1,0:T(8,128)(2,1)S(1)}, u32[]{:S(2)}, u32[]{:S(2)}) collective-permute-start(bf16[64,4096]{1,0:T(8,128)(2,1)S(1)} %pad_maximum_fusion.9), channel_id=1, source_target_pairs={{0,1},{1,0},{2,3},{3,2},{4,5},{5,4},{6,7},{7,6},{8,9},{9,8},{10,11... | collective-permute-start | bytes 1572872 | tf_op jit(solution)/shard_map/ppermute | solution.py:25
  117.8 6.3 %collective-permute-start.29 = (f32[144,128]{1,0:T(8,128)S(1)}, f32[144,128]{1,0:T(8,128)S(1)}, u32[]{:S(2)}, u32[]{:S(2)}) collective-permute-start(f32[144,128]{1,0:T(8,128)S(1)} %get-tuple-element.65), channel_id=1, source_target_pairs={{0,12},{4,0},{8,4},{12,8},{1,13},{5,1},{9,5},{13,9},{2,14},{6,2},{... | collective-permute-start | bytes 221192 | tf_op jit(solution)/shard_map/ppermute | solution.py:61
  121.3 7.7 %collective-permute-start.28 = (f32[144,128]{1,0:T(8,128)S(1)}, f32[144,128]{1,0:T(8,128)S(1)}, u32[]{:S(2)}, u32[]{:S(2)}) collective-permute-start(f32[144,128]{1,0:T(8,128)S(1)} %get-tuple-element.66), channel_id=1, source_target_pairs={{0,8},{4,12},{8,0},{12,4},{1,9},{5,13},{9,1},{13,5},{2,10},{6,14},... | collective-permute-start | bytes 221192 | tf_op jit(solution)/shard_map/ppermute | solution.py:61
  121.3 7.7 %collective-permute-start.27 = (f32[144,128]{1,0:T(8,128)S(1)}, f32[144,128]{1,0:T(8,128)S(1)}, u32[]{:S(2)}, u32[]{:S(2)}) collective-permute-start(f32[144,128]{1,0:T(8,128)S(1)} %get-tuple-element.64), channel_id=1, source_target_pairs={{0,4},{4,8},{8,12},{12,0},{1,5},{5,9},{9,13},{13,1},{2,6},{6,10},{... | collective-permute-start | bytes 221192 | tf_op jit(solution)/shard_map/ppermute | solution.py:61
  129.1 6.1 %collective-permute-start.30 = (bf16[144,128]{1,0:T(8,128)(2,1)S(1)}, bf16[144,128]{1,0:T(8,128)(2,1)S(1)}, u32[]{:S(2)}, u32[]{:S(2)}) collective-permute-start(bf16[144,128]{1,0:T(8,128)(2,1)S(1)} %get-tuple-element.29), channel_id=1, source_target_pairs={{0,4},{4,8},{8,12},{12,0},{1,5},{5,9},{9,13},{13,1},{2,6},{6,10},{... | collective-permute-start | bytes 110600 | tf_op jit(solution)/shard_map/ppermute | solution.py:73
  139.9 15.7 %collective-permute-start.37 = (bf16[64,4096]{1,0:T(8,128)(2,1)S(1)}, bf16[64,4096]{1,0:T(8,128)(2,1)S(1)}, u32[]{:S(2)}, u32[]{:S(2)}) collective-permute-start(bf16[64,4096]{1,0:T(8,128)(2,1)S(1)} %constant_dynamic-slice_fusion.2), channel_id=1, source_target_pairs={{0,1},{1,0},{2,3},{3,2},{4,5},{5,4},{6,7},{7,6},{8,9},{9,8},{10,11... | collective-permute-start | bytes 1572872 | tf_op jit(solution)/shard_map/ppermute | solution.py:25
  140.0 16.7 %collective-permute-start.33 = (bf16[64,4096]{1,0:T(8,128)(2,1)S(1)}, bf16[64,4096]{1,0:T(8,128)(2,1)S(1)}, u32[]{:S(2)}, u32[]{:S(2)}) collective-permute-start(bf16[64,4096]{1,0:T(8,128)(2,1)S(1)} %constant_dynamic-slice_fusion.3), channel_id=1, source_target_pairs={{0,1},{1,0},{2,3},{3,2},{4,5},{5,4},{6,7},{7,6},{8,9},{9,8},{10,11... | collective-permute-start | bytes 1572872 | tf_op jit(solution)/shard_map/ppermute | solution.py:25
  140.6 17.5 %collective-permute-start.45 = (bf16[64,4096]{1,0:T(8,128)(2,1)S(1)}, bf16[64,4096]{1,0:T(8,128)(2,1)S(1)}, u32[]{:S(2)}, u32[]{:S(2)}) collective-permute-start(bf16[64,4096]{1,0:T(8,128)(2,1)S(1)} %constant_dynamic-slice_fusion), channel_id=1, source_target_pairs={{0,1},{1,0},{2,3},{3,2},{4,5},{5,4},{6,7},{7,6},{8,9},{9,8},{10,11... | collective-permute-start | bytes 1572872 | tf_op jit(solution)/shard_map/ppermute | solution.py:25
  140.7 18.5 %collective-permute-start.41 = (bf16[64,4096]{1,0:T(8,128)(2,1)S(1)}, bf16[64,4096]{1,0:T(8,128)(2,1)S(1)}, u32[]{:S(2)}, u32[]{:S(2)}) collective-permute-start(bf16[64,4096]{1,0:T(8,128)(2,1)S(1)} %constant_dynamic-slice_fusion.1), channel_id=1, source_target_pairs={{0,1},{1,0},{2,3},{3,2},{4,5},{5,4},{6,7},{7,6},{8,9},{9,8},{10,11... | collective-permute-start | bytes 1572872 | tf_op jit(solution)/shard_map/ppermute | solution.py:25
  155.7 9.2 %collective-permute-start.38 = (bf16[32,4096]{1,0:T(8,128)(2,1)S(1)}, bf16[32,4096]{1,0:T(8,128)(2,1)S(1)}, u32[]{:S(2)}, u32[]{:S(2)}) collective-permute-start(bf16[32,4096]{1,0:T(8,128)(2,1)S(1)} %dynamic-slice_convert_fusion.2), channel_id=1, source_target_pairs={{0,2},{1,3},{2,0},{3,1},{4,6},{5,7},{6,4},{7,5},{8,10},{9,11},{10,... | collective-permute-start | bytes 786440 | tf_op jit(solution)/shard_map/ppermute | solution.py:25
  156.9 13.7 %collective-permute-start.34 = (bf16[32,4096]{1,0:T(8,128)(2,1)S(1)}, bf16[32,4096]{1,0:T(8,128)(2,1)S(1)}, u32[]{:S(2)}, u32[]{:S(2)}) collective-permute-start(bf16[32,4096]{1,0:T(8,128)(2,1)S(1)} %dynamic-slice_convert_fusion.3), channel_id=1, source_target_pairs={{0,2},{1,3},{2,0},{3,1},{4,6},{5,7},{6,4},{7,5},{8,10},{9,11},{10,... | collective-permute-start | bytes 786440 | tf_op jit(solution)/shard_map/ppermute | solution.py:25
  158.2 18.0 %collective-permute-start.46 = (bf16[32,4096]{1,0:T(8,128)(2,1)S(1)}, bf16[32,4096]{1,0:T(8,128)(2,1)S(1)}, u32[]{:S(2)}, u32[]{:S(2)}) collective-permute-start(bf16[32,4096]{1,0:T(8,128)(2,1)S(1)} %dynamic-slice_convert_fusion), channel_id=1, source_target_pairs={{0,2},{1,3},{2,0},{3,1},{4,6},{5,7},{6,4},{7,5},{8,10},{9,11},{10,... | collective-permute-start | bytes 786440 | tf_op jit(solution)/shard_map/ppermute | solution.py:25
  159.3 22.5 %collective-permute-start.42 = (bf16[32,4096]{1,0:T(8,128)(2,1)S(1)}, bf16[32,4096]{1,0:T(8,128)(2,1)S(1)}, u32[]{:S(2)}, u32[]{:S(2)}) collective-permute-start(bf16[32,4096]{1,0:T(8,128)(2,1)S(1)} %dynamic-slice_convert_fusion.1), channel_id=1, source_target_pairs={{0,2},{1,3},{2,0},{3,1},{4,6},{5,7},{6,4},{7,5},{8,10},{9,11},{10,... | collective-permute-start | bytes 786440 | tf_op jit(solution)/shard_map/ppermute | solution.py:25
  165.2 22.2 %collective-permute-start.39 = (bf16[32,4096]{1,0:T(8,128)(2,1)S(1)}, bf16[32,4096]{1,0:T(8,128)(2,1)S(1)}, u32[]{:S(2)}, u32[]{:S(2)}) collective-permute-start(bf16[32,4096]{1,0:T(8,128)(2,1)S(1)} %multiply_convert_fusion.2), channel_id=1, source_target_pairs={{0,2},{1,3},{2,0},{3,1},{4,6},{5,7},{6,4},{7,5},{8,10},{9,11},{10,... | collective-permute-start | bytes 786440 | tf_op jit(solution)/shard_map/ppermute | solution.py:25
  170.9 32.9 %collective-permute-start.35 = (bf16[32,4096]{1,0:T(8,128)(2,1)S(1)}, bf16[32,4096]{1,0:T(8,128)(2,1)S(1)}, u32[]{:S(2)}, u32[]{:S(2)}) collective-permute-start(bf16[32,4096]{1,0:T(8,128)(2,1)S(1)} %multiply_convert_fusion.3), channel_id=1, source_target_pairs={{0,2},{1,3},{2,0},{3,1},{4,6},{5,7},{6,4},{7,5},{8,10},{9,11},{10,... | collective-permute-start | bytes 786440 | tf_op jit(solution)/shard_map/ppermute | solution.py:25
  176.5 22.2 %collective-permute-start.47 = (bf16[32,4096]{1,0:T(8,128)(2,1)S(1)}, bf16[32,4096]{1,0:T(8,128)(2,1)S(1)}, u32[]{:S(2)}, u32[]{:S(2)}) collective-permute-start(bf16[32,4096]{1,0:T(8,128)(2,1)S(1)} %multiply_convert_fusion), channel_id=1, source_target_pairs={{0,2},{1,3},{2,0},{3,1},{4,6},{5,7},{6,4},{7,5},{8,10},{9,11},{10,... | collective-permute-start | bytes 786440 | tf_op jit(solution)/shard_map/ppermute | solution.py:25
  182.1 21.5 %collective-permute-start.43 = (bf16[32,4096]{1,0:T(8,128)(2,1)S(1)}, bf16[32,4096]{1,0:T(8,128)(2,1)S(1)}, u32[]{:S(2)}, u32[]{:S(2)}) collective-permute-start(bf16[32,4096]{1,0:T(8,128)(2,1)S(1)} %multiply_convert_fusion.1), channel_id=1, source_target_pairs={{0,2},{1,3},{2,0},{3,1},{4,6},{5,7},{6,4},{7,5},{8,10},{9,11},{10,... | collective-permute-start | bytes 786440 | tf_op jit(solution)/shard_map/ppermute | solution.py:25
  187.5 23.4 %collective-permute-start.40 = (bf16[64,4096]{1,0:T(8,128)(2,1)S(1)}, bf16[64,4096]{1,0:T(8,128)(2,1)S(1)}, u32[]{:S(2)}, u32[]{:S(2)}) collective-permute-start(bf16[64,4096]{1,0:T(8,128)(2,1)S(1)} %pad_maximum_fusion.13), channel_id=1, source_target_pairs={{0,1},{1,0},{2,3},{3,2},{4,5},{5,4},{6,7},{7,6},{8,9},{9,8},{10,11... | collective-permute-start | bytes 1572872 | tf_op jit(solution)/shard_map/ppermute | solution.py:25
  203.9 7.0 %collective-permute-start.36 = (bf16[64,4096]{1,0:T(8,128)(2,1)S(1)}, bf16[64,4096]{1,0:T(8,128)(2,1)S(1)}, u32[]{:S(2)}, u32[]{:S(2)}) collective-permute-start(bf16[64,4096]{1,0:T(8,128)(2,1)S(1)} %pad_maximum_fusion.12), channel_id=1, source_target_pairs={{0,1},{1,0},{2,3},{3,2},{4,5},{5,4},{6,7},{7,6},{8,9},{9,8},{10,11... | collective-permute-start | bytes 1572872 | tf_op jit(solution)/shard_map/ppermute | solution.py:25
  (27 other events, 406.1 us)

commit v4 on v3

--- a/solution.py
+++ b/solution.py
@@ -39,14 +39,29 @@
     return x
 
 
-def halves_gather(x, axis, n):
+def halves_gather(x, axis, n, ordered=True):
     me = lax.axis_index(axis)
     bit = n // 2
     while bit >= 1:
         got = swap(x, axis, n, bit)
+        if not ordered:
+            x = jnp.concatenate([x, got], axis=0)
+            bit //= 2
+            continue
         first = ((me // bit) % 2) == 0
         x = jnp.concatenate([jnp.where(first, x, got), jnp.where(first, got, x)], axis=0)
         bit //= 2
+    return x
+
+
+def own_first(x, axis, n):
+    me = lax.axis_index(axis)
+    bit, size = 1, x.shape[1]
+    while bit < n:
+        half = size // 2
+        split = x.reshape(x.shape[0], -1, 2, half)
+        x = jnp.where(((me // bit) % 2) == 0, split, split[:, :, ::-1]).reshape(x.shape)
+        bit, size = bit * 2, half
     return x
 
 
@@ -89,7 +104,7 @@
 def update(rate, left, right, weight, first, buf, grant):
     depth, tokens = left.shape
     columns = right.shape[1]
-    tile = min(2048, columns)
+    tile = min(512, columns)
     base = first // tile
     block = pl.BlockSpec((depth, tile), lambda i: (0, base + i))
     in_specs = [
@@ -178,13 +193,14 @@
         part = lax.dot_general(residual_grad, dec_turned[:, span], over_width, preferred_element_type=F32).astype(BF16)
         back = halves_scatter(part, "rows", n_rows, BF16)
         mine = (jax.nn.sigmoid(sharpness * pres[c]) * (dec_scale * back + sparsity_cost)).astype(BF16)
-        grads.append(halves_gather(mine, "rows", n_rows))
+        grads.append(halves_gather(mine, "rows", n_rows, ordered=False))
     dec_new = enc_new = None
     for c, span in enumerate(spans):
         dec_new, _ = update(weight_rate * dec_scale, residual_grad, latents[c], dec_turned, c * step, dec_new, 24 << 20)
     sums = []
+    turned_inputs = own_first(inputs, "rows", n_rows)
     for c, span in enumerate(spans):
-        enc_new, total = update(weight_rate * enc_scale, inputs, grads[c], enc_weight, c * step, enc_new, 52 << 20)
+        enc_new, total = update(weight_rate * enc_scale, turned_inputs, grads[c], enc_weight, c * step, enc_new, 52 << 20)
         sums.append(total[0])
     enc_bias = enc_bias - enc_bias_rate * jnp.concatenate(sums)
     dec_bias = dec_bias - dec_bias_rate * jnp.sum(residual_grad, axis=1, dtype=F32)

time: 227 us -> 253 us (1.11)
  Pallas kernels: 32.4 us -> 51.8 us
  local copies, waits for them, and re-layouts: 1 us -> 6.54 us
    pallas_call x8, Pallas kernels: 32.4 us -> 51.8 us  [update(): pl.pallas_call(functools.partial(update_kernel, rate, buf is not None), g...]
    dynamic_slice x8, local copies, waits for them, and re-layouts: 0.31 us -> 3.68 us  [halves_scatter(): give = lax.dynamic_slice_in_dim(x, (1 - mine) * size, size, 0)]
    dot_general x4, matrix products: 13.7 us -> 16.4 us  [body(): lax.dot_general(inputs, enc_weight[:, span], over_width, preferred_elemen...]
  transfers between devices with their start and end apart: 49 -> 49, of which waited for: 30 -> 29; matrix products, arithmetic and copies ran while one was open for 5% -> 6% of each run, Pallas kernels for 8% -> 17%
where the time goes in v4:
time: 253 us; the launch traced here: 252 us
  waiting for transfers between devices  102 us (40%)
  starting transfers between devices  54.3 us (21%)
  Pallas kernels  51.8 us (20%)
  matrix products  27.7 us (11%)
  other arithmetic  8.33 us (3%)
  local copies, waits for them, and re-layouts  6.54 us (3%)
    ppermute x36, waiting for transfers between devices, swap(): return lax.ppermute(x, axis, [(i, i ^ bit) for i in range(n)])  86 us
    pallas_call x8, Pallas kernels, update(): pl.pallas_call(functools.partial(update_kernel, rate, buf is not None), g...  51.8 us
    ppermute x36, starting transfers between devices, swap(): return lax.ppermute(x, axis, [(i, i ^ bit) for i in range(n)])  36.3 us
    dot_general x4, matrix products, body(): lax.dot_general(inputs, enc_weight[:, span], over_width, preferred_elemen...  16.4 us
    ppermute x6, waiting for transfers between devices, direct_scatter(): lax.ppermute(give, axis, [(i, (i + shift) % n) for i in range(n)])  12 us
    ppermute x6, starting transfers between devices, direct_gather(): got = lax.ppermute(x, axis, [(i, (i + shift) % n) for i in range(n)])  8.94 us
    ppermute x6, starting transfers between devices, direct_scatter(): lax.ppermute(give, axis, [(i, (i + shift) % n) for i in range(n)])  7.34 us
    dot_general x4, matrix products, body(): lax.dot_general(dec_turned[:, span], full, (((1,), (1,)), ((), ())), pref...  5.79 us
  transfers between devices with their start and end apart: 49, of which 29 were waited for; matrix products, arithmetic and copies ran while one was open for 6% of the time, Pallas kernels for 17%

profile of v4, /device:TPU:0, one launch (start us, length us, event | category | flops | bytes accessed | tf_op | source)
XLA Modules:
  0.0 252.0 jit_solution(1354769179374511029)
XLA Ops:
  3.3 6.7 %collective-permute-start.1 = (bf16[64,2304]{1,0:T(8,128)(2,1)S(1)}, bf16[64,2304]{1,0:T(8,128)(2,1)S(1)}, u32[]{:S(2)}, u32[]{:S(2)}) collective-permute-start(bf16[64,2304]{1,0:T(8,128)(2,1)S(1)} %fusion.33), channel_id=1, source_target_pairs={{0,1},{1,0},{2,3},{3,2},{4,5},{5,4},{6,7},{7,6},{8,9},{9,8},{10,11... | collective-permute-start | bytes 884744 | tf_op jit(solution)/shard_map/ppermute | solution.py:25
  11.4 8.6 %collective-permute-start.2 = (bf16[32,2304]{1,0:T(8,128)(2,1)S(1)}, bf16[32,2304]{1,0:T(8,128)(2,1)S(1)}, u32[]{:S(2)}, u32[]{:S(2)}) collective-permute-start(bf16[32,2304]{1,0:T(8,128)(2,1)S(1)} %dynamic-slice_convert_fusion.8), channel_id=1, source_target_pairs={{0,2},{1,3},{2,0},{3,1},{4,6},{5,7},{6,4},{7,5},{8,10},{9,11},{10,... | collective-permute-start | bytes 442376 | tf_op jit(solution)/shard_map/ppermute | solution.py:25
  20.0 4.1 %collective-permute-done.2 = bf16[32,2304]{1,0:T(8,128)(2,1)S(1)} collective-permute-done((bf16[32,2304]{1,0:T(8,128)(2,1)S(1)}, bf16[32,2304]{1,0:T(8,128)(2,1)S(1)}, u32[]{:S(2)}, u32[]{:S(2)}) %collective-permute-start.2) | collective-permute-done | bytes 147488 | tf_op jit(solution)/shard_map/ppermute | solution.py:25
  35.2 3.2 %collective-permute-done.6 = bf16[144,128]{1,0:T(8,128)(2,1)S(1)} collective-permute-done((bf16[144,128]{1,0:T(8,128)(2,1)S(1)}, bf16[144,128]{1,0:T(8,128)(2,1)S(1)}, u32[]{:S(2)}, u32[]{:S(2)}) %collective-permute-start.6) | collective-permute-done | bytes 36896 | tf_op jit(solution)/shard_map/ppermute | solution.py:76
  47.6 4.3 %convolution_convert_fusion.7 = bf16[128,4096]{1,0:T(8,128)(2,1)} fusion(bf16[576,128]{1,0:T(8,128)(2,1)S(1)} %constant_dynamic-update-slice_fusion.4, bf16[576,16384]{1,0:T(8,128)(2,1)} %w_ref.7), kind=kOutput, calls=%fused_computation.7 | convolution fusion | flops 604504064 | bytes 5914624 | tf_op jit(solution)/shard_map/dot_general | solution.py:176
  51.9 4.3 %convolution_convert_fusion.4 = bf16[128,4096]{1,0:T(8,128)(2,1)} fusion(bf16[576,128]{1,0:T(8,128)(2,1)S(1)} %constant_dynamic-update-slice_fusion.4, bf16[576,16384]{1,0:T(8,128)(2,1)} %w_ref.7), kind=kOutput, calls=%fused_computation.4 | convolution fusion | flops 604504064 | bytes 5914624 | tf_op jit(solution)/shard_map/dot_general | solution.py:176
  56.3 4.3 %convolution_convert_fusion.5 = bf16[128,4096]{1,0:T(8,128)(2,1)} fusion(bf16[576,128]{1,0:T(8,128)(2,1)S(1)} %constant_dynamic-update-slice_fusion.4, bf16[576,16384]{1,0:T(8,128)(2,1)} %w_ref.7), kind=kOutput, calls=%fused_computation.5 | convolution fusion | flops 604504064 | bytes 5914624 | tf_op jit(solution)/shard_map/dot_general | solution.py:176
  60.6 3.5 %convolution_convert_fusion.6 = bf16[128,4096]{1,0:T(8,128)(2,1)S(1)} fusion(bf16[576,128]{1,0:T(8,128)(2,1)S(1)} %constant_dynamic-update-slice_fusion.4, bf16[576,16384]{1,0:T(8,128)(2,1)} %w_ref.7), kind=kOutput, calls=%fused_computation.6 | convolution fusion | flops 604504064 | bytes 5914624 | tf_op jit(solution)/shard_map/dot_general | solution.py:176
  75.1 4.4 %collective-permute-done.12 = bf16[32,4096]{1,0:T(8,128)(2,1)S(1)} collective-permute-done((bf16[32,4096]{1,0:T(8,128)(2,1)S(1)}, bf16[32,4096]{1,0:T(8,128)(2,1)S(1)}, u32[]{:S(2)}, u32[]{:S(2)}) %collective-permute-start.12) | collective-permute-done | bytes 262176 | tf_op jit(solution)/shard_map/ppermute | solution.py:25
  80.9 4.3 %collective-permute-done.22 = bf16[32,4096]{1,0:T(8,128)(2,1)S(1)} collective-permute-done((bf16[32,4096]{1,0:T(8,128)(2,1)S(1)}, bf16[32,4096]{1,0:T(8,128)(2,1)S(1)}, u32[]{:S(2)}, u32[]{:S(2)}) %collective-permute-start.22) | collective-permute-done | bytes 262176 | tf_op jit(solution)/shard_map/ppermute | solution.py:25
  86.5 4.2 %collective-permute-done.18 = bf16[32,4096]{1,0:T(8,128)(2,1)S(1)} collective-permute-done((bf16[32,4096]{1,0:T(8,128)(2,1)S(1)}, bf16[32,4096]{1,0:T(8,128)(2,1)S(1)}, u32[]{:S(2)}, u32[]{:S(2)}) %collective-permute-start.18) | collective-permute-done | bytes 262176 | tf_op jit(solution)/shard_map/ppermute | solution.py:25
  92.1 4.3 %collective-permute-done.14 = bf16[32,4096]{1,0:T(8,128)(2,1)S(1)} collective-permute-done((bf16[32,4096]{1,0:T(8,128)(2,1)S(1)}, bf16[32,4096]{1,0:T(8,128)(2,1)S(1)}, u32[]{:S(2)}, u32[]{:S(2)}) %collective-permute-start.14) | collective-permute-done | bytes 262176 | tf_op jit(solution)/shard_map/ppermute | solution.py:25
  97.7 4.3 %collective-permute-done.25 = bf16[32,4096]{1,0:T(8,128)(2,1)S(1)} collective-permute-done((bf16[32,4096]{1,0:T(8,128)(2,1)S(1)}, bf16[32,4096]{1,0:T(8,128)(2,1)S(1)}, u32[]{:S(2)}, u32[]{:S(2)}) %collective-permute-start.25) | collective-permute-done | bytes 262176 | tf_op jit(solution)/shard_map/ppermute | solution.py:25
  102.1 5.5 %collective-permute-done.23 = bf16[32,4096]{1,0:T(8,128)(2,1)S(1)} collective-permute-done((bf16[32,4096]{1,0:T(8,128)(2,1)S(1)}, bf16[32,4096]{1,0:T(8,128)(2,1)S(1)}, u32[]{:S(2)}, u32[]{:S(2)}) %collective-permute-start.23) | collective-permute-done | bytes 262176 | tf_op jit(solution)/shard_map/ppermute | solution.py:25
  107.8 5.4 %collective-permute-done.19 = bf16[32,4096]{1,0:T(8,128)(2,1)S(1)} collective-permute-done((bf16[32,4096]{1,0:T(8,128)(2,1)S(1)}, bf16[32,4096]{1,0:T(8,128)(2,1)S(1)}, u32[]{:S(2)}, u32[]{:S(2)}) %collective-permute-start.19) | collective-permute-done | bytes 262176 | tf_op jit(solution)/shard_map/ppermute | solution.py:25
  113.4 4.6 %collective-permute-done.15 = bf16[32,4096]{1,0:T(8,128)(2,1)S(1)} collective-permute-done((bf16[32,4096]{1,0:T(8,128)(2,1)S(1)}, bf16[32,4096]{1,0:T(8,128)(2,1)S(1)}, u32[]{:S(2)}, u32[]{:S(2)}) %collective-permute-start.15) | collective-permute-done | bytes 262176 | tf_op jit(solution)/shard_map/ppermute | solution.py:25
  125.1 3.5 %collective-permute-start.29 = (f32[144,128]{1,0:T(8,128)S(1)}, f32[144,128]{1,0:T(8,128)S(1)}, u32[]{:S(2)}, u32[]{:S(2)}) collective-permute-start(f32[144,128]{1,0:T(8,128)S(1)} %get-tuple-element.49), channel_id=1, source_target_pairs={{0,12},{4,0},{8,4},{12,8},{1,13},{5,1},{9,5},{13,9},{2,14},{6,2},{... | collective-permute-start | bytes 221192 | tf_op jit(solution)/shard_map/ppermute | solution.py:76
  131.4 4.9 %collective-permute-done.28 = f32[144,128]{1,0:T(8,128)S(1)} collective-permute-done((f32[144,128]{1,0:T(8,128)S(1)}, f32[144,128]{1,0:T(8,128)S(1)}, u32[]{:S(2)}, u32[]{:S(2)}) %collective-permute-start.28) | collective-permute-done | bytes 73760 | tf_op jit(solution)/shard_map/ppermute | solution.py:76
  148.6 5.1 %shard_map.115 = (bf16[576,16384]{1,0:T(8,128)(2,1)}, f32[8,4096]{1,0:T(8,128)}) custom-call(bf16[576,128]{1,0:T(8,128)(2,1)S(1)} %constant_dynamic-update-slice_fusion.left_ref, bf16[128,4096]{1,0:T(8,128)(2,1)S(1)} %pad_maximum_fusion.right_ref, bf16[576,16384]{1,0:T(8,128)(2,1)S(1)} %bitcast.71), custom_call_target="tpu_custom_call" | custom-call | flops 603979776 | bytes 9437184 | tf_op jit(solution)/shard_map/pallas_call | solution.py:119
  153.7 5.1 %shard_map.116 = (bf16[576,16384]{1,0:T(8,128)(2,1)}, f32[8,4096]{1,0:T(8,128)}) custom-call(bf16[576,128]{1,0:T(8,128)(2,1)S(1)} %constant_dynamic-update-slice_fusion.left_ref, bf16[128,4096]{1,0:T(8,128)(2,1)S(1)} %pad_maximum_fusion.1.right_ref, bf16[576,16384]{1,0:T(8,128)(2,1)S(1)} %bitcast.72, ...), custom_call_target="tpu_custom_call", output_to_operand_aliasing={{0}: (3, {})} | custom-call | flops 603979776 | bytes 9437184 | tf_op jit(solution)/shard_map/pallas_call | solution.py:119
  158.8 5.1 %shard_map.117 = (bf16[576,16384]{1,0:T(8,128)(2,1)}, f32[8,4096]{1,0:T(8,128)}) custom-call(bf16[576,128]{1,0:T(8,128)(2,1)S(1)} %constant_dynamic-update-slice_fusion.left_ref, bf16[128,4096]{1,0:T(8,128)(2,1)S(1)} %pad_maximum_fusion.2.right_ref, bf16[576,16384]{1,0:T(8,128)(2,1)S(1)} %bitcast.73, ...), custom_call_target="tpu_custom_call", output_to_operand_aliasing={{0}: (3, {})} | custom-call | flops 603979776 | bytes 9437184 | tf_op jit(solution)/shard_map/pallas_call | solution.py:119
  163.9 5.1 %shard_map.118 = (bf16[576,16384]{1,0:T(8,128)(2,1)}, f32[8,4096]{1,0:T(8,128)}) custom-call(bf16[576,128]{1,0:T(8,128)(2,1)S(1)} %constant_dynamic-update-slice_fusion.left_ref, bf16[128,4096]{1,0:T(8,128)(2,1)S(1)} %pad_maximum_fusion.3.right_ref, bf16[576,16384]{1,0:T(8,128)(2,1)S(1)} %bitcast.74, ...), custom_call_target="tpu_custom_call", output_to_operand_aliasing={{0}: (3, {})} | custom-call | flops 603979776 | bytes 9437184 | tf_op jit(solution)/shard_map/pallas_call | solution.py:119
  174.7 4.4 %collective-permute-done.34 = bf16[32,4096]{1,0:T(8,128)(2,1)S(1)} collective-permute-done((bf16[32,4096]{1,0:T(8,128)(2,1)S(1)}, bf16[32,4096]{1,0:T(8,128)(2,1)S(1)}, u32[]{:S(2)}, u32[]{:S(2)}) %collective-permute-start.34) | collective-permute-done | bytes 262176 | tf_op jit(solution)/shard_map/ppermute | solution.py:25
  180.2 4.6 %collective-permute-done.38 = bf16[32,4096]{1,0:T(8,128)(2,1)S(1)} collective-permute-done((bf16[32,4096]{1,0:T(8,128)(2,1)S(1)}, bf16[32,4096]{1,0:T(8,128)(2,1)S(1)}, u32[]{:S(2)}, u32[]{:S(2)}) %collective-permute-start.38) | collective-permute-done | bytes 262176 | tf_op jit(solution)/shard_map/ppermute | solution.py:25
  185.8 4.6 %collective-permute-done.42 = bf16[32,4096]{1,0:T(8,128)(2,1)S(1)} collective-permute-done((bf16[32,4096]{1,0:T(8,128)(2,1)S(1)}, bf16[32,4096]{1,0:T(8,128)(2,1)S(1)}, u32[]{:S(2)}, u32[]{:S(2)}) %collective-permute-start.42) | collective-permute-done | bytes 262176 | tf_op jit(solution)/shard_map/ppermute | solution.py:25
  191.4 4.6 %collective-permute-done.46 = bf16[32,4096]{1,0:T(8,128)(2,1)S(1)} collective-permute-done((bf16[32,4096]{1,0:T(8,128)(2,1)S(1)}, bf16[32,4096]{1,0:T(8,128)(2,1)S(1)}, u32[]{:S(2)}, u32[]{:S(2)}) %collective-permute-start.46) | collective-permute-done | bytes 262176 | tf_op jit(solution)/shard_map/ppermute | solution.py:25
  197.0 4.6 %collective-permute-done.35 = bf16[32,4096]{1,0:T(8,128)(2,1)S(1)} collective-permute-done((bf16[32,4096]{1,0:T(8,128)(2,1)S(1)}, bf16[32,4096]{1,0:T(8,128)(2,1)S(1)}, u32[]{:S(2)}, u32[]{:S(2)}) %collective-permute-start.35) | collective-permute-done | bytes 262176 | tf_op jit(solution)/shard_map/ppermute | solution.py:25
  201.7 15.8 %collective-permute-done.47 = bf16[32,4096]{1,0:T(8,128)(2,1)S(1)} collective-permute-done((bf16[32,4096]{1,0:T(8,128)(2,1)S(1)}, bf16[32,4096]{1,0:T(8,128)(2,1)S(1)}, u32[]{:S(2)}, u32[]{:S(2)}) %collective-permute-start.47) | collective-permute-done | bytes 262176 | tf_op jit(solution)/shard_map/ppermute | solution.py:25
  219.6 7.8 %shard_map.111 = (bf16[576,16384]{1,0:T(8,128)(2,1)}, f32[8,4096]{1,0:T(8,128)S(1)}) custom-call(bf16[576,128]{1,0:T(8,128)(2,1)S(1)} %copy.22.left_ref, bf16[128,4096]{1,0:T(8,128)(2,1)S(1)} %pad_maximum_fusion.7.right_ref, bf16[576,16384]{1,0:T(8,128)(2,1)} %w_ref.7), custom_call_target="tpu_custom_call" | custom-call | flops 603979776 | bytes 9437184 | tf_op jit(solution)/shard_map/pallas_call | solution.py:119
  227.5 7.8 %shard_map.112 = (bf16[576,16384]{1,0:T(8,128)(2,1)}, f32[8,4096]{1,0:T(8,128)S(1)}) custom-call(bf16[576,128]{1,0:T(8,128)(2,1)S(1)} %copy.22.left_ref, bf16[128,4096]{1,0:T(8,128)(2,1)S(1)} %pad_maximum_fusion.6.right_ref, bf16[576,16384]{1,0:T(8,128)(2,1)} %w_ref.7, bf16[576,16384]{1,0:T(8,128)(2,1)} %get-tuple-element.16.rest_0_), custom_call_target="tpu_custom_call", output_to_operand_aliasing={{0}: (3, {})} | custom-call | flops 603979776 | bytes 9437184 | tf_op jit(solution)/shard_map/pallas_call | solution.py:119
  235.5 7.8 %shard_map.113 = (bf16[576,16384]{1,0:T(8,128)(2,1)}, f32[8,4096]{1,0:T(8,128)S(1)}) custom-call(bf16[576,128]{1,0:T(8,128)(2,1)S(1)} %copy.22.left_ref, bf16[128,4096]{1,0:T(8,128)(2,1)S(1)} %pad_maximum_fusion.5.right_ref, bf16[576,16384]{1,0:T(8,128)(2,1)} %w_ref.7, bf16[576,16384]{1,0:T(8,128)(2,1)} %get-tuple-element.17.rest_0_), custom_call_target="tpu_custom_call", output_to_operand_aliasing={{0}: (3, {})} | custom-call | flops 603979776 | bytes 9437184 | tf_op jit(solution)/shard_map/pallas_call | solution.py:119
  243.4 7.9 %shard_map.114 = (bf16[576,16384]{1,0:T(8,128)(2,1)}, f32[8,4096]{1,0:T(8,128)S(1)}) custom-call(bf16[576,128]{1,0:T(8,128)(2,1)S(1)} %copy.22.left_ref, bf16[128,4096]{1,0:T(8,128)(2,1)S(1)} %pad_maximum_fusion.4.right_ref, bf16[576,16384]{1,0:T(8,128)(2,1)} %w_ref.7, bf16[576,16384]{1,0:T(8,128)(2,1)} %get-tuple-element.18.rest_0_), custom_call_target="tpu_custom_call", output_to_operand_aliasing={{0}: (3, {})} | custom-call | flops 603979776 | bytes 9437184 | tf_op jit(solution)/shard_map/pallas_call | solution.py:119
  (214 shorter events, 75.6 us)
Async XLA Ops:
  3.3 7.9 %collective-permute-start.1 = (bf16[64,2304]{1,0:T(8,128)(2,1)S(1)}, bf16[64,2304]{1,0:T(8,128)(2,1)S(1)}, u32[]{:S(2)}, u32[]{:S(2)}) collective-permute-start(bf16[64,2304]{1,0:T(8,128)(2,1)S(1)} %fusion.33), channel_id=1, source_target_pairs={{0,1},{1,0},{2,3},{3,2},{4,5},{5,4},{6,7},{7,6},{8,9},{9,8},{10,11... | collective-permute-start | bytes 884744 | tf_op jit(solution)/shard_map/ppermute | solution.py:25
  11.4 12.8 %collective-permute-start.2 = (bf16[32,2304]{1,0:T(8,128)(2,1)S(1)}, bf16[32,2304]{1,0:T(8,128)(2,1)S(1)}, u32[]{:S(2)}, u32[]{:S(2)}) collective-permute-start(bf16[32,2304]{1,0:T(8,128)(2,1)S(1)} %dynamic-slice_convert_fusion.8), channel_id=1, source_target_pairs={{0,2},{1,3},{2,0},{3,1},{4,6},{5,7},{6,4},{7,5},{8,10},{9,11},{10,... | collective-permute-start | bytes 442376 | tf_op jit(solution)/shard_map/ppermute | solution.py:25
  39.1 6.2 %collective-permute-start.8 = (bf16[144,128]{1,0:T(8,128)(2,1)S(1)}, bf16[144,128]{1,0:T(8,128)(2,1)S(1)}, u32[]{:S(2)}, u32[]{:S(2)}) collective-permute-start(bf16[144,128]{1,0:T(8,128)(2,1)S(1)} %get-tuple-element.31), channel_id=1, source_target_pairs={{0,4},{4,8},{8,12},{12,0},{1,5},{5,9},{9,13},{13,1},{2,6},{6,10},{... | collective-permute-start | bytes 110600 | tf_op jit(solution)/shard_map/ppermute | solution.py:88
  70.3 9.2 %collective-permute-start.12 = (bf16[32,4096]{1,0:T(8,128)(2,1)S(1)}, bf16[32,4096]{1,0:T(8,128)(2,1)S(1)}, u32[]{:S(2)}, u32[]{:S(2)}) collective-permute-start(bf16[32,4096]{1,0:T(8,128)(2,1)S(1)} %dynamic-slice_convert_fusion.7), channel_id=1, source_target_pairs={{0,2},{1,3},{2,0},{3,1},{4,6},{5,7},{6,4},{7,5},{8,10},{9,11},{10,... | collective-permute-start | bytes 786440 | tf_op jit(solution)/shard_map/ppermute | solution.py:25
  71.4 13.7 %collective-permute-start.22 = (bf16[32,4096]{1,0:T(8,128)(2,1)S(1)}, bf16[32,4096]{1,0:T(8,128)(2,1)S(1)}, u32[]{:S(2)}, u32[]{:S(2)}) collective-permute-start(bf16[32,4096]{1,0:T(8,128)(2,1)S(1)} %dynamic-slice_convert_fusion.4), channel_id=1, source_target_pairs={{0,2},{1,3},{2,0},{3,1},{4,6},{5,7},{6,4},{7,5},{8,10},{9,11},{10,... | collective-permute-start | bytes 786440 | tf_op jit(solution)/shard_map/ppermute | solution.py:25
  72.8 18.0 %collective-permute-start.18 = (bf16[32,4096]{1,0:T(8,128)(2,1)S(1)}, bf16[32,4096]{1,0:T(8,128)(2,1)S(1)}, u32[]{:S(2)}, u32[]{:S(2)}) collective-permute-start(bf16[32,4096]{1,0:T(8,128)(2,1)S(1)} %dynamic-slice_convert_fusion.5), channel_id=1, source_target_pairs={{0,2},{1,3},{2,0},{3,1},{4,6},{5,7},{6,4},{7,5},{8,10},{9,11},{10,... | collective-permute-start | bytes 786440 | tf_op jit(solution)/shard_map/ppermute | solution.py:25
  73.9 22.5 %collective-permute-start.14 = (bf16[32,4096]{1,0:T(8,128)(2,1)S(1)}, bf16[32,4096]{1,0:T(8,128)(2,1)S(1)}, u32[]{:S(2)}, u32[]{:S(2)}) collective-permute-start(bf16[32,4096]{1,0:T(8,128)(2,1)S(1)} %dynamic-slice_convert_fusion.6), channel_id=1, source_target_pairs={{0,2},{1,3},{2,0},{3,1},{4,6},{5,7},{6,4},{7,5},{8,10},{9,11},{10,... | collective-permute-start | bytes 786440 | tf_op jit(solution)/shard_map/ppermute | solution.py:25
  79.9 22.1 %collective-permute-start.25 = (bf16[32,4096]{1,0:T(8,128)(2,1)S(1)}, bf16[32,4096]{1,0:T(8,128)(2,1)S(1)}, u32[]{:S(2)}, u32[]{:S(2)}) collective-permute-start(bf16[32,4096]{1,0:T(8,128)(2,1)S(1)} %fusion.32), channel_id=1, source_target_pairs={{0,2},{1,3},{2,0},{3,1},{4,6},{5,7},{6,4},{7,5},{8,10},{9,11},{10,... | collective-permute-start | bytes 786440 | tf_op jit(solution)/shard_map/ppermute | solution.py:25
  85.5 22.1 %collective-permute-start.23 = (bf16[32,4096]{1,0:T(8,128)(2,1)S(1)}, bf16[32,4096]{1,0:T(8,128)(2,1)S(1)}, u32[]{:S(2)}, u32[]{:S(2)}) collective-permute-start(bf16[32,4096]{1,0:T(8,128)(2,1)S(1)} %fusion.30), channel_id=1, source_target_pairs={{0,2},{1,3},{2,0},{3,1},{4,6},{5,7},{6,4},{7,5},{8,10},{9,11},{10,... | collective-permute-start | bytes 786440 | tf_op jit(solution)/shard_map/ppermute | solution.py:25
  91.1 22.1 %collective-permute-start.19 = (bf16[32,4096]{1,0:T(8,128)(2,1)S(1)}, bf16[32,4096]{1,0:T(8,128)(2,1)S(1)}, u32[]{:S(2)}, u32[]{:S(2)}) collective-permute-start(bf16[32,4096]{1,0:T(8,128)(2,1)S(1)} %fusion.28), channel_id=1, source_target_pairs={{0,2},{1,3},{2,0},{3,1},{4,6},{5,7},{6,4},{7,5},{8,10},{9,11},{10,... | collective-permute-start | bytes 786440 | tf_op jit(solution)/shard_map/ppermute | solution.py:25
  96.7 21.2 %collective-permute-start.15 = (bf16[32,4096]{1,0:T(8,128)(2,1)S(1)}, bf16[32,4096]{1,0:T(8,128)(2,1)S(1)}, u32[]{:S(2)}, u32[]{:S(2)}) collective-permute-start(bf16[32,4096]{1,0:T(8,128)(2,1)S(1)} %fusion.26), channel_id=1, source_target_pairs={{0,2},{1,3},{2,0},{3,1},{4,6},{5,7},{6,4},{7,5},{8,10},{9,11},{10,... | collective-permute-start | bytes 786440 | tf_op jit(solution)/shard_map/ppermute | solution.py:25
  102.1 16.1 %collective-permute-start.26 = (bf16[64,4096]{1,0:T(8,128)(2,1)S(1)}, bf16[64,4096]{1,0:T(8,128)(2,1)S(1)}, u32[]{:S(2)}, u32[]{:S(2)}) collective-permute-start(bf16[64,4096]{1,0:T(8,128)(2,1)S(1)} %pad_maximum_fusion.11), channel_id=1, source_target_pairs={{0,1},{1,0},{2,3},{3,2},{4,5},{5,4},{6,7},{7,6},{8,9},{9,8},{10,11... | collective-permute-start | bytes 1572872 | tf_op jit(solution)/shard_map/ppermute | solution.py:25
  107.7 10.5 %collective-permute-start.24 = (bf16[64,4096]{1,0:T(8,128)(2,1)S(1)}, bf16[64,4096]{1,0:T(8,128)(2,1)S(1)}, u32[]{:S(2)}, u32[]{:S(2)}) collective-permute-start(bf16[64,4096]{1,0:T(8,128)(2,1)S(1)} %pad_maximum_fusion.10), channel_id=1, source_target_pairs={{0,1},{1,0},{2,3},{3,2},{4,5},{5,4},{6,7},{7,6},{8,9},{9,8},{10,11... | collective-permute-start | bytes 1572872 | tf_op jit(solution)/shard_map/ppermute | solution.py:25
  113.3 8.2 %collective-permute-start.20 = (bf16[64,4096]{1,0:T(8,128)(2,1)S(1)}, bf16[64,4096]{1,0:T(8,128)(2,1)S(1)}, u32[]{:S(2)}, u32[]{:S(2)}) collective-permute-start(bf16[64,4096]{1,0:T(8,128)(2,1)S(1)} %pad_maximum_fusion.9), channel_id=1, source_target_pairs={{0,1},{1,0},{2,3},{3,2},{4,5},{5,4},{6,7},{7,6},{8,9},{9,8},{10,11... | collective-permute-start | bytes 1572872 | tf_op jit(solution)/shard_map/ppermute | solution.py:25
  125.1 6.2 %collective-permute-start.29 = (f32[144,128]{1,0:T(8,128)S(1)}, f32[144,128]{1,0:T(8,128)S(1)}, u32[]{:S(2)}, u32[]{:S(2)}) collective-permute-start(f32[144,128]{1,0:T(8,128)S(1)} %get-tuple-element.49), channel_id=1, source_target_pairs={{0,12},{4,0},{8,4},{12,8},{1,13},{5,1},{9,5},{13,9},{2,14},{6,2},{... | collective-permute-start | bytes 221192 | tf_op jit(solution)/shard_map/ppermute | solution.py:76
  128.7 7.6 %collective-permute-start.28 = (f32[144,128]{1,0:T(8,128)S(1)}, f32[144,128]{1,0:T(8,128)S(1)}, u32[]{:S(2)}, u32[]{:S(2)}) collective-permute-start(f32[144,128]{1,0:T(8,128)S(1)} %get-tuple-element.50), channel_id=1, source_target_pairs={{0,8},{4,12},{8,0},{12,4},{1,9},{5,13},{9,1},{13,5},{2,10},{6,14},... | collective-permute-start | bytes 221192 | tf_op jit(solution)/shard_map/ppermute | solution.py:76
  128.7 7.6 %collective-permute-start.27 = (f32[144,128]{1,0:T(8,128)S(1)}, f32[144,128]{1,0:T(8,128)S(1)}, u32[]{:S(2)}, u32[]{:S(2)}) collective-permute-start(f32[144,128]{1,0:T(8,128)S(1)} %get-tuple-element.48), channel_id=1, source_target_pairs={{0,4},{4,8},{8,12},{12,0},{1,5},{5,9},{9,13},{13,1},{2,6},{6,10},{... | collective-permute-start | bytes 221192 | tf_op jit(solution)/shard_map/ppermute | solution.py:76
  147.2 22.5 %collective-permute-start.33 = (bf16[64,4096]{1,0:T(8,128)(2,1)S(1)}, bf16[64,4096]{1,0:T(8,128)(2,1)S(1)}, u32[]{:S(2)}, u32[]{:S(2)}) collective-permute-start(bf16[64,4096]{1,0:T(8,128)(2,1)S(1)} %constant_dynamic-slice_fusion.3), channel_id=1, source_target_pairs={{0,1},{1,0},{2,3},{3,2},{4,5},{5,4},{6,7},{7,6},{8,9},{9,8},{10,11... | collective-permute-start | bytes 1572872 | tf_op jit(solution)/shard_map/ppermute | solution.py:25
  147.3 23.4 %collective-permute-start.37 = (bf16[64,4096]{1,0:T(8,128)(2,1)S(1)}, bf16[64,4096]{1,0:T(8,128)(2,1)S(1)}, u32[]{:S(2)}, u32[]{:S(2)}) collective-permute-start(bf16[64,4096]{1,0:T(8,128)(2,1)S(1)} %constant_dynamic-slice_fusion.2), channel_id=1, source_target_pairs={{0,1},{1,0},{2,3},{3,2},{4,5},{5,4},{6,7},{7,6},{8,9},{9,8},{10,11... | collective-permute-start | bytes 1572872 | tf_op jit(solution)/shard_map/ppermute | solution.py:25
  147.9 24.3 %collective-permute-start.41 = (bf16[64,4096]{1,0:T(8,128)(2,1)S(1)}, bf16[64,4096]{1,0:T(8,128)(2,1)S(1)}, u32[]{:S(2)}, u32[]{:S(2)}) collective-permute-start(bf16[64,4096]{1,0:T(8,128)(2,1)S(1)} %constant_dynamic-slice_fusion.1), channel_id=1, source_target_pairs={{0,1},{1,0},{2,3},{3,2},{4,5},{5,4},{6,7},{7,6},{8,9},{9,8},{10,11... | collective-permute-start | bytes 1572872 | tf_op jit(solution)/shard_map/ppermute | solution.py:25
  148.0 25.1 %collective-permute-start.45 = (bf16[64,4096]{1,0:T(8,128)(2,1)S(1)}, bf16[64,4096]{1,0:T(8,128)(2,1)S(1)}, u32[]{:S(2)}, u32[]{:S(2)}) collective-permute-start(bf16[64,4096]{1,0:T(8,128)(2,1)S(1)} %constant_dynamic-slice_fusion), channel_id=1, source_target_pairs={{0,1},{1,0},{2,3},{3,2},{4,5},{5,4},{6,7},{7,6},{8,9},{9,8},{10,11... | collective-permute-start | bytes 1572872 | tf_op jit(solution)/shard_map/ppermute | solution.py:25
  169.9 9.2 %collective-permute-start.34 = (bf16[32,4096]{1,0:T(8,128)(2,1)S(1)}, bf16[32,4096]{1,0:T(8,128)(2,1)S(1)}, u32[]{:S(2)}, u32[]{:S(2)}) collective-permute-start(bf16[32,4096]{1,0:T(8,128)(2,1)S(1)} %dynamic-slice_convert_fusion.3), channel_id=1, source_target_pairs={{0,2},{1,3},{2,0},{3,1},{4,6},{5,7},{6,4},{7,5},{8,10},{9,11},{10,... | collective-permute-start | bytes 786440 | tf_op jit(solution)/shard_map/ppermute | solution.py:25
  170.8 13.9 %collective-permute-start.38 = (bf16[32,4096]{1,0:T(8,128)(2,1)S(1)}, bf16[32,4096]{1,0:T(8,128)(2,1)S(1)}, u32[]{:S(2)}, u32[]{:S(2)}) collective-permute-start(bf16[32,4096]{1,0:T(8,128)(2,1)S(1)} %dynamic-slice_convert_fusion.2), channel_id=1, source_target_pairs={{0,2},{1,3},{2,0},{3,1},{4,6},{5,7},{6,4},{7,5},{8,10},{9,11},{10,... | collective-permute-start | bytes 786440 | tf_op jit(solution)/shard_map/ppermute | solution.py:25
  172.4 18.0 %collective-permute-start.42 = (bf16[32,4096]{1,0:T(8,128)(2,1)S(1)}, bf16[32,4096]{1,0:T(8,128)(2,1)S(1)}, u32[]{:S(2)}, u32[]{:S(2)}) collective-permute-start(bf16[32,4096]{1,0:T(8,128)(2,1)S(1)} %dynamic-slice_convert_fusion.1), channel_id=1, source_target_pairs={{0,2},{1,3},{2,0},{3,1},{4,6},{5,7},{6,4},{7,5},{8,10},{9,11},{10,... | collective-permute-start | bytes 786440 | tf_op jit(solution)/shard_map/ppermute | solution.py:25
  173.3 22.7 %collective-permute-start.46 = (bf16[32,4096]{1,0:T(8,128)(2,1)S(1)}, bf16[32,4096]{1,0:T(8,128)(2,1)S(1)}, u32[]{:S(2)}, u32[]{:S(2)}) collective-permute-start(bf16[32,4096]{1,0:T(8,128)(2,1)S(1)} %dynamic-slice_convert_fusion), channel_id=1, source_target_pairs={{0,2},{1,3},{2,0},{3,1},{4,6},{5,7},{6,4},{7,5},{8,10},{9,11},{10,... | collective-permute-start | bytes 786440 | tf_op jit(solution)/shard_map/ppermute | solution.py:25
  179.4 22.2 %collective-permute-start.35 = (bf16[32,4096]{1,0:T(8,128)(2,1)S(1)}, bf16[32,4096]{1,0:T(8,128)(2,1)S(1)}, u32[]{:S(2)}, u32[]{:S(2)}) collective-permute-start(bf16[32,4096]{1,0:T(8,128)(2,1)S(1)} %multiply_convert_fusion.3), channel_id=1, source_target_pairs={{0,2},{1,3},{2,0},{3,1},{4,6},{5,7},{6,4},{7,5},{8,10},{9,11},{10,... | collective-permute-start | bytes 786440 | tf_op jit(solution)/shard_map/ppermute | solution.py:25
  185.0 32.6 %collective-permute-start.39 = (bf16[32,4096]{1,0:T(8,128)(2,1)S(1)}, bf16[32,4096]{1,0:T(8,128)(2,1)S(1)}, u32[]{:S(2)}, u32[]{:S(2)}) collective-permute-start(bf16[32,4096]{1,0:T(8,128)(2,1)S(1)} %multiply_convert_fusion.2), channel_id=1, source_target_pairs={{0,2},{1,3},{2,0},{3,1},{4,6},{5,7},{6,4},{7,5},{8,10},{9,11},{10,... | collective-permute-start | bytes 786440 | tf_op jit(solution)/shard_map/ppermute | solution.py:25
  190.6 27.6 %collective-permute-start.43 = (bf16[32,4096]{1,0:T(8,128)(2,1)S(1)}, bf16[32,4096]{1,0:T(8,128)(2,1)S(1)}, u32[]{:S(2)}, u32[]{:S(2)}) collective-permute-start(bf16[32,4096]{1,0:T(8,128)(2,1)S(1)} %multiply_convert_fusion.1), channel_id=1, source_target_pairs={{0,2},{1,3},{2,0},{3,1},{4,6},{5,7},{6,4},{7,5},{8,10},{9,11},{10,... | collective-permute-start | bytes 786440 | tf_op jit(solution)/shard_map/ppermute | solution.py:25
  196.2 21.3 %collective-permute-start.47 = (bf16[32,4096]{1,0:T(8,128)(2,1)S(1)}, bf16[32,4096]{1,0:T(8,128)(2,1)S(1)}, u32[]{:S(2)}, u32[]{:S(2)}) collective-permute-start(bf16[32,4096]{1,0:T(8,128)(2,1)S(1)} %multiply_convert_fusion), channel_id=1, source_target_pairs={{0,2},{1,3},{2,0},{3,1},{4,6},{5,7},{6,4},{7,5},{8,10},{9,11},{10,... | collective-permute-start | bytes 786440 | tf_op jit(solution)/shard_map/ppermute | solution.py:25
  201.6 41.7 %collective-permute-start.36 = (bf16[64,4096]{1,0:T(8,128)(2,1)S(1)}, bf16[64,4096]{1,0:T(8,128)(2,1)S(1)}, u32[]{:S(2)}, u32[]{:S(2)}) collective-permute-start(bf16[64,4096]{1,0:T(8,128)(2,1)S(1)} %pad_maximum_fusion.12), channel_id=1, source_target_pairs={{0,1},{1,0},{2,3},{3,2},{4,5},{5,4},{6,7},{7,6},{8,9},{9,8},{10,11... | collective-permute-start | bytes 1572872 | tf_op jit(solution)/shard_map/ppermute | solution.py:25
  217.7 17.7 %collective-permute-start.40 = (bf16[64,4096]{1,0:T(8,128)(2,1)S(1)}, bf16[64,4096]{1,0:T(8,128)(2,1)S(1)}, u32[]{:S(2)}, u32[]{:S(2)}) collective-permute-start(bf16[64,4096]{1,0:T(8,128)(2,1)S(1)} %pad_maximum_fusion.13), channel_id=1, source_target_pairs={{0,1},{1,0},{2,3},{3,2},{4,5},{5,4},{6,7},{7,6},{8,9},{9,8},{10,11... | collective-permute-start | bytes 1572872 | tf_op jit(solution)/shard_map/ppermute | solution.py:25
  218.3 9.2 %collective-permute-start.44 = (bf16[64,4096]{1,0:T(8,128)(2,1)S(1)}, bf16[64,4096]{1,0:T(8,128)(2,1)S(1)}, u32[]{:S(2)}, u32[]{:S(2)}) collective-permute-start(bf16[64,4096]{1,0:T(8,128)(2,1)S(1)} %pad_maximum_fusion.14), channel_id=1, source_target_pairs={{0,1},{1,0},{2,3},{3,2},{4,5},{5,4},{6,7},{7,6},{8,9},{9,8},{10,11... | collective-permute-start | bytes 1572872 | tf_op jit(solution)/shard_map/ppermute | solution.py:25
  (35 other events, 391.6 us)
